TPU v7x, 512 devices: a whole 4x8x8 slice. The times are simulated.
512 devices in a mesh: row: 16 (over z, core), col: 32 (over y, x).
Axes of the slice: x: 4, y: 8, z: 8, core: 2. Of those that a mesh axis runs over, the one named last changes fastest.
Arguments:
- block: float32 [8192, 4096], P('row', 'col'), may hold values from -6 to 6
- panels: float32 [2, 8192, 256], P(None, 'row', 'col'), may hold values from -0.125 to 0.125
- pivots: int32 [2, 256], replicated, may hold values from 0 to 8191, as said below
Outputs:
- updated: float32 [8192, 4096], P('row', 'col')
Inputs may be any that keep to these rules, and one draw needn't show every extreme that they name: `pivots`: entry j of list k is either k*256+j itself or a global row at or beyond (k+1)*256; within one list the entries beyond are all different; entry 0 of list 0 is 0 and entry 255 of list 0 is 8191.
All inputs are finite; a program needn't handle non-finite values.
Results may differ from a plain program's by a relative error of at most 0.0001.
Values sent between devices are 32-bit elements; how exact they have to be, the bound alone decides.
No kernel may reach another device: no remote copies, remote signals or barrier semaphores. Data moves between devices by JAX's collectives and lax.ppermute only.
A program may use at most 64 MiB of HBM per device.

v0:
```python
import jax
import jax.numpy as jnp
from jax import lax
from jax.sharding import PartitionSpec as P

PW = 256


def swap_order(piv_row, offset, count):
    own = offset + jnp.arange(piv_row.shape[0], dtype=jnp.int32)
    base = jnp.arange(count, dtype=jnp.int32)
    return base.at[own].set(piv_row).at[piv_row].set(own)


def pick_rows(data, perm, targets, start):
    local_src = perm[targets] - start
    owned = (local_src >= 0) & (local_src < data.shape[0])
    taken = jnp.take(data, jnp.clip(local_src, 0, data.shape[0] - 1), axis=0)
    return jnp.where(owned[:, None], taken, 0.0)


def place_rows(data, targets, values, start):
    local_dst = targets - start
    inside = (local_dst >= 0) & (local_dst < data.shape[0])
    where_to = jnp.where(inside, local_dst, data.shape[0])
    return data.at[where_to].set(values, mode="drop")


def solve_top(diag_rows, rows):
    strict = jnp.tril(diag_rows, -1)
    inverse = jnp.eye(PW, dtype=jnp.float32) - strict
    power = strict
    for level in range(1, PW.bit_length() - 1):
        power = jnp.dot(
            power, power, precision=lax.Precision.HIGHEST, preferred_element_type=jnp.float32
        )
        inverse = inverse + jnp.dot(
            inverse, power, precision=lax.Precision.HIGHEST, preferred_element_type=jnp.float32
        )
    return jnp.dot(
        inverse, rows, precision=lax.Precision.HIGHEST, preferred_element_type=jnp.float32
    )


def finish(work, lower, offset, start, upper):
    product = jnp.dot(
        lower, upper, precision=lax.Precision.HIGHEST, preferred_element_type=jnp.float32
    )
    global_rows = start + jnp.arange(work.shape[0], dtype=jnp.int32)
    work = jnp.where((global_rows >= offset + PW)[:, None], work - product, work)
    placed = work.at[offset : offset + PW].set(upper)
    in_top = (global_rows >= offset) & (global_rows < offset + PW)
    return jnp.where(in_top[:, None], placed, work)


def body(block, panels, pivots):
    rows_here = block.shape[0]
    rows_all = rows_here * lax.axis_size("row")
    start = lax.axis_index("row") * rows_here
    identity_perm = jnp.arange(rows_all, dtype=jnp.int32)
    perms = [swap_order(pivots[panel], panel * PW, rows_all) for panel in range(2)]
    targets = [
        jnp.concatenate([jnp.arange(panel * PW, panel * PW + PW, dtype=jnp.int32), pivots[panel]])
        for panel in range(2)
    ]
    tops_index = [jnp.arange(panel * PW, panel * PW + PW, dtype=jnp.int32) for panel in range(2)]
    work = block
    lowers = lax.all_gather(panels, "col", axis=2, tiled=True)
    for panel in range(2):
        offset = panel * PW
        diag_rows = pick_rows(lowers[panel], identity_perm, tops_index[panel], start)
        picked = pick_rows(work, perms[panel], targets[panel], start)
        moved, diag_all = lax.psum((picked, diag_rows), "row")
        work = place_rows(work, targets[panel], moved, start)
        upper = solve_top(diag_all, moved[:PW])
        work = finish(work, lowers[panel], offset, start, upper)
    return work


def solution(mesh):
    return jax.shard_map(
        body,
        mesh=mesh,
        in_specs=(P("row", "col"), P(None, "row", "col"), P()),
        out_specs=P("row", "col"),
        check_vma=False,
    )
```

profile of v0, /device:TPU:1, one launch (start us, length us, event | category | flops | bytes accessed | tf_op | source)
XLA Modules:
  0.0 366.2 jit_solution(5757545376210844859)
XLA Ops:
  6.5 1.0 copy.32
  7.5 0.6 copy.10
  8.2 0.6 copy-done.5
  8.9 1.5 scatter_fusion
  10.4 1.5 scatter_fusion.1
  11.9 3.1 gather_fusion
  15.1 1.0 gather_fusion.4
  16.2 1.7 gather_fusion.3
  18.0 1.7 gather_fusion.1
  19.7 1.5 scatter_fusion.3
  21.2 1.5 scatter_fusion.4
  22.7 3.1 gather_fusion.2
  26.0 0.9 select_select_fusion.3
  26.9 65.8 %all-gather.2.cloned.1.call-done = f32[2,512,256]{1,0,2:T(2,128)} async-done(((f32[2,512,8]{1,0,2:T(2,128)}), f32[2,512,256]{1,0,2:T(2,128)}) %all-gather.2.cloned.1.call-update) | async-done | bytes 1048592 | tf_op jit(solution)/shard_map/all_gather | solution.py:68
  92.7 2.5 fusion.34
  95.2 0.5 copy.17
  95.7 1.0 gather_fusion.5
  96.7 0.8 select_select_fusion.2
  97.8 0.5 copy.18
  98.3 1.0 gather_fusion.7
  99.2 0.8 select_select_fusion
  100.1 117.6 %all-reduce.7.cloned.1.call-done = (f32[512,128]{1,0:T(8,128)}, f32[256,256]{1,0:T(8,128)}) async-done(((f32[512,128]{1,0:T(8,128)}, f32[256,256]{1,0:T(8,128)}), (f32[512,128]{1,0:T(8,128)}, f32[256,256]{1,0:T(8,128)})) %all-reduce.7.cloned.1.call-update) | async-done | bytes 524304 | tf_op jit(solution)/shard_map/psum | solution.py:73
  217.7 1.6 fusion.6
  219.3 0.4 convolution_add_fusion.13
  219.7 0.4 fusion.36
  220.5 0.4 convolution_add_fusion.12
  221.2 0.4 convolution_add_fusion.11
  221.6 0.4 fusion.39
  222.0 0.4 convolution_add_fusion.10
  222.8 0.4 convolution_add_fusion.9
  223.2 0.4 fusion.41
  223.6 0.4 convolution_add_fusion.8
  224.0 0.6 copy-done.2
  224.5 2.0 scatter_fusion.2
  226.6 0.4 convolution_add_fusion.7
  227.3 0.6 fusion.3
  228.1 1.0 gather_fusion.6
  229.1 0.9 select_select_fusion.1
  230.0 117.2 %all-reduce.5.cloned.1.call-done = (f32[512,128]{1,0:T(8,128)}, f32[256,256]{1,0:T(8,128)}) async-done(((f32[512,128]{1,0:T(8,128)}, f32[256,256]{1,0:T(8,128)}), (f32[512,128]{1,0:T(8,128)}, f32[256,256]{1,0:T(8,128)})) %all-reduce.5.cloned.1.call-update) | async-done | bytes 524304 | tf_op jit(solution)/shard_map/psum | solution.py:73
  347.3 1.6 fusion.9
  348.9 0.4 convolution_add_fusion.6
  349.7 0.4 fusion.43
  350.1 0.4 convolution_add_fusion.5
  353.2 0.4 convolution_add_fusion.1
  353.6 0.6 copy-done.3
  354.1 1.8 scatter_fusion.5
  356.7 1.3 fusion.1
  358.0 1.7 fusion.12
  (59 shorter events, 5.9 us)
Async XLA Ops:
  6.5 1.0 copy-start.4
  6.5 86.2 %all-gather.2.cloned.1.call-start = ((), (), s32[]{:S(2)}) async-start(), calls=%async_computation | async-start | bytes 1081344 | tf_op jit(solution)/shard_map/all_gather | solution.py:68
  8.2 0.7 copy-start.5
  8.2 209.5 %all-reduce.7.cloned.1.call-start = ((), (), s32[]{:S(2)}) async-start(), calls=%async_computation.2 | async-start | bytes 1048576 | tf_op jit(solution)/shard_map/psum | solution.py:73
  97.5 249.8 %all-reduce.5.cloned.1.call-start = ((), (), s32[]{:S(2)}) async-start(), calls=%async_computation.1 | async-start | bytes 1048576 | tf_op jit(solution)/shard_map/psum | solution.py:73
  217.7 1.6 copy-start
  223.6 1.0 copy-start.2
  347.3 1.6 copy-start.1
  353.2 1.0 copy-start.3
Sparse Core Ops, SparseCore 0:
  10.5 82.1 all-gather.1
  97.6 119.9 all-reduce.6
  230.2 117.0 all-reduce.4
where the time goes:
time: 367 us; the launch traced here: 366 us
  waiting for transfers between devices  301 us (82%)
  local copies, waits for them, and re-layouts  30.4 us (8%)
  matrix products  15.7 us (4%)
  between operations  13.7 us (4%)
  other arithmetic  5.41 us (1%)
    psum x2, waiting for transfers between devices, body(): moved, diag_all = lax.psum((picked, diag_rows), 'row')  235 us
    all_gather x1, waiting for transfers between devices, body(): lowers = lax.all_gather(panels, 'col', axis=2, tiled=True)  65.8 us
    gather x4, local copies, waits for them, and re-layouts, pick_rows(): local_src = perm[targets] - start  9.73 us
    dot_general x14, matrix products, solve_top(): jnp.dot(power, power, precision=lax.Precision.HIGHEST, preferred_element_...  7.69 us
  transfers between devices with their start and end apart: 3, of which 3 were waited for; matrix products, arithmetic and copies ran while one was open for 5% of the time, Pallas kernels for 0%

commit v1 on v0

v1 whole, which is shorter than its diff:
```python
import jax
import jax.numpy as jnp
from jax import lax
from jax.sharding import PartitionSpec as P

PW = 256
NZ, NC = 8, 2
NY, NX = 8, 4
Z_GROUPS = [[NC * z + core for z in range(NZ)] for core in range(NC)]
X_GROUPS = [[NX * y + x for x in range(NX)] for y in range(NY)]
Y_GROUPS = [[NX * y + x for y in range(NY)] for x in range(NX)]
PAIR = [(i, i ^ 1) for i in range(NZ * NC)]


def mm(a, b, ca=1, cb=0):
    return lax.dot_general(
        a, b, (((ca,), (cb,)), ((), ())),
        precision=lax.Precision.HIGHEST, preferred_element_type=jnp.float32,
    )


def spread(x, axis, groups):
    n = len(groups[0])
    return lax.all_to_all(
        jnp.broadcast_to(x[None], (n,) + x.shape), axis, 0, 0, tiled=True, axis_index_groups=groups
    )


def invert_t(diag_t):
    strict = jnp.triu(diag_t, 1)
    inverse = jnp.eye(PW, dtype=jnp.float32) - strict
    power = strict
    for _ in range(1, PW.bit_length() - 1):
        power = mm(power, power)
        inverse = inverse + mm(inverse, power)
    return inverse


def body(block, panels, pivots):
    me = lax.axis_index("row")
    core = me % NC
    start = me * 512
    first = me == 0
    p0, p1 = pivots[0], pivots[1]
    j = jnp.arange(PW, dtype=jnp.int32)
    lane = jnp.arange(512, dtype=jnp.int32)

    def through0(rows):
        hit = p0[None, :] == rows[:, None]
        found = jnp.max(jnp.where(hit, j[None, :], -1), axis=1)
        return jnp.where(found >= 0, found, rows)

    source = jnp.concatenate([p0, through0(p1), j, through0(PW + j)])
    pick = (source[:, None] - start == lane[None, :]).astype(jnp.float32)
    rows = mm(pick, block).reshape(2, NC, NZ, 32, 128)
    rows = rows.transpose(1, 2, 0, 3, 4).reshape(NC, NZ, 64, 128)

    pan_t = panels.transpose(0, 2, 1)
    at1 = (p1[:, None] - start == lane[None, :]).astype(jnp.float32)
    piv_t = mm(pan_t[0], at1, 1, 1)
    zero = jnp.zeros((8, PW), jnp.float32)
    own = lambda t: jnp.where(first, t, zero)
    pieces = jnp.stack([own(pan_t[0, :, :PW]), own(pan_t[1, :, PW:]), own(pan_t[0, :, PW:]), piv_t])
    tiles = pieces.reshape(4, 8, 2, 128).transpose(0, 2, 1, 3).reshape(8, 8, 128)

    mine = jnp.where(core == 0, rows[0], rows[1])
    other = jnp.where(core == 0, rows[1], rows[0])
    got = lax.ppermute(jnp.concatenate([other, tiles], 1), "row", PAIR)
    part = jnp.concatenate([mine, tiles], 1) + got
    part = lax.all_to_all(part, "row", 0, 0, tiled=True, axis_index_groups=Z_GROUPS)
    part = jnp.sum(part, 0)

    own_tiles = pan_t.reshape(2, 8, 4, 128).transpose(0, 2, 1, 3).reshape(64, 128)
    sent = jnp.concatenate([own_tiles, part[64:]], 0)
    sent = spread(sent, "col", Y_GROUPS)
    sent = spread(sent, "col", X_GROUPS)
    lower_t = sent[:, :, :64].reshape(NX, NY, 2, 4, 8, 128).transpose(2, 1, 0, 4, 3, 5).reshape(2, PW, 512)
    tile = sent[:, :, 64:]
    half = jnp.where(core == 0, tile[:2], tile[2:]).reshape(128, 128)

    wide = spread(jnp.concatenate([part[:64], half], 0), "row", Z_GROUPS)
    got = lax.ppermute(wide, "row", PAIR)
    low = jnp.where(core == 0, wide, got)
    high = jnp.where(core == 0, got, wide)
    both = jnp.stack([low, high])
    top = both[:, :, :32].reshape(512, 128)
    moved = both[:, :, 32:64].reshape(512, 128)
    square = both[:, :, 64:].reshape(NC, 4, 2, 2, NY, 8, 128)
    square = square.transpose(1, 4, 0, 3, 5, 2, 6).reshape(4, PW, PW)

    upper0 = mm(invert_t(square[0]), top[:PW], 0, 0)
    upper1 = mm(invert_t(square[1]), top[PW:] - mm(square[3], upper0, 0, 0), 0, 0)
    second = moved[PW:] - mm(square[2], upper0, 0, 0)

    at0 = (p0[:, None] - start == lane[None, :]).astype(jnp.float32)
    in0 = jnp.sum(at0, 0)[:, None] > 0
    in1 = jnp.sum(at1, 0)[:, None] > 0
    work = jnp.where(in0, mm(at0, moved[:PW], 0, 0), block) - mm(lower_t[0], upper0, 0, 0)
    work = jnp.where(in1, mm(at1, second, 0, 0), work) - mm(lower_t[1], upper1, 0, 0)
    return jnp.where(first, jnp.concatenate([upper0, upper1], 0), work)


def solution(mesh):
    return jax.shard_map(
        body,
        mesh=mesh,
        in_specs=(P("row", "col"), P(None, "row", "col"), P()),
        out_specs=P("row", "col"),
        check_vma=False,
    )
```

time: 367 us -> 118 us (0.32)
  waiting for transfers between devices: 301 us -> 35.4 us
  blocking collectives: 0 us -> 33.7 us
  local copies, waits for them, and re-layouts: 30.4 us -> 3.45 us
  starting transfers between devices: 0.27 us -> 22.2 us
  between operations: 13.7 us -> 0.57 us
  matrix products: 15.7 us -> 20.4 us
    psum x2 -> x0, waiting for transfers between devices: 235 us -> none  [body(): moved, diag_all = lax.psum((picked, diag_rows), 'row')]
    all_gather x1 -> x0, waiting for transfers between devices: 65.8 us -> none  [body(): lowers = lax.all_gather(panels, 'col', axis=2, tiled=True)]
    all_to_all x0 -> x2, blocking collectives: none -> 33.7 us  [the longest x1 17.1 us: spread(): lax.all_to_all(jnp.broadcast_to(x[None], (n,) + x.shape), axis, 0, 0, til...]
    all_to_all x0 -> x2, waiting for transfers between devices: none -> 32.8 us  [spread(): lax.all_to_all(jnp.broadcast_to(x[None], (n,) + x.shape), axis, 0, 0, til...]
    ppermute x0 -> x2, starting transfers between devices: none -> 14.7 us  [the longest x1 8.75 us: body(): got = lax.ppermute(jnp.concatenate([other, tiles], 1), 'row', PAIR)]
    gather x8 -> x0, local copies, waits for them, and re-layouts: 13.7 us -> none  [the longest x4 9.73 us: pick_rows(): local_src = perm[targets] - start]
    scatter x6 -> x0, local copies, waits for them, and re-layouts: 9.8 us -> none  [the longest x4 5.93 us: swap_order(): return base.at[own].set(piv_row).at[piv_row].set(own)]
    all_to_all x0 -> x2, starting transfers between devices: none -> 7.56 us  [spread(): lax.all_to_all(jnp.broadcast_to(x[None], (n,) + x.shape), axis, 0, 0, til...]
  transfers between devices with their start and end apart: 3 -> 4, of which waited for: 3 -> 4; matrix products, arithmetic and copies ran while one was open for 5% -> 0% of each run, Pallas kernels for 0% -> 0%
where the time goes in v1:
time: 118 us
  waiting for transfers between devices  35.4 us (30%)
  blocking collectives  33.7 us (29%)
  starting transfers between devices  22.2 us (19%)
  matrix products  20.4 us (17%)
  local copies, waits for them, and re-layouts  3.45 us (3%)
  other arithmetic  1.85 us (2%)
    all_to_all x2, waiting for transfers between devices, spread(): lax.all_to_all(jnp.broadcast_to(x[None], (n,) + x.shape), axis, 0, 0, til...  32.8 us
    dot_general x38, matrix products, mm(): lax.dot_general(a, b, (((ca,), (cb,)), ((), ())), precision=lax.Precision...  20.4 us
    all_to_all x1, blocking collectives, spread(): lax.all_to_all(jnp.broadcast_to(x[None], (n,) + x.shape), axis, 0, 0, til...  17.1 us
    all_to_all x1, blocking collectives, body(): lax.all_to_all(part, 'row', 0, 0, tiled=True, axis_index_groups=Z_GROUPS)  16.7 us
    ppermute x1, starting transfers between devices, body(): got = lax.ppermute(jnp.concatenate([other, tiles], 1), 'row', PAIR)  8.75 us
    all_to_all x2, starting transfers between devices, spread(): lax.all_to_all(jnp.broadcast_to(x[None], (n,) + x.shape), axis, 0, 0, til...  7.56 us
    ppermute x1, starting transfers between devices, body(): got = lax.ppermute(wide, 'row', PAIR)  5.92 us
  transfers between devices with their start and end apart: 4, of which 4 were waited for; matrix products, arithmetic and copies ran while one was open for 0% of the time, Pallas kernels for 0%

profile of v1, /device:TPU:1, one launch (start us, length us, event | category | flops | bytes accessed | tf_op | source)
XLA Modules:
  0.0 117.7 jit_solution(13416108908017804442)
XLA Ops:
  0.0 0.8 fusion.17
  1.0 1.1 convolution_bitcast_fusion
  2.1 0.8 slice_select_fusion.5
  2.9 2.0 %fusion = f32[1024,128]{1,0:T(8,128)S(1)} fusion(f32[512,128]{1,0:T(8,128)} %param.3, s32[1024]{0:T(1024)S(1)} %add_subtract_fusion), kind=kOutput, calls=%fused_computation.1 | convolution fusion | flops 805830656 | bytes 790528 | tf_op jit(solution)/shard_map/dot_general | solution.py:16
  5.1 8.7 %collective-permute-start = (f32[8,72,128]{2,1,0:T(8,128)S(1)}, f32[8,72,128]{2,1,0:T(8,128)S(1)}, u32[]{:S(2)}, u32[]{:S(2)}) collective-permute-start(f32[8,72,128]{2,1,0:T(8,128)S(1)} %pad_maximum_fusion.1), channel_id=1, source_target_pairs={{0,32},{32,0},{64,96},{96,64},{128,160},{160,128},{192,224},{224,1... | collective-permute-start | bytes 884744 | tf_op jit(solution)/shard_map/ppermute | solution.py:68
  13.9 1.2 %collective-permute-done = f32[8,72,128]{2,1,0:T(8,128)S(1)} collective-permute-done((f32[8,72,128]{2,1,0:T(8,128)S(1)}, f32[8,72,128]{2,1,0:T(8,128)S(1)}, u32[]{:S(2)}, u32[]{:S(2)}) %collective-permute-start) | collective-permute-done | bytes 294944 | tf_op jit(solution)/shard_map/ppermute | solution.py:68
  15.1 16.7 %all_to_all.20 = f32[8,72,128]{2,1,0:T(8,128)S(1)} all-to-all(f32[8,72,128]{2,1,0:T(8,128)S(1)} %fusion.3), channel_id=1, replica_groups={{0,64,128,192,256,320,384,448},{32,96,160,224,288,352,416,480},{1,65,12..., dimensions={0} | all-to-all | bytes 589824 | tf_op jit(solution)/shard_map/all_to_all | solution.py:70
  31.9 17.1 %all_to_all.21 = f32[8,72,128]{2,1,0:T(8,128)S(1)} all-to-all(f32[8,72,128]{2,1,0:T(8,128)S(1)} %broadcast_in_dim.73), channel_id=1, replica_groups={{0,4,8,12,16,20,24,28},{1,5,9,13,17,21,25,29},{2,6,10,14,18,22,26,30},{..., dimensions={0} | all-to-all | bytes 589824 | tf_op jit(solution)/shard_map/all_to_all | solution.py:24
  48.9 1.1 broadcast_in_dim.74
  50.0 4.0 %all-to-all-start.2 = ((f32[4,8,72,128]{3,2,1,0:T(8,128)}), f32[4,8,72,128]{3,2,1,0:T(8,128)S(1)}, u32[]{:S(2)}, u32[]{:S(2)}) async-start(f32[4,8,72,128]{3,2,1,0:T(8,128)} %broadcast_in_dim.74), calls=%async_computation.2 | async-start | bytes 2359296 | tf_op jit(solution)/shard_map/all_to_all | solution.py:24
  54.0 12.9 %all-to-all-done.2 = f32[4,8,72,128]{3,2,1,0:T(8,128)S(1)} async-done(((f32[4,8,72,128]{3,2,1,0:T(8,128)}), f32[4,8,72,128]{3,2,1,0:T(8,128)S(1)}, u32[]{:S(2)}, u32[]{:S(2)}) %all-to-all-start.2) | async-done | bytes 1179680 | tf_op jit(solution)/shard_map/all_to_all | solution.py:24
  67.0 0.9 broadcast_in_dim.75
  68.0 3.5 %all-to-all-start.3 = ((f32[8,192,128]{2,1,0:T(8,128)}), f32[8,192,128]{2,1,0:T(8,128)S(1)}, u32[]{:S(2)}, u32[]{:S(2)}) async-start(f32[8,192,128]{2,1,0:T(8,128)} %broadcast_in_dim.75), calls=%async_computation.3 | async-start | bytes 1572864 | tf_op jit(solution)/shard_map/all_to_all | solution.py:24
  71.8 19.9 %all-to-all-done.3 = f32[8,192,128]{2,1,0:T(8,128)S(1)} async-done(((f32[8,192,128]{2,1,0:T(8,128)}), f32[8,192,128]{2,1,0:T(8,128)S(1)}, u32[]{:S(2)}, u32[]{:S(2)}) %all-to-all-start.3) | async-done | bytes 786464 | tf_op jit(solution)/shard_map/all_to_all | solution.py:24
  91.7 5.9 %collective-permute-start.1 = (f32[8,192,128]{2,1,0:T(8,128)S(1)}, f32[8,192,128]{2,1,0:T(8,128)S(1)}, u32[]{:S(2)}, u32[]{:S(2)}) collective-permute-start(f32[8,192,128]{2,1,0:T(8,128)S(1)} %all-to-all-done.3), channel_id=1, source_target_pairs={{0,32},{32,0},{64,96},{96,64},{128,160},{160,128},{192,224},{224,1... | collective-permute-start | bytes 2359304 | tf_op jit(solution)/shard_map/ppermute | solution.py:82
  98.0 1.4 %collective-permute-done.1 = f32[8,192,128]{2,1,0:T(8,128)S(1)} collective-permute-done((f32[8,192,128]{2,1,0:T(8,128)S(1)}, f32[8,192,128]{2,1,0:T(8,128)S(1)}, u32[]{:S(2)}, u32[]{:S(2)}) %collective-permute-start.1) | collective-permute-done | bytes 786464 | tf_op jit(solution)/shard_map/ppermute | solution.py:82
  99.8 0.4 fusion.18
  100.2 0.4 fusion.19
  100.6 0.4 convolution_add_fusion.13
  101.0 0.4 fusion.20
  101.4 0.4 convolution_add_fusion.12
  102.2 0.4 convolution_add_fusion.11
  102.6 0.4 fusion.22
  103.0 0.4 convolution_add_fusion.10
  103.7 0.4 convolution_add_fusion.9
  104.1 0.4 fusion.24
  104.5 0.4 convolution_add_fusion.8
  104.9 0.4 fusion.26
  105.4 0.4 fusion.27
  105.7 0.4 convolution_add_fusion.6
  106.5 0.4 convolution_add_fusion.5
  106.9 0.4 fusion.29
  107.3 0.4 convolution_add_fusion.4
  108.1 0.4 convolution_add_fusion.3
  108.5 0.4 fusion.31
  108.9 0.4 convolution_add_fusion.2
  109.3 0.4 fusion.32
  109.6 0.4 convolution_add_fusion.1
  110.2 0.7 convolution_select_fusion
  110.9 0.4 convolution_add_fusion.7
  111.3 0.6 fusion.25
  111.9 1.2 %convolution_subtract_fusion.1 = f32[512,128]{1,0:T(8,128)S(1)} fusion(f32[512,128]{1,0:T(8,128)S(1)} %convolution_select_fusion, f32[256,512]{1,0:T(8,128)S(1)} %bitcast.122, f32[256,128]{1,0:T(8,128)S(1)} %fusion.25), kind=kOutput, calls=%fused_computation.17 | convolution fusion | flops 201392128 | bytes 1179648 | tf_op jit(solution)/shard_map/dot_general | solution.py:16
  113.1 0.6 bitcast_subtract_fusion
  113.7 0.4 convolution_add_fusion
  114.1 0.6 bitcast_subtract_fusion.1
  114.7 0.6 fusion.33
  115.3 0.7 convolution_select_fusion.1
  116.0 1.7 %fusion.1 = f32[512,128]{1,0:T(8,128)} fusion(f32[512,128]{1,0:T(8,128)S(1)} %convolution_select_fusion.1, f32[256,512]{1,0:T(8,128)S(1)} %bitcast.121, f32[256,128]{1,0:T(8,128)S(1)} %fusion.33, f32[256,128]{1,0:T(8,128)S(1)} %fusion.25, pred[]{:T(512)S(6)} %eq.40), kind=kOutput, calls=%fused_computation.20 | convolution fusion | flops 201523200 | bytes 1310721 | tf_op jit(solution)/shard_map/dot_general | solution.py:16
  (49 shorter events, 3.3 us)
Async XLA Ops:
  5.1 26.7 %copy-start.1 = (f32[2,512,8]{1,2,0:T(8,128)S(1)}, f32[2,512,8]{1,2,0:T(8,128)}, u32[]{:S(2)}) copy-start(f32[2,512,8]{1,2,0:T(8,128)} %param.4) | copy-start | bytes 98308
  5.1 9.9 %collective-permute-start = (f32[8,72,128]{2,1,0:T(8,128)S(1)}, f32[8,72,128]{2,1,0:T(8,128)S(1)}, u32[]{:S(2)}, u32[]{:S(2)}) collective-permute-start(f32[8,72,128]{2,1,0:T(8,128)S(1)} %pad_maximum_fusion.1), channel_id=1, source_target_pairs={{0,32},{32,0},{64,96},{96,64},{128,160},{160,128},{192,224},{224,1... | collective-permute-start | bytes 884744 | tf_op jit(solution)/shard_map/ppermute | solution.py:68
  50.0 17.0 %all-to-all-start.2 = ((f32[4,8,72,128]{3,2,1,0:T(8,128)}), f32[4,8,72,128]{3,2,1,0:T(8,128)S(1)}, u32[]{:S(2)}, u32[]{:S(2)}) async-start(f32[4,8,72,128]{3,2,1,0:T(8,128)} %broadcast_in_dim.74), calls=%async_computation.2 | async-start | bytes 2359296 | tf_op jit(solution)/shard_map/all_to_all | solution.py:24
  68.0 23.7 %all-to-all-start.3 = ((f32[8,192,128]{2,1,0:T(8,128)}), f32[8,192,128]{2,1,0:T(8,128)S(1)}, u32[]{:S(2)}, u32[]{:S(2)}) async-start(f32[8,192,128]{2,1,0:T(8,128)} %broadcast_in_dim.75), calls=%async_computation.3 | async-start | bytes 1572864 | tf_op jit(solution)/shard_map/all_to_all | solution.py:24
  91.7 7.6 %collective-permute-start.1 = (f32[8,192,128]{2,1,0:T(8,128)S(1)}, f32[8,192,128]{2,1,0:T(8,128)S(1)}, u32[]{:S(2)}, u32[]{:S(2)}) collective-permute-start(f32[8,192,128]{2,1,0:T(8,128)S(1)} %all-to-all-done.3), channel_id=1, source_target_pairs={{0,32},{32,0},{64,96},{96,64},{128,160},{160,128},{192,224},{224,1... | collective-permute-start | bytes 2359304 | tf_op jit(solution)/shard_map/ppermute | solution.py:82
  109.2 1.0 copy-start

commit v2 on v1

--- a/solution.py
+++ b/solution.py
@@ -7,8 +7,9 @@
 NZ, NC = 8, 2
 NY, NX = 8, 4
 Z_GROUPS = [[NC * z + core for z in range(NZ)] for core in range(NC)]
-X_GROUPS = [[NX * y + x for x in range(NX)] for y in range(NY)]
-Y_GROUPS = [[NX * y + x for y in range(NY)] for x in range(NX)]
+ORDER = [0]
+for step in (4, 8, 16, 1, 2):
+    ORDER = ORDER + [i ^ step for i in ORDER]
 PAIR = [(i, i ^ 1) for i in range(NZ * NC)]
 
 
@@ -24,6 +25,11 @@
     return lax.all_to_all(
         jnp.broadcast_to(x[None], (n,) + x.shape), axis, 0, 0, tiled=True, axis_index_groups=groups
     )
+
+
+def double(x, step):
+    pairs = [(i, i ^ step) for i in range(NX * NY)]
+    return jnp.concatenate([x, lax.ppermute(x, "col", pairs)], 0)
 
 
 def invert_t(diag_t):
@@ -67,26 +73,35 @@
     other = jnp.where(core == 0, rows[1], rows[0])
     got = lax.ppermute(jnp.concatenate([other, tiles], 1), "row", PAIR)
     part = jnp.concatenate([mine, tiles], 1) + got
+    near = pan_t.reshape(2, 8, 4, 128).transpose(0, 2, 1, 3).reshape(1, 64, 128)
+
+    part, near = lax.optimization_barrier((part, near))
     part = lax.all_to_all(part, "row", 0, 0, tiled=True, axis_index_groups=Z_GROUPS)
+    near = double(near, 4)
+    near = double(near, 8)
+    part, near = lax.optimization_barrier((part, near))
+
     part = jnp.sum(part, 0)
+    tile = lax.all_to_all(jnp.broadcast_to(part[64:], (NX * NY, 8, 128)), "col", 0, 0, tiled=True)
+    near = double(near, 16)
+    tile, near = lax.optimization_barrier((tile, near))
 
-    own_tiles = pan_t.reshape(2, 8, 4, 128).transpose(0, 2, 1, 3).reshape(64, 128)
-    sent = jnp.concatenate([own_tiles, part[64:]], 0)
-    sent = spread(sent, "col", Y_GROUPS)
-    sent = spread(sent, "col", X_GROUPS)
-    lower_t = sent[:, :, :64].reshape(NX, NY, 2, 4, 8, 128).transpose(2, 1, 0, 4, 3, 5).reshape(2, PW, 512)
-    tile = sent[:, :, 64:]
-    half = jnp.where(core == 0, tile[:2], tile[2:]).reshape(128, 128)
+    half = jnp.where(core == 0, tile[:16], tile[16:]).reshape(128, 128)
+    wide = spread(jnp.concatenate([part[:64], half], 0), "row", Z_GROUPS)
+    near = double(near, 1)
+    near = double(near, 2)
+    wide, near = lax.optimization_barrier((wide, near))
 
-    wide = spread(jnp.concatenate([part[:64], half], 0), "row", Z_GROUPS)
     got = lax.ppermute(wide, "row", PAIR)
     low = jnp.where(core == 0, wide, got)
     high = jnp.where(core == 0, got, wide)
     both = jnp.stack([low, high])
     top = both[:, :, :32].reshape(512, 128)
     moved = both[:, :, 32:64].reshape(512, 128)
-    square = both[:, :, 64:].reshape(NC, 4, 2, 2, NY, 8, 128)
-    square = square.transpose(1, 4, 0, 3, 5, 2, 6).reshape(4, PW, PW)
+    square = both[:, :, 64:].reshape(NC, 4, 2, 16, 8, 128)
+    square = square.transpose(1, 0, 3, 4, 2, 5).reshape(4, PW, PW)
+    lower_t = near.reshape(32, 2, 4, 8, 128).transpose(1, 0, 3, 2, 4).reshape(2, PW, 512)
+    seen = lax.axis_index("col") ^ jnp.array(ORDER, jnp.int32)
 
     upper0 = mm(invert_t(square[0]), top[:PW], 0, 0)
     upper1 = mm(invert_t(square[1]), top[PW:] - mm(square[3], upper0, 0, 0), 0, 0)
@@ -95,8 +110,8 @@
     at0 = (p0[:, None] - start == lane[None, :]).astype(jnp.float32)
     in0 = jnp.sum(at0, 0)[:, None] > 0
     in1 = jnp.sum(at1, 0)[:, None] > 0
-    work = jnp.where(in0, mm(at0, moved[:PW], 0, 0), block) - mm(lower_t[0], upper0, 0, 0)
-    work = jnp.where(in1, mm(at1, second, 0, 0), work) - mm(lower_t[1], upper1, 0, 0)
+    work = jnp.where(in0, mm(at0, moved[:PW], 0, 0), block) - mm(lower_t[0], upper0.reshape(32, 8, 128)[seen].reshape(PW, 128), 0, 0)
+    work = jnp.where(in1, mm(at1, second, 0, 0), work) - mm(lower_t[1], upper1.reshape(32, 8, 128)[seen].reshape(PW, 128), 0, 0)
     return jnp.where(first, jnp.concatenate([upper0, upper1], 0), work)
 
 

time: 118 us -> 112 us (0.949); the launches traced: 118 us -> 110 us
  starting transfers between devices: 22.2 us -> 57.5 us
  blocking collectives: 33.7 us -> 0 us
  waiting for transfers between devices: 35.4 us -> 25.3 us
    all_to_all x2 -> x0, blocking collectives: 33.7 us -> none  [the longest x1 17.1 us: spread(): lax.all_to_all(jnp.broadcast_to(x[None], (n,) + x.shape), axis, 0, 0, til...]
    all_to_all x2 -> x1, waiting for transfers between devices: 32.8 us -> 0.01 us  [spread(): lax.all_to_all(jnp.broadcast_to(x[None], (n,) + x.shape), axis, 0, 0, til...]
    ppermute x0 -> x5, starting transfers between devices: none -> 22.2 us  [double(): return jnp.concatenate([x, lax.ppermute(x, 'col', pairs)], 0)]
    ppermute x0 -> x5, waiting for transfers between devices: none -> 21.1 us  [double(): return jnp.concatenate([x, lax.ppermute(x, 'col', pairs)], 0)]
    all_to_all x0 -> x2, starting transfers between devices: none -> 14.4 us  [the longest x1 9.67 us: body(): lax.all_to_all(jnp.broadcast_to(part[64:], (NX * NY, 8, 128)), 'col', 0,...]
    all_to_all x2 -> x1, starting transfers between devices: 7.56 us -> 4.42 us  [spread(): lax.all_to_all(jnp.broadcast_to(x[None], (n,) + x.shape), axis, 0, 0, til...]
    ppermute x1, starting transfers between devices: 5.92 us -> 7.72 us  [body(): got = lax.ppermute(wide, 'row', PAIR)]
    all_to_all x0 -> x2, waiting for transfers between devices: none -> 1.49 us  [the longest x1 1.49 us: body(): lax.all_to_all(part, 'row', 0, 0, tiled=True, axis_index_groups=Z_GROUPS)]
  transfers between devices with their start and end apart: 4 -> 10, of which waited for: 4 -> 8; matrix products, arithmetic and copies ran while one was open for 0% -> 0% of each run, Pallas kernels for 0% -> 0%
where the time goes in v2:
time: 112 us; the launch traced here: 110 us
  starting transfers between devices  57.5 us (51%)
  waiting for transfers between devices  25.3 us (23%)
  matrix products  20.5 us (18%)
  local copies, waits for them, and re-layouts  3.76 us (3%)
  other arithmetic  2.72 us (2%)
    ppermute x5, starting transfers between devices, double(): return jnp.concatenate([x, lax.ppermute(x, 'col', pairs)], 0)  22.2 us
    ppermute x5, waiting for transfers between devices, double(): return jnp.concatenate([x, lax.ppermute(x, 'col', pairs)], 0)  21.1 us
    dot_general x38, matrix products, mm(): lax.dot_general(a, b, (((ca,), (cb,)), ((), ())), precision=lax.Precision...  20.5 us
    all_to_all x1, starting transfers between devices, body(): lax.all_to_all(jnp.broadcast_to(part[64:], (NX * NY, 8, 128)), 'col', 0,...  9.67 us
    ppermute x1, starting transfers between devices, body(): got = lax.ppermute(jnp.concatenate([other, tiles], 1), 'row', PAIR)  8.75 us
    ppermute x1, starting transfers between devices, body(): got = lax.ppermute(wide, 'row', PAIR)  7.72 us
    all_to_all x1, starting transfers between devices, body(): lax.all_to_all(part, 'row', 0, 0, tiled=True, axis_index_groups=Z_GROUPS)  4.69 us
    all_to_all x1, starting transfers between devices, spread(): lax.all_to_all(jnp.broadcast_to(x[None], (n,) + x.shape), axis, 0, 0, til...  4.42 us
  transfers between devices with their start and end apart: 10, of which 8 were waited for; matrix products, arithmetic and copies ran while one was open for 0% of the time, Pallas kernels for 0%

profile of v2, /device:TPU:1, one launch (start us, length us, event | category | flops | bytes accessed | tf_op | source)
XLA Modules:
  0.0 110.4 jit_solution(1009827438301850316)
XLA Ops:
  0.0 0.8 fusion.18
  1.0 1.1 %convolution_bitcast_fusion = f32[1,8,256]{2,1,0:T(8,128)S(1)} fusion(s32[256]{0:T(256)S(1)} %get-tuple-element.45, f32[2,8,512]{2,1,0:T(8,128)} %bitcast.145), kind=kOutput, calls=%fused_computation.23 | convolution fusion | flops 12713984 | bytes 25600 | tf_op jit(solution)/shard_map/dot_general | solution.py:17
  2.1 0.8 slice_select_fusion.4
  2.9 2.0 %fusion = f32[1024,128]{1,0:T(8,128)S(1)} fusion(f32[512,128]{1,0:T(8,128)} %param.4, s32[1024]{0:T(1024)S(1)} %add_subtract_fusion), kind=kOutput, calls=%fused_computation.3 | convolution fusion | flops 805830656 | bytes 790528 | tf_op jit(solution)/shard_map/dot_general | solution.py:17
  5.1 8.7 %collective-permute-start = (f32[8,72,128]{2,1,0:T(8,128)S(1)}, f32[8,72,128]{2,1,0:T(8,128)S(1)}, u32[]{:S(2)}, u32[]{:S(2)}) collective-permute-start(f32[8,72,128]{2,1,0:T(8,128)S(1)} %pad_maximum_fusion.3), channel_id=1, source_target_pairs={{0,32},{32,0},{64,96},{96,64},{128,160},{160,128},{192,224},{224,1... | collective-permute-start | bytes 884744 | tf_op jit(solution)/shard_map/ppermute | solution.py:74
  13.9 1.2 %collective-permute-done = f32[8,72,128]{2,1,0:T(8,128)S(1)} collective-permute-done((f32[8,72,128]{2,1,0:T(8,128)S(1)}, f32[8,72,128]{2,1,0:T(8,128)S(1)}, u32[]{:S(2)}, u32[]{:S(2)}) %collective-permute-start) | collective-permute-done | bytes 294944 | tf_op jit(solution)/shard_map/ppermute | solution.py:74
  15.1 0.7 fusion.3
  15.8 4.7 %all-to-all-start = ((f32[8,72,128]{2,1,0:T(8,128)}), f32[8,72,128]{2,1,0:T(8,128)S(1)}, u32[]{:S(2)}, u32[]{:S(2)}) async-start(f32[8,72,128]{2,1,0:T(8,128)} %fusion.3), calls=%async_computation | async-start | bytes 589824 | tf_op jit(solution)/shard_map/all_to_all | solution.py:79
  20.5 3.2 %collective-permute-start.1 = (f32[1,64,128]{2,1,0:T(8,128)S(1)}, f32[1,64,128]{2,1,0:T(8,128)S(1)}, u32[]{:S(2)}, u32[]{:S(2)}) collective-permute-start(f32[1,64,128]{2,1,0:T(8,128)S(1)} %bitcast.147), channel_id=1, source_target_pairs={{0,4},{1,5},{2,6},{3,7},{4,0},{5,1},{6,2},{7,3},{8,12},{9,13},{10,... | collective-permute-start | bytes 98312 | tf_op jit(solution)/shard_map/ppermute | solution.py:32
  23.7 1.7 %collective-permute-done.1 = f32[1,64,128]{2,1,0:T(8,128)S(1)} collective-permute-done((f32[1,64,128]{2,1,0:T(8,128)S(1)}, f32[1,64,128]{2,1,0:T(8,128)S(1)}, u32[]{:S(2)}, u32[]{:S(2)}) %collective-permute-start.1) | collective-permute-done | bytes 32800 | tf_op jit(solution)/shard_map/ppermute | solution.py:32
  25.5 4.2 %collective-permute-start.2 = (f32[2,64,128]{2,1,0:T(8,128)S(1)}, f32[2,64,128]{2,1,0:T(8,128)S(1)}, u32[]{:S(2)}, u32[]{:S(2)}) collective-permute-start(f32[2,64,128]{2,1,0:T(8,128)S(1)} %pad_maximum_fusion.8), channel_id=1, source_target_pairs={{0,8},{1,9},{2,10},{3,11},{4,12},{5,13},{6,14},{7,15},{8,0},{9,1},... | collective-permute-start | bytes 196616 | tf_op jit(solution)/shard_map/ppermute | solution.py:32
  29.7 1.7 %collective-permute-done.2 = f32[2,64,128]{2,1,0:T(8,128)S(1)} collective-permute-done((f32[2,64,128]{2,1,0:T(8,128)S(1)}, f32[2,64,128]{2,1,0:T(8,128)S(1)}, u32[]{:S(2)}, u32[]{:S(2)}) %collective-permute-start.2) | collective-permute-done | bytes 65568 | tf_op jit(solution)/shard_map/ppermute | solution.py:32
  31.4 1.5 %all-to-all-done = f32[8,72,128]{2,1,0:T(8,128)S(1)} async-done(((f32[8,72,128]{2,1,0:T(8,128)}), f32[8,72,128]{2,1,0:T(8,128)S(1)}, u32[]{:S(2)}, u32[]{:S(2)}) %all-to-all-start) | async-done | bytes 294944 | tf_op jit(solution)/shard_map/all_to_all | solution.py:79
  32.9 0.7 broadcast_in_dim.68
  33.6 9.7 %all-to-all-start.1 = ((f32[32,8,128]{2,1,0:T(8,128)}), f32[32,8,128]{2,1,0:T(8,128)S(1)}, u32[]{:S(2)}, u32[]{:S(2)}) async-start(f32[32,8,128]{2,1,0:T(8,128)} %broadcast_in_dim.68), calls=%async_computation.1 | async-start | bytes 262144 | tf_op jit(solution)/shard_map/all_to_all | solution.py:85
  43.2 7.1 %collective-permute-start.3 = (f32[4,64,128]{2,1,0:T(8,128)S(1)}, f32[4,64,128]{2,1,0:T(8,128)S(1)}, u32[]{:S(2)}, u32[]{:S(2)}) collective-permute-start(f32[4,64,128]{2,1,0:T(8,128)S(1)} %pad_maximum_fusion.6), channel_id=1, source_target_pairs={{0,16},{1,17},{2,18},{3,19},{4,20},{5,21},{6,22},{7,23},{8,24},{9,... | collective-permute-start | bytes 393224 | tf_op jit(solution)/shard_map/ppermute | solution.py:32
  50.3 4.3 %collective-permute-done.3 = f32[4,64,128]{2,1,0:T(8,128)S(1)} collective-permute-done((f32[4,64,128]{2,1,0:T(8,128)S(1)}, f32[4,64,128]{2,1,0:T(8,128)S(1)}, u32[]{:S(2)}, u32[]{:S(2)}) %collective-permute-start.3) | collective-permute-done | bytes 131104 | tf_op jit(solution)/shard_map/ppermute | solution.py:32
  54.7 0.9 broadcast_in_dim.69
  55.7 4.4 %all-to-all-start.2 = ((f32[8,192,128]{2,1,0:T(8,128)}), f32[8,192,128]{2,1,0:T(8,128)S(1)}, u32[]{:S(2)}, u32[]{:S(2)}) async-start(f32[8,192,128]{2,1,0:T(8,128)} %broadcast_in_dim.69), calls=%async_computation.2 | async-start | bytes 1572864 | tf_op jit(solution)/shard_map/all_to_all | solution.py:25
  60.1 3.0 %collective-permute-start.4 = (f32[8,64,128]{2,1,0:T(8,128)S(1)}, f32[8,64,128]{2,1,0:T(8,128)S(1)}, u32[]{:S(2)}, u32[]{:S(2)}) collective-permute-start(f32[8,64,128]{2,1,0:T(8,128)S(1)} %pad_maximum_fusion.5), channel_id=1, source_target_pairs={{0,1},{1,0},{2,3},{3,2},{4,5},{5,4},{6,7},{7,6},{8,9},{9,8},{10,11... | collective-permute-start | bytes 786440 | tf_op jit(solution)/shard_map/ppermute | solution.py:32
  63.2 4.0 %collective-permute-done.4 = f32[8,64,128]{2,1,0:T(8,128)S(1)} collective-permute-done((f32[8,64,128]{2,1,0:T(8,128)S(1)}, f32[8,64,128]{2,1,0:T(8,128)S(1)}, u32[]{:S(2)}, u32[]{:S(2)}) %collective-permute-start.4) | collective-permute-done | bytes 262176 | tf_op jit(solution)/shard_map/ppermute | solution.py:32
  67.2 4.7 %collective-permute-start.5 = (f32[16,64,128]{2,1,0:T(8,128)S(1)}, f32[16,64,128]{2,1,0:T(8,128)S(1)}, u32[]{:S(2)}, u32[]{:S(2)}) collective-permute-start(f32[16,64,128]{2,1,0:T(8,128)S(1)} %pad_maximum_fusion.2), channel_id=1, source_target_pairs={{0,2},{1,3},{2,0},{3,1},{4,6},{5,7},{6,4},{7,5},{8,10},{9,11},{10,... | collective-permute-start | bytes 1572872 | tf_op jit(solution)/shard_map/ppermute | solution.py:32
  72.1 9.3 %collective-permute-done.5 = f32[16,64,128]{2,1,0:T(8,128)S(1)} collective-permute-done((f32[16,64,128]{2,1,0:T(8,128)S(1)}, f32[16,64,128]{2,1,0:T(8,128)S(1)}, u32[]{:S(2)}, u32[]{:S(2)}) %collective-permute-start.5) | collective-permute-done | bytes 524320 | tf_op jit(solution)/shard_map/ppermute | solution.py:32
  81.5 7.7 %collective-permute-start.6 = (f32[8,192,128]{2,1,0:T(8,128)S(1)}, f32[8,192,128]{2,1,0:T(8,128)S(1)}, u32[]{:S(2)}, u32[]{:S(2)}) collective-permute-start(f32[8,192,128]{2,1,0:T(8,128)S(1)} %all-to-all-done.2), channel_id=1, source_target_pairs={{0,32},{32,0},{64,96},{96,64},{128,160},{160,128},{192,224},{224,1... | collective-permute-start | bytes 2359304 | tf_op jit(solution)/shard_map/ppermute | solution.py:95
  89.4 1.5 %collective-permute-done.6 = f32[8,192,128]{2,1,0:T(8,128)S(1)} collective-permute-done((f32[8,192,128]{2,1,0:T(8,128)S(1)}, f32[8,192,128]{2,1,0:T(8,128)S(1)}, u32[]{:S(2)}, u32[]{:S(2)}) %collective-permute-start.6) | collective-permute-done | bytes 786464 | tf_op jit(solution)/shard_map/ppermute | solution.py:95
  91.4 0.4 fusion.19
  91.9 0.4 fusion.20
  92.2 0.4 convolution_add_fusion.13
  92.6 0.4 fusion.21
  93.0 0.4 convolution_add_fusion.12
  93.4 0.4 fusion.22
  94.2 0.4 fusion.23
  94.6 0.4 convolution_add_fusion.10
  96.1 0.4 convolution_add_fusion.8
  97.4 0.4 convolution_add_fusion.6
  97.8 0.4 fusion.29
  99.7 0.4 convolution_add_fusion.3
  102.1 0.6 fusion.26
  102.7 0.6 gather_fusion
  103.3 0.4 convolution_add_fusion
  103.7 0.6 bitcast_subtract_fusion.1
  104.3 0.8 fusion.34
  105.1 0.6 gather_fusion.1
  105.7 0.7 convolution_select_fusion
  106.4 0.6 bitcast_subtract_fusion
  107.0 1.0 convolution_subtract_fusion.1
  108.0 0.7 convolution_select_fusion.1
  108.7 1.7 %fusion.1 = f32[512,128]{1,0:T(8,128)} fusion(f32[512,128]{1,0:T(8,128)S(1)} %convolution_select_fusion.1, f32[2,32,8,4,128]{4,2,3,0,1:T(8,128)S(1)} %bitcast.128, f32[256,128]{1,0:T(8,128)S(1)} %fusion.34, f32[256,128]{1,0:T(8,128)S(1)} %fusion.26, f32[32,8,128]{2,1,0:T(8,128)S(1)} %gather_fusion.1, pred[]{:T(512)S(6)} %eq.40), kind=kOutput, calls=%fused_computation.22 | convolution fusion | flops 201523200 | bytes 1441793 | tf_op jit(solution)/shard_map/dot_general | solution.py:17
  (64 shorter events, 7.1 us)
Async XLA Ops:
  5.1 15.4 %copy-start.1 = (f32[2,512,8]{1,2,0:T(8,128)S(1)}, f32[2,512,8]{1,2,0:T(8,128)}, u32[]{:S(2)}) copy-start(f32[2,512,8]{1,2,0:T(8,128)} %param.5) | copy-start | bytes 98308
  5.1 9.9 %collective-permute-start = (f32[8,72,128]{2,1,0:T(8,128)S(1)}, f32[8,72,128]{2,1,0:T(8,128)S(1)}, u32[]{:S(2)}, u32[]{:S(2)}) collective-permute-start(f32[8,72,128]{2,1,0:T(8,128)S(1)} %pad_maximum_fusion.3), channel_id=1, source_target_pairs={{0,32},{32,0},{64,96},{96,64},{128,160},{160,128},{192,224},{224,1... | collective-permute-start | bytes 884744 | tf_op jit(solution)/shard_map/ppermute | solution.py:74
  15.8 17.1 %all-to-all-start = ((f32[8,72,128]{2,1,0:T(8,128)}), f32[8,72,128]{2,1,0:T(8,128)S(1)}, u32[]{:S(2)}, u32[]{:S(2)}) async-start(f32[8,72,128]{2,1,0:T(8,128)} %fusion.3), calls=%async_computation | async-start | bytes 589824 | tf_op jit(solution)/shard_map/all_to_all | solution.py:79
  20.5 5.0 %collective-permute-start.1 = (f32[1,64,128]{2,1,0:T(8,128)S(1)}, f32[1,64,128]{2,1,0:T(8,128)S(1)}, u32[]{:S(2)}, u32[]{:S(2)}) collective-permute-start(f32[1,64,128]{2,1,0:T(8,128)S(1)} %bitcast.147), channel_id=1, source_target_pairs={{0,4},{1,5},{2,6},{3,7},{4,0},{5,1},{6,2},{7,3},{8,12},{9,13},{10,... | collective-permute-start | bytes 98312 | tf_op jit(solution)/shard_map/ppermute | solution.py:32
  25.5 5.9 %collective-permute-start.2 = (f32[2,64,128]{2,1,0:T(8,128)S(1)}, f32[2,64,128]{2,1,0:T(8,128)S(1)}, u32[]{:S(2)}, u32[]{:S(2)}) collective-permute-start(f32[2,64,128]{2,1,0:T(8,128)S(1)} %pad_maximum_fusion.8), channel_id=1, source_target_pairs={{0,8},{1,9},{2,10},{3,11},{4,12},{5,13},{6,14},{7,15},{8,0},{9,1},... | collective-permute-start | bytes 196616 | tf_op jit(solution)/shard_map/ppermute | solution.py:32
  33.6 21.1 %all-to-all-start.1 = ((f32[32,8,128]{2,1,0:T(8,128)}), f32[32,8,128]{2,1,0:T(8,128)S(1)}, u32[]{:S(2)}, u32[]{:S(2)}) async-start(f32[32,8,128]{2,1,0:T(8,128)} %broadcast_in_dim.68), calls=%async_computation.1 | async-start | bytes 262144 | tf_op jit(solution)/shard_map/all_to_all | solution.py:85
  43.2 11.4 %collective-permute-start.3 = (f32[4,64,128]{2,1,0:T(8,128)S(1)}, f32[4,64,128]{2,1,0:T(8,128)S(1)}, u32[]{:S(2)}, u32[]{:S(2)}) collective-permute-start(f32[4,64,128]{2,1,0:T(8,128)S(1)} %pad_maximum_fusion.6), channel_id=1, source_target_pairs={{0,16},{1,17},{2,18},{3,19},{4,20},{5,21},{6,22},{7,23},{8,24},{9,... | collective-permute-start | bytes 393224 | tf_op jit(solution)/shard_map/ppermute | solution.py:32
  55.7 16.3 %copy-start.2 = (s32[32]{0:T(128)S(1)}, s32[32]{0:T(128)}, u32[]{:S(2)}) copy-start(s32[32]{0:T(128)} %constant.58.clone) | copy-start | bytes 388
  55.7 25.9 %all-to-all-start.2 = ((f32[8,192,128]{2,1,0:T(8,128)}), f32[8,192,128]{2,1,0:T(8,128)S(1)}, u32[]{:S(2)}, u32[]{:S(2)}) async-start(f32[8,192,128]{2,1,0:T(8,128)} %broadcast_in_dim.69), calls=%async_computation.2 | async-start | bytes 1572864 | tf_op jit(solution)/shard_map/all_to_all | solution.py:25
  60.1 7.1 %collective-permute-start.4 = (f32[8,64,128]{2,1,0:T(8,128)S(1)}, f32[8,64,128]{2,1,0:T(8,128)S(1)}, u32[]{:S(2)}, u32[]{:S(2)}) collective-permute-start(f32[8,64,128]{2,1,0:T(8,128)S(1)} %pad_maximum_fusion.5), channel_id=1, source_target_pairs={{0,1},{1,0},{2,3},{3,2},{4,5},{5,4},{6,7},{7,6},{8,9},{9,8},{10,11... | collective-permute-start | bytes 786440 | tf_op jit(solution)/shard_map/ppermute | solution.py:32
  67.2 14.2 %collective-permute-start.5 = (f32[16,64,128]{2,1,0:T(8,128)S(1)}, f32[16,64,128]{2,1,0:T(8,128)S(1)}, u32[]{:S(2)}, u32[]{:S(2)}) collective-permute-start(f32[16,64,128]{2,1,0:T(8,128)S(1)} %pad_maximum_fusion.2), channel_id=1, source_target_pairs={{0,2},{1,3},{2,0},{3,1},{4,6},{5,7},{6,4},{7,5},{8,10},{9,11},{10,... | collective-permute-start | bytes 1572872 | tf_op jit(solution)/shard_map/ppermute | solution.py:32
  81.5 9.4 %collective-permute-start.6 = (f32[8,192,128]{2,1,0:T(8,128)S(1)}, f32[8,192,128]{2,1,0:T(8,128)S(1)}, u32[]{:S(2)}, u32[]{:S(2)}) collective-permute-start(f32[8,192,128]{2,1,0:T(8,128)S(1)} %all-to-all-done.2), channel_id=1, source_target_pairs={{0,32},{32,0},{64,96},{96,64},{128,160},{160,128},{192,224},{224,1... | collective-permute-start | bytes 2359304 | tf_op jit(solution)/shard_map/ppermute | solution.py:95
  103.3 2.4 %copy-start = (f32[512,128]{1,0:T(8,128)S(1)}, f32[512,128]{1,0:T(8,128)}, u32[]{:S(2)}) copy-start(f32[512,128]{1,0:T(8,128)} %param.4) | copy-start | bytes 786436

commit v3 on v2

v3 whole, which is shorter than its diff:
```python
import jax
import jax.numpy as jnp
from jax import lax
from jax.sharding import PartitionSpec as P


PW = 256
NZ, NC = 8, 2
NY, NX = 8, 4
Z_GROUPS = [[NC * z + core for z in range(NZ)] for core in range(NC)]
Y_GROUPS = [[NX * y + x for y in range(NY)] for x in range(NX)]
PAIR = [(i, i ^ 1) for i in range(NZ * NC)]


def mm(a, b, ca=1, cb=0):
    return lax.dot_general(
        a, b, (((ca,), (cb,)), ((), ())),
        precision=lax.Precision.HIGH, preferred_element_type=jnp.float32,
    )


def spread(x, axis, groups):
    n = len(groups[0])
    return lax.all_to_all(
        jnp.broadcast_to(x[None], (n,) + x.shape), axis, 0, 0, tiled=True, axis_index_groups=groups
    )


def double(x, step):
    pairs = [(i, i ^ step) for i in range(NX * NY)]
    return jnp.concatenate([x, lax.ppermute(x, "col", pairs)], 0)


def join(core, own, got):
    return jnp.stack([jnp.where(core == 0, own, got), jnp.where(core == 0, got, own)])


def invert_t(diag_t):
    strict = jnp.triu(diag_t, 1)
    inverse = jnp.eye(PW, dtype=jnp.float32) - strict
    power = strict
    for _ in range(1, PW.bit_length() - 1):
        power = mm(power, power)
        inverse = inverse + mm(inverse, power)
    return inverse


def step(block, panels, pivots):
    me = lax.axis_index("row")
    core = me % NC
    start = me * 512
    first = me == 0
    p0, p1 = pivots[0], pivots[1]
    j = jnp.arange(PW, dtype=jnp.int32)
    lane = jnp.arange(512, dtype=jnp.int32)

    def through0(rows):
        hit = p0[None, :] == rows[:, None]
        found = jnp.max(jnp.where(hit, j[None, :], -1), axis=1)
        return jnp.where(found >= 0, found, rows)

    source = jnp.concatenate([p0, through0(p1), j, through0(PW + j)])
    pick = (source[:, None] - start == lane[None, :]).astype(jnp.float32)
    rows = mm(pick, block).reshape(2, NC, NZ, 32, 128)
    rows = rows.transpose(1, 2, 0, 3, 4).reshape(NC, NZ, 64, 128)

    pan_t = panels.transpose(0, 2, 1)
    near = pan_t.reshape(2, 8, 4, 128).transpose(0, 2, 1, 3).reshape(64, 128)
    near = spread(near, "col", Y_GROUPS)

    at1 = (p1[:, None] - start == lane[None, :]).astype(jnp.float32)
    piv_t = mm(pan_t[0], at1, 1, 1)
    zero = jnp.zeros((8, PW), jnp.float32)
    own = lambda t: jnp.where(first, t, zero)
    pieces = jnp.stack([own(pan_t[0, :, :PW]), own(pan_t[1, :, PW:]), own(pan_t[0, :, PW:]), piv_t])
    tiles = pieces.reshape(4, 8, 2, 128).transpose(2, 0, 1, 3).reshape(2, 32, 128)

    def side(pair, mine):
        return jnp.where((core == 0) == mine, pair[0], pair[1])

    def halves(mine):
        return jnp.concatenate([side(rows, mine).reshape(512, 128), side(tiles, mine)], 0)

    part = halves(True) + lax.ppermute(halves(False), "row", PAIR)
    part = jnp.concatenate(
        [part[:512].reshape(NZ, 64, 128), jnp.broadcast_to(part[None, 512:], (NZ, 32, 128))], 1
    )
    part, near = lax.optimization_barrier((part, near))

    part = lax.all_to_all(part, "row", 0, 0, tiled=True, axis_index_groups=Z_GROUPS)
    near = double(near, 1)
    part, near = lax.optimization_barrier((part, near))

    part = jnp.sum(part, 0)
    tile = lax.all_to_all(jnp.broadcast_to(part[64:], (NX * NY, 32, 128)), "col", 0, 0, tiled=True)
    near = double(near, 2)
    tile, part, near = lax.optimization_barrier((tile, part, near))

    wide = spread(part[:64], "row", Z_GROUPS)
    far = lax.ppermute(tile, "row", PAIR)
    square = join(core, tile, far).reshape(NC, 32, 4, 8, 128)
    square = square.transpose(2, 1, 3, 0, 4).reshape(4, PW, PW)
    inverse0 = invert_t(square[0])
    inverse1 = invert_t(square[1])
    wide, inverse0, inverse1 = lax.optimization_barrier((wide, inverse0, inverse1))

    both = join(core, wide, lax.ppermute(wide, "row", PAIR))
    top = both[:, :, :32].reshape(512, 128)
    moved = both[:, :, 32:].reshape(512, 128)
    lower_t = near.reshape(32, 2, 4, 8, 128).transpose(1, 0, 3, 2, 4).reshape(2, PW, 512)
    x_at = lax.axis_index("col") % NX
    seen = jnp.concatenate([NX * jnp.arange(NY, dtype=jnp.int32) + (x_at ^ b) for b in range(NX)])

    upper0 = mm(inverse0, top[:PW], 0, 0)
    upper1 = mm(inverse1, top[PW:] - mm(square[3], upper0, 0, 0), 0, 0)
    second = moved[PW:] - mm(square[2], upper0, 0, 0)

    at0 = (p0[:, None] - start == lane[None, :]).astype(jnp.float32)
    in0 = jnp.sum(at0, 0)[:, None] > 0
    in1 = jnp.sum(at1, 0)[:, None] > 0
    work = jnp.where(in0, mm(at0, moved[:PW], 0, 0), block) - mm(lower_t[0], upper0.reshape(32, 8, 128)[seen].reshape(PW, 128), 0, 0)
    work = jnp.where(in1, mm(at1, second, 0, 0), work) - mm(lower_t[1], upper1.reshape(32, 8, 128)[seen].reshape(PW, 128), 0, 0)
    return jnp.where(first, jnp.concatenate([upper0, upper1], 0), work)


def solution(mesh):
    return jax.shard_map(
        step,
        mesh=mesh,
        in_specs=(P("row", "col"), P(None, "row", "col"), P()),
        out_specs=P("row", "col"),
        check_vma=False,
    )
```

time: 112 us -> 109 us (0.973)
  waiting for transfers between devices: 25.3 us -> 45.2 us
  starting transfers between devices: 57.5 us -> 41.6 us
  matrix products: 20.5 us -> 14.2 us
    all_to_all x1 -> x2, waiting for transfers between devices: 0.01 us -> 15.5 us  [spread(): lax.all_to_all(jnp.broadcast_to(x[None], (n,) + x.shape), axis, 0, 0, til...]
    ppermute x5 -> x2, starting transfers between devices: 22.2 us -> 7.75 us  [double(): return jnp.concatenate([x, lax.ppermute(x, 'col', pairs)], 0)]
    dot_general x38, matrix products: 20.5 us -> 14.2 us  [mm(): lax.dot_general(a, b, (((ca,), (cb,)), ((), ())), precision=lax.Precision...]
    all_to_all x2, waiting for transfers between devices: 1.49 us -> 6.05 us  [the longest x1 6.05 us: step(): lax.all_to_all(part, 'row', 0, 0, tiled=True, axis_index_groups=Z_GROUPS)]
    all_to_all x1 -> x2, starting transfers between devices: 4.42 us -> 6.83 us  [spread(): lax.all_to_all(jnp.broadcast_to(x[None], (n,) + x.shape), axis, 0, 0, til...]
    ppermute x2 -> x3, starting transfers between devices: 16.5 us -> 14.4 us  [the longest x1 8.75 us: step(): part = halves(True) + lax.ppermute(halves(False), 'row', PAIR)]
    all_to_all x2, starting transfers between devices: 14.4 us -> 12.6 us  [the longest x1 8.15 us: step(): lax.all_to_all(part, 'row', 0, 0, tiled=True, axis_index_groups=Z_GROUPS)]
    ppermute x2 -> x3, waiting for transfers between devices: 2.73 us -> 0.94 us  [the longest x1 0.93 us: step(): both = join(core, wide, lax.ppermute(wide, 'row', PAIR))]
  transfers between devices with their start and end apart: 10 -> 9, of which waited for: 8 -> 6; matrix products, arithmetic and copies ran while one was open for 0% -> 10% of each run, Pallas kernels for 0% -> 0%
where the time goes in v3:
time: 109 us; the launch traced here: 108 us
  waiting for transfers between devices  45.2 us (41%)
  starting transfers between devices  41.6 us (38%)
  matrix products  14.2 us (13%)
  local copies, waits for them, and re-layouts  4.36 us (4%)
  other arithmetic  2.06 us (2%)
    ppermute x2, waiting for transfers between devices, double(): return jnp.concatenate([x, lax.ppermute(x, 'col', pairs)], 0)  22.7 us
    all_to_all x2, waiting for transfers between devices, spread(): lax.all_to_all(jnp.broadcast_to(x[None], (n,) + x.shape), axis, 0, 0, til...  15.5 us
    dot_general x38, matrix products, mm(): lax.dot_general(a, b, (((ca,), (cb,)), ((), ())), precision=lax.Precision...  14.2 us
    ppermute x1, starting transfers between devices, step(): part = halves(True) + lax.ppermute(halves(False), 'row', PAIR)  8.75 us
    all_to_all x1, starting transfers between devices, step(): lax.all_to_all(part, 'row', 0, 0, tiled=True, axis_index_groups=Z_GROUPS)  8.15 us
    ppermute x2, starting transfers between devices, double(): return jnp.concatenate([x, lax.ppermute(x, 'col', pairs)], 0)  7.75 us
    all_to_all x2, starting transfers between devices, spread(): lax.all_to_all(jnp.broadcast_to(x[None], (n,) + x.shape), axis, 0, 0, til...  6.83 us
    all_to_all x1, waiting for transfers between devices, step(): lax.all_to_all(part, 'row', 0, 0, tiled=True, axis_index_groups=Z_GROUPS)  6.05 us
  transfers between devices with their start and end apart: 9, of which 6 were waited for; matrix products, arithmetic and copies ran while one was open for 10% of the time, Pallas kernels for 0%

profile of v3, /device:TPU:1, one launch (start us, length us, event | category | flops | bytes accessed | tf_op | source)
XLA Modules:
  0.0 108.0 jit_solution(2092447800384282516)
XLA Ops:
  0.0 0.8 fusion.32
  1.1 1.7 %fusion = f32[1024,128]{1,0:T(8,128)S(1)} fusion(f32[512,128]{1,0:T(8,128)} %param.3, s32[1024]{0:T(1024)S(1)} %add_subtract_fusion), kind=kOutput, calls=%fused_computation.3 | convolution fusion | flops 403177472 | bytes 790528 | tf_op jit(solution)/shard_map/dot_general | solution.py:16
  2.8 0.3 convolution_bitcast_fusion
  3.3 8.7 %collective-permute-start = (f32[544,128]{1,0:T(8,128)S(1)}, f32[544,128]{1,0:T(8,128)S(1)}, u32[]{:S(2)}, u32[]{:S(2)}) collective-permute-start(f32[544,128]{1,0:T(8,128)S(1)} %pad_maximum_fusion.3), channel_id=1, source_target_pairs={{0,32},{32,0},{64,96},{96,64},{128,160},{160,128},{192,224},{224,1... | collective-permute-start | bytes 835592 | tf_op jit(solution)/shard_map/ppermute | solution.py:84
  12.0 0.7 broadcast_in_dim.80
  12.7 3.4 %all-to-all-start = ((f32[8,64,128]{2,1,0:T(8,128)}), f32[8,64,128]{2,1,0:T(8,128)S(1)}, u32[]{:S(2)}, u32[]{:S(2)}) async-start(f32[8,64,128]{2,1,0:T(8,128)} %broadcast_in_dim.80), calls=%async_computation | async-start | bytes 524288 | tf_op jit(solution)/shard_map/all_to_all | solution.py:24
  16.3 0.8 pad_maximum_fusion.2
  17.0 11.4 %all-to-all-done = f32[8,64,128]{2,1,0:T(8,128)S(1)} async-done(((f32[8,64,128]{2,1,0:T(8,128)}), f32[8,64,128]{2,1,0:T(8,128)S(1)}, u32[]{:S(2)}, u32[]{:S(2)}) %all-to-all-start) | async-done | bytes 262176 | tf_op jit(solution)/shard_map/all_to_all | solution.py:24
  28.5 8.2 %all-to-all-start.1 = ((f32[8,96,128]{2,1,0:T(8,128)}), f32[8,96,128]{2,1,0:T(8,128)S(1)}, u32[]{:S(2)}, u32[]{:S(2)}) async-start(f32[8,96,128]{2,1,0:T(8,128)} %pad_maximum_fusion.2), calls=%async_computation.1 | async-start | bytes 786432 | tf_op jit(solution)/shard_map/all_to_all | solution.py:90
  36.6 3.1 %collective-permute-start.1 = (f32[8,64,128]{2,1,0:T(8,128)S(1)}, f32[8,64,128]{2,1,0:T(8,128)S(1)}, u32[]{:S(2)}, u32[]{:S(2)}) collective-permute-start(f32[8,64,128]{2,1,0:T(8,128)S(1)} %all-to-all-done), channel_id=1, source_target_pairs={{0,1},{1,0},{2,3},{3,2},{4,5},{5,4},{6,7},{7,6},{8,9},{9,8},{10,11... | collective-permute-start | bytes 786440 | tf_op jit(solution)/shard_map/ppermute | solution.py:31
  39.7 5.9 %collective-permute-done.1 = f32[8,64,128]{2,1,0:T(8,128)S(1)} collective-permute-done((f32[8,64,128]{2,1,0:T(8,128)S(1)}, f32[8,64,128]{2,1,0:T(8,128)S(1)}, u32[]{:S(2)}, u32[]{:S(2)}) %collective-permute-start.1) | collective-permute-done | bytes 262176 | tf_op jit(solution)/shard_map/ppermute | solution.py:31
  45.7 6.0 %all-to-all-done.1 = f32[8,96,128]{2,1,0:T(8,128)S(1)} async-done(((f32[8,96,128]{2,1,0:T(8,128)}), f32[8,96,128]{2,1,0:T(8,128)S(1)}, u32[]{:S(2)}, u32[]{:S(2)}) %all-to-all-start.1) | async-done | bytes 393248 | tf_op jit(solution)/shard_map/all_to_all | solution.py:90
  51.8 0.9 broadcast_in_dim.81
  52.6 4.4 %all-to-all-start.2 = ((f32[32,32,128]{2,1,0:T(8,128)}), f32[32,32,128]{2,1,0:T(8,128)S(1)}, u32[]{:S(2)}, u32[]{:S(2)}) async-start(f32[32,32,128]{2,1,0:T(8,128)} %broadcast_in_dim.81), calls=%async_computation.2 | async-start | bytes 1048576 | tf_op jit(solution)/shard_map/all_to_all | solution.py:95
  57.1 4.6 %collective-permute-start.2 = (f32[16,64,128]{2,1,0:T(8,128)S(1)}, f32[16,64,128]{2,1,0:T(8,128)S(1)}, u32[]{:S(2)}, u32[]{:S(2)}) collective-permute-start(f32[16,64,128]{2,1,0:T(8,128)S(1)} %pad_maximum_fusion.1), channel_id=1, source_target_pairs={{0,2},{1,3},{2,0},{3,1},{4,6},{5,7},{6,4},{7,5},{8,10},{9,11},{10,... | collective-permute-start | bytes 1572872 | tf_op jit(solution)/shard_map/ppermute | solution.py:31
  62.0 16.8 %collective-permute-done.2 = f32[16,64,128]{2,1,0:T(8,128)S(1)} collective-permute-done((f32[16,64,128]{2,1,0:T(8,128)S(1)}, f32[16,64,128]{2,1,0:T(8,128)S(1)}, u32[]{:S(2)}, u32[]{:S(2)}) %collective-permute-start.2) | collective-permute-done | bytes 524320 | tf_op jit(solution)/shard_map/ppermute | solution.py:31
  78.9 3.2 %collective-permute-start.3 = (f32[32,32,128]{2,1,0:T(8,128)S(1)}, f32[32,32,128]{2,1,0:T(8,128)S(1)}, u32[]{:S(2)}, u32[]{:S(2)}) collective-permute-start(f32[32,32,128]{2,1,0:T(8,128)S(1)} %all-to-all-done.2), channel_id=1, source_target_pairs={{0,32},{32,0},{64,96},{96,64},{128,160},{160,128},{192,224},{224,1... | collective-permute-start | bytes 1572872 | tf_op jit(solution)/shard_map/ppermute | solution.py:100
  82.2 0.7 broadcast_in_dim.82
  83.0 3.4 %all-to-all-start.3 = ((f32[8,64,128]{2,1,0:T(8,128)}), f32[8,64,128]{2,1,0:T(8,128)S(1)}, u32[]{:S(2)}, u32[]{:S(2)}) async-start(f32[8,64,128]{2,1,0:T(8,128)} %broadcast_in_dim.82), calls=%async_computation.3 | async-start | bytes 524288 | tf_op jit(solution)/shard_map/all_to_all | solution.py:24
  86.7 0.3 fusion.7
  87.0 0.3 fusion.39
  87.3 0.3 convolution_add_fusion.6
  87.6 0.3 fusion.40
  88.1 0.3 fusion.41
  88.7 0.3 fusion.42
  89.2 0.3 fusion.43
  89.8 0.3 fusion.44
  90.4 0.3 fusion.9
  90.7 0.3 fusion.33
  90.9 0.3 convolution_add_fusion.13
  91.2 0.3 fusion.34
  91.8 0.3 fusion.35
  92.4 0.3 fusion.36
  92.9 0.3 fusion.37
  93.5 0.3 fusion.38
  94.6 4.1 %all-to-all-done.3 = f32[8,64,128]{2,1,0:T(8,128)S(1)} async-done(((f32[8,64,128]{2,1,0:T(8,128)}), f32[8,64,128]{2,1,0:T(8,128)S(1)}, u32[]{:S(2)}, u32[]{:S(2)}) %all-to-all-start.3) | async-done | bytes 262176 | tf_op jit(solution)/shard_map/all_to_all | solution.py:24
  98.7 2.5 %collective-permute-start.4 = (f32[8,64,128]{2,1,0:T(8,128)S(1)}, f32[8,64,128]{2,1,0:T(8,128)S(1)}, u32[]{:S(2)}, u32[]{:S(2)}) collective-permute-start(f32[8,64,128]{2,1,0:T(8,128)S(1)} %all-to-all-done.3), channel_id=1, source_target_pairs={{0,32},{32,0},{64,96},{96,64},{128,160},{160,128},{192,224},{224,1... | collective-permute-start | bytes 786440 | tf_op jit(solution)/shard_map/ppermute | solution.py:107
  101.2 0.9 collective-permute-done.4
  102.3 0.4 fusion.45
  102.7 0.4 bitcast_subtract_fusion.1
  103.1 0.4 fusion.46
  103.4 0.6 gather_fusion.1
  104.0 0.6 gather_fusion
  104.6 0.4 bitcast_subtract_fusion
  105.0 0.5 convolution_select_fusion
  105.6 0.6 convolution_subtract_fusion.1
  106.2 0.5 convolution_select_fusion.1
  106.7 1.3 %fusion.1 = f32[512,128]{1,0:T(8,128)} fusion(f32[512,128]{1,0:T(8,128)S(1)} %convolution_select_fusion.1, f32[2,32,8,4,128]{4,2,3,0,1:T(8,128)S(1)} %bitcast.164, f32[256,128]{1,0:T(8,128)S(1)} %fusion.46, f32[256,128]{1,0:T(8,128)S(1)} %fusion.45, f32[32,8,128]{2,1,0:T(8,128)S(1)} %gather_fusion.1, pred[]{:T(512)S(6)} %eq.43), kind=kOutput, calls=%fused_computation.22 | convolution fusion | flops 100859904 | bytes 1441793 | tf_op jit(solution)/shard_map/dot_general | solution.py:16
  (56 shorter events, 4.7 us)
Async XLA Ops:
  0.0 2.8 %copy-start.1 = (f32[2,512,8]{1,2,0:T(8,128)S(1)}, f32[2,512,8]{1,2,0:T(8,128)}, u32[]{:S(2)}) copy-start(f32[2,512,8]{1,2,0:T(8,128)} %param.4) | copy-start | bytes 98308
  3.3 12.9 %collective-permute-start = (f32[544,128]{1,0:T(8,128)S(1)}, f32[544,128]{1,0:T(8,128)S(1)}, u32[]{:S(2)}, u32[]{:S(2)}) collective-permute-start(f32[544,128]{1,0:T(8,128)S(1)} %pad_maximum_fusion.3), channel_id=1, source_target_pairs={{0,32},{32,0},{64,96},{96,64},{128,160},{160,128},{192,224},{224,1... | collective-permute-start | bytes 835592 | tf_op jit(solution)/shard_map/ppermute | solution.py:84
  12.7 15.7 %all-to-all-start = ((f32[8,64,128]{2,1,0:T(8,128)}), f32[8,64,128]{2,1,0:T(8,128)S(1)}, u32[]{:S(2)}, u32[]{:S(2)}) async-start(f32[8,64,128]{2,1,0:T(8,128)} %broadcast_in_dim.80), calls=%async_computation | async-start | bytes 524288 | tf_op jit(solution)/shard_map/all_to_all | solution.py:24
  28.5 23.3 %all-to-all-start.1 = ((f32[8,96,128]{2,1,0:T(8,128)}), f32[8,96,128]{2,1,0:T(8,128)S(1)}, u32[]{:S(2)}, u32[]{:S(2)}) async-start(f32[8,96,128]{2,1,0:T(8,128)} %pad_maximum_fusion.2), calls=%async_computation.1 | async-start | bytes 786432 | tf_op jit(solution)/shard_map/all_to_all | solution.py:90
  36.6 9.0 %collective-permute-start.1 = (f32[8,64,128]{2,1,0:T(8,128)S(1)}, f32[8,64,128]{2,1,0:T(8,128)S(1)}, u32[]{:S(2)}, u32[]{:S(2)}) collective-permute-start(f32[8,64,128]{2,1,0:T(8,128)S(1)} %all-to-all-done), channel_id=1, source_target_pairs={{0,1},{1,0},{2,3},{3,2},{4,5},{5,4},{6,7},{7,6},{8,9},{9,8},{10,11... | collective-permute-start | bytes 786440 | tf_op jit(solution)/shard_map/ppermute | solution.py:31
  52.6 26.3 %all-to-all-start.2 = ((f32[32,32,128]{2,1,0:T(8,128)}), f32[32,32,128]{2,1,0:T(8,128)S(1)}, u32[]{:S(2)}, u32[]{:S(2)}) async-start(f32[32,32,128]{2,1,0:T(8,128)} %broadcast_in_dim.81), calls=%async_computation.2 | async-start | bytes 1048576 | tf_op jit(solution)/shard_map/all_to_all | solution.py:95
  57.1 21.7 %collective-permute-start.2 = (f32[16,64,128]{2,1,0:T(8,128)S(1)}, f32[16,64,128]{2,1,0:T(8,128)S(1)}, u32[]{:S(2)}, u32[]{:S(2)}) collective-permute-start(f32[16,64,128]{2,1,0:T(8,128)S(1)} %pad_maximum_fusion.1), channel_id=1, source_target_pairs={{0,2},{1,3},{2,0},{3,1},{4,6},{5,7},{6,4},{7,5},{8,10},{9,11},{10,... | collective-permute-start | bytes 1572872 | tf_op jit(solution)/shard_map/ppermute | solution.py:31
  78.9 7.5 %collective-permute-start.3 = (f32[32,32,128]{2,1,0:T(8,128)S(1)}, f32[32,32,128]{2,1,0:T(8,128)S(1)}, u32[]{:S(2)}, u32[]{:S(2)}) collective-permute-start(f32[32,32,128]{2,1,0:T(8,128)S(1)} %all-to-all-done.2), channel_id=1, source_target_pairs={{0,32},{32,0},{64,96},{96,64},{128,160},{160,128},{192,224},{224,1... | collective-permute-start | bytes 1572872 | tf_op jit(solution)/shard_map/ppermute | solution.py:100
  83.0 15.7 %all-to-all-start.3 = ((f32[8,64,128]{2,1,0:T(8,128)}), f32[8,64,128]{2,1,0:T(8,128)S(1)}, u32[]{:S(2)}, u32[]{:S(2)}) async-start(f32[8,64,128]{2,1,0:T(8,128)} %broadcast_in_dim.82), calls=%async_computation.3 | async-start | bytes 524288 | tf_op jit(solution)/shard_map/all_to_all | solution.py:24
  98.7 3.5 %collective-permute-start.4 = (f32[8,64,128]{2,1,0:T(8,128)S(1)}, f32[8,64,128]{2,1,0:T(8,128)S(1)}, u32[]{:S(2)}, u32[]{:S(2)}) collective-permute-start(f32[8,64,128]{2,1,0:T(8,128)S(1)} %all-to-all-done.3), channel_id=1, source_target_pairs={{0,32},{32,0},{64,96},{96,64},{128,160},{160,128},{192,224},{224,1... | collective-permute-start | bytes 786440 | tf_op jit(solution)/shard_map/ppermute | solution.py:107
  102.7 2.4 %copy-start = (f32[512,128]{1,0:T(8,128)S(1)}, f32[512,128]{1,0:T(8,128)}, u32[]{:S(2)}) copy-start(f32[512,128]{1,0:T(8,128)} %param.3) | copy-start | bytes 786436

commit v4 on v3

v4 whole, which is shorter than its diff:
```python
import jax
import jax.numpy as jnp
from jax import lax
from jax.experimental import pallas as pl
from jax.experimental.pallas import tpu as pltpu
from jax.sharding import PartitionSpec as P


PW = 256
LIMIT = 16 << 20
NZ, NC = 8, 2
NY, NX = 8, 4
Z_GROUPS = [[NC * z + core for z in range(NZ)] for core in range(NC)]
Y_GROUPS = [[NX * y + x for y in range(NY)] for x in range(NX)]
PAIR = [(i, i ^ 1) for i in range(NZ * NC)]


def mm(a, b, ca=1, cb=0):
    return lax.dot_general(
        a, b, (((ca,), (cb,)), ((), ())),
        precision=lax.Precision.HIGH, preferred_element_type=jnp.float32,
    )


def spread(x, axis, groups):
    n = len(groups[0])
    return lax.all_to_all(
        jnp.broadcast_to(x[None], (n,) + x.shape), axis, 0, 0, tiled=True, axis_index_groups=groups
    )


def flip(x, bits):
    return lax.ppermute(x, "col", [(i, i ^ bits) for i in range(NX * NY)])


def split(x):
    high = x.astype(jnp.bfloat16)
    return high, (x - high.astype(jnp.float32)).astype(jnp.bfloat16)


def dot(a, b):
    return jnp.dot(a, b, preferred_element_type=jnp.float32)


def dot3(a, b):
    return dot(a[0], b[0]) + dot(a[0], b[1]) + dot(a[1], b[0])


def halves_of(core, own, far):
    return jnp.where(core == 0, own, far), jnp.where(core == 0, far, own)


def squares_kernel(core_ref, own_ref, far_ref, high_ref, low_ref):
    core = core_ref[0]
    squares = []
    for p in range(4):
        own = own_ref[:, 8 * p : 8 * p + 8, :].reshape(PW, 128)
        far = far_ref[:, 8 * p : 8 * p + 8, :].reshape(PW, 128)
        squares.append(jnp.concatenate(halves_of(core, own, far), 1).T)
    row = lax.broadcasted_iota(jnp.int32, (PW, PW), 0)
    col = lax.broadcasted_iota(jnp.int32, (PW, PW), 1)
    eye = (row == col).astype(jnp.float32)
    power = [split(jnp.where(row > col, x, 0.0)) for x in squares[:2]]
    inverse = [eye - jnp.where(row > col, x, 0.0) for x in squares[:2]]
    for _ in range(1, PW.bit_length() - 1):
        power = [split(dot3(x, x)) for x in power]
        inverse = [x + dot3(split(x), y) for x, y in zip(inverse, power)]
    for p, x in enumerate(inverse + squares[2:]):
        high, low = split(x)
        high_ref[p] = high
        low_ref[p] = low


def squares_of(core, own, far):
    vmem = pl.BlockSpec(memory_space=pltpu.VMEM)
    pair = jax.ShapeDtypeStruct((4, PW, PW), jnp.bfloat16)
    return pl.pallas_call(
        squares_kernel,
        out_shape=(pair, pair),
        in_specs=[pl.BlockSpec(memory_space=pltpu.SMEM), vmem, vmem],
        out_specs=(vmem, vmem),
        cost_estimate=pl.CostEstimate(flops=6 * 28 * PW**3, bytes_accessed=2 << 20, transcendentals=0),
        compiler_params=pltpu.CompilerParams(vmem_limit_bytes=LIMIT),
        name="squares",
    )(core, own, far)


def lower_kernel(col_ref, near0_ref, near1_ref, near2_ref, near3_ref, high_ref, low_ref, turned_ref):
    x_at = col_ref[0] % NX
    for bits, ref in enumerate((near0_ref, near1_ref, near2_ref, near3_ref)):
        x = x_at ^ bits
        for y in range(NY):
            at = pl.multiple_of((NX * y + x) * 8, 8)
            for p in range(2):
                for h in range(4):
                    tile = ref[y, 32 * p + 8 * h : 32 * p + 8 * h + 8, :]
                    turned_ref[p, pl.ds(at, 8), 128 * h : 128 * h + 128] = tile

    for p in range(2):
        high, low = split(turned_ref[p].T)
        high_ref[p] = high
        low_ref[p] = low


def lower_of(col, *near):
    vmem = pl.BlockSpec(memory_space=pltpu.VMEM)
    pair = jax.ShapeDtypeStruct((2, 512, PW), jnp.bfloat16)
    return pl.pallas_call(
        lower_kernel,
        out_shape=(pair, pair),
        in_specs=[pl.BlockSpec(memory_space=pltpu.SMEM)] + [vmem] * 4,
        out_specs=(vmem, vmem),
        scratch_shapes=[pltpu.VMEM((2, PW, 512), jnp.float32)],
        cost_estimate=pl.CostEstimate(flops=1 << 20, bytes_accessed=2 << 20, transcendentals=0),
        compiler_params=pltpu.CompilerParams(vmem_limit_bytes=LIMIT),
        name="lower",
    )(col, *near)


def update_kernel(me_ref, piv_ref, wide_ref, sq_high_ref, sq_low_ref, lo_high_ref, lo_low_ref, block_ref, out_ref):
    me = me_ref[0]
    start = me * 512

    def rows(at):
        return wide_ref[:, at : at + 32, :].reshape(PW, 128)

    square = [(sq_high_ref[p], sq_low_ref[p]) for p in range(4)]
    upper0 = dot3(square[0], split(rows(0)))
    pair0 = split(upper0)
    upper1 = dot3(square[1], split(rows(64) - dot3(square[3], pair0)))

    @pl.when(me == 0)
    def _():
        out_ref[:PW] = upper0
        out_ref[PW:] = upper1

    @pl.when(me != 0)
    def _():
        second = rows(96) - dot3(square[2], pair0)
        at = lax.broadcasted_iota(jnp.int32, (512, PW), 0) + start

        def place(p, x, work):
            select = (at == piv_ref[p : p + 1, :]).astype(jnp.bfloat16)
            high = x.astype(jnp.bfloat16)
            rest = x - high.astype(jnp.float32)
            mid = rest.astype(jnp.bfloat16)
            low = (rest - mid.astype(jnp.float32)).astype(jnp.bfloat16)
            one = dot(select, jnp.concatenate([high, jnp.ones((PW, 128), jnp.bfloat16)], 1))
            two = dot(select, jnp.concatenate([mid, low], 1))
            moved = one[:, :128] + two[:, :128] + two[:, 128:]
            return jnp.where(one[:, 128:] > 0, moved, work)

        work = place(0, rows(32), block_ref[...])
        work = work - dot3((lo_high_ref[0], lo_low_ref[0]), pair0)
        work = place(1, second, work)
        out_ref[...] = work - dot3((lo_high_ref[1], lo_low_ref[1]), split(upper1))


def update_of(me, pivots, wide, squares, lower, block):
    vmem = pl.BlockSpec(memory_space=pltpu.VMEM)
    return pl.pallas_call(
        update_kernel,
        out_shape=jax.ShapeDtypeStruct((512, 128), jnp.float32),
        in_specs=[pl.BlockSpec(memory_space=pltpu.SMEM)] + [vmem] * 7,
        out_specs=vmem,
        cost_estimate=pl.CostEstimate(flops=1 << 29, bytes_accessed=3 << 20, transcendentals=0),
        compiler_params=pltpu.CompilerParams(vmem_limit_bytes=LIMIT),
        name="update",
    )(me, pivots, wide, *squares, *lower, block)


def step(block, panels, pivots):
    me = lax.axis_index("row")
    core = me % NC
    start = me * 512
    first = me == 0
    p0, p1 = pivots[0], pivots[1]
    j = jnp.arange(PW, dtype=jnp.int32)
    lane = jnp.arange(512, dtype=jnp.int32)

    def through0(rows):
        hit = p0[None, :] == rows[:, None]
        found = jnp.max(jnp.where(hit, j[None, :], -1), axis=1)
        return jnp.where(found >= 0, found, rows)

    source = jnp.concatenate([p0, through0(p1), j, through0(PW + j)])
    pick = (source[:, None] - start == lane[None, :]).astype(jnp.float32)
    rows = mm(pick, block).reshape(2, NC, NZ, 32, 128)
    rows = rows.transpose(1, 2, 0, 3, 4).reshape(NC, NZ, 64, 128)

    pan_t = panels.transpose(0, 2, 1)
    near = pan_t.reshape(2, 8, 4, 128).transpose(0, 2, 1, 3).reshape(64, 128)
    near = spread(near, "col", Y_GROUPS)

    at1 = (p1[:, None] - start == lane[None, :]).astype(jnp.float32)
    piv_t = mm(pan_t[0], at1, 1, 1)
    zero = jnp.zeros((8, PW), jnp.float32)
    own = lambda t: jnp.where(first, t, zero)
    pieces = jnp.stack([own(pan_t[0, :, :PW]), own(pan_t[1, :, PW:]), own(pan_t[0, :, PW:]), piv_t])
    tiles = pieces.reshape(4, 8, 2, 128).transpose(2, 0, 1, 3).reshape(2, 32, 128)

    def side(pair, mine):
        return jnp.where((core == 0) == mine, pair[0], pair[1])

    def halves(mine):
        return jnp.concatenate([side(rows, mine).reshape(512, 128), side(tiles, mine)], 0)

    part = halves(True) + lax.ppermute(halves(False), "row", PAIR)
    part = jnp.concatenate(
        [part[:512].reshape(NZ, 64, 128), jnp.broadcast_to(part[None, 512:], (NZ, 32, 128))], 1
    )
    part, near = lax.optimization_barrier((part, near))

    part = lax.all_to_all(part, "row", 0, 0, tiled=True, axis_index_groups=Z_GROUPS)
    near1 = flip(near, 1)
    part, near, near1 = lax.optimization_barrier((part, near, near1))

    part = jnp.sum(part, 0)
    tile = jnp.broadcast_to(part[64:], (NX * NY, 32, 128))
    tile = lax.all_to_all(tile, "col", 0, 0, tiled=True)
    near2 = flip(near, 2)
    far = lax.ppermute(part[:64], "row", PAIR)
    both = jnp.where(core == 0, jnp.concatenate([part[:64], far]), jnp.concatenate([far, part[:64]]))
    tile, both, near2 = lax.optimization_barrier((tile, both, near2))

    wide = spread(both, "row", Z_GROUPS)
    far = lax.ppermute(tile, "row", PAIR)
    near3 = flip(near, 3)
    squares = squares_of(core.reshape(1), tile, far)
    lower = lower_of(lax.axis_index("col").reshape(1), near, near1, near2, near3)
    wide, squares, lower = lax.optimization_barrier((wide, squares, lower))
    return update_of(me.reshape(1), pivots, wide, squares, lower, block)


def solution(mesh):
    return jax.shard_map(
        step,
        mesh=mesh,
        in_specs=(P("row", "col"), P(None, "row", "col"), P()),
        out_specs=P("row", "col"),
        check_vma=False,
    )
```

time: 109 us -> 103 us (0.945)
  matrix products: 14.2 us -> 2 us
  Pallas kernels: 0 us -> 8.3 us
  waiting for transfers between devices: 45.2 us -> 39.2 us
  starting transfers between devices: 41.6 us -> 47.1 us
    dot_general x38 -> x2, matrix products: 14.2 us -> 2 us  [mm(): lax.dot_general(a, b, (((ca,), (cb,)), ((), ())), precision=lax.Precision...]
    pallas_call x0 -> x3, Pallas kernels: none -> 8.3 us  [the longest x1 5.29 us: squares_of(): pl.pallas_call(squares_kernel, out_shape=(pair, pair), in_specs=[pl.Block...]
    ppermute x3 -> x4, starting transfers between devices: 10.3 us -> 14.7 us  [the longest x3 11.4 us: flip(): return lax.ppermute(x, 'col', [(i, i ^ bits) for i in range(NX * NY)])]
    all_to_all x2, waiting for transfers between devices: 15.5 us -> 11.4 us  [spread(): lax.all_to_all(jnp.broadcast_to(x[None], (n,) + x.shape), axis, 0, 0, til...]
    ppermute x3 -> x4, waiting for transfers between devices: 23.6 us -> 20.4 us  [the longest x3 19.6 us: flip(): return lax.ppermute(x, 'col', [(i, i ^ bits) for i in range(NX * NY)])]
    all_to_all x1, waiting for transfers between devices: 0.01 us -> 1.21 us  [step(): tile = lax.all_to_all(tile, 'col', 0, 0, tiled=True)]
    gather x2 -> x0, local copies, waits for them, and re-layouts: 1.17 us -> none  [the longest x1 0.59 us: step(): upper1.reshape(32, 8, 128)[seen].reshape(PW, 128)]
  transfers between devices with their start and end apart: 9 -> 10, of which waited for: 6 -> 7; matrix products, arithmetic and copies ran while one was open for 10% -> 2% of each run, Pallas kernels for 0% -> 6%
where the time goes in v4:
time: 103 us; the launch traced here: 102 us
  starting transfers between devices  47.1 us (46%)
  waiting for transfers between devices  39.2 us (38%)
  Pallas kernels  8.3 us (8%)
  local copies, waits for them, and re-layouts  3.96 us (4%)
  matrix products  2 us (2%)
  other arithmetic  1.24 us (1%)
    ppermute x3, waiting for transfers between devices, flip(): return lax.ppermute(x, 'col', [(i, i ^ bits) for i in range(NX * NY)])  19.6 us
    ppermute x3, starting transfers between devices, flip(): return lax.ppermute(x, 'col', [(i, i ^ bits) for i in range(NX * NY)])  11.4 us
    all_to_all x2, waiting for transfers between devices, spread(): lax.all_to_all(jnp.broadcast_to(x[None], (n,) + x.shape), axis, 0, 0, til...  11.4 us
    ppermute x1, starting transfers between devices, step(): part = halves(True) + lax.ppermute(halves(False), 'row', PAIR)  8.75 us
    all_to_all x1, starting transfers between devices, step(): lax.all_to_all(part, 'row', 0, 0, tiled=True, axis_index_groups=Z_GROUPS)  8.15 us
    all_to_all x2, starting transfers between devices, spread(): lax.all_to_all(jnp.broadcast_to(x[None], (n,) + x.shape), axis, 0, 0, til...  6.9 us
    all_to_all x1, waiting for transfers between devices, step(): lax.all_to_all(part, 'row', 0, 0, tiled=True, axis_index_groups=Z_GROUPS)  6.1 us
    pallas_call x1, Pallas kernels, squares_of(): pl.pallas_call(squares_kernel, out_shape=(pair, pair), in_specs=[pl.Block...  5.29 us
  transfers between devices with their start and end apart: 10, of which 7 were waited for; matrix products, arithmetic and copies ran while one was open for 2% of the time, Pallas kernels for 6%

profile of v4, /device:TPU:1, one launch (start us, length us, event | category | flops | bytes accessed | tf_op | source)
XLA Modules:
  0.0 102.0 jit_solution(6614753028036498245)
XLA Ops:
  0.0 0.8 fusion.6
  0.8 0.2 select_reduce_fusion.1
  1.1 1.7 %fusion = f32[1024,128]{1,0:T(8,128)S(1)} fusion(f32[512,128]{1,0:T(8,128)} %block_ref.1, s32[1024]{0:T(1024)S(1)} %add_subtract_fusion), kind=kOutput, calls=%fused_computation.1 | convolution fusion | flops 403177472 | bytes 790528 | tf_op jit(solution)/shard_map/dot_general | solution.py:19
  2.8 0.0 copy-start.2
  2.8 0.7 copy-done.2
  3.5 0.3 convolution_bitcast_fusion
  3.8 0.1 slice_select_fusion.1
  4.0 8.7 %collective-permute-start = (f32[544,128]{1,0:T(8,128)S(1)}, f32[544,128]{1,0:T(8,128)S(1)}, u32[]{:S(2)}, u32[]{:S(2)}) collective-permute-start(f32[544,128]{1,0:T(8,128)S(1)} %pad_maximum_fusion.1), channel_id=1, source_target_pairs={{0,32},{32,0},{64,96},{96,64},{128,160},{160,128},{192,224},{224,1... | collective-permute-start | bytes 835592 | tf_op jit(solution)/shard_map/ppermute | solution.py:208
  12.7 0.7 broadcast_in_dim.55
  13.5 3.4 %all-to-all-start = ((f32[8,64,128]{2,1,0:T(8,128)}), f32[8,64,128]{2,1,0:T(8,128)S(1)}, u32[]{:S(2)}, u32[]{:S(2)}) async-start(f32[8,64,128]{2,1,0:T(8,128)} %broadcast_in_dim.55), calls=%async_computation | async-start | bytes 524288 | tf_op jit(solution)/shard_map/all_to_all | solution.py:27
  16.9 0.0 collective-permute-done
  17.0 0.8 pad_maximum_fusion
  17.8 11.4 %all-to-all-done.near0_ref = f32[8,64,128]{2,1,0:T(8,128)S(1)} async-done(((f32[8,64,128]{2,1,0:T(8,128)}), f32[8,64,128]{2,1,0:T(8,128)S(1)}, u32[]{:S(2)}, u32[]{:S(2)}) %all-to-all-start) | async-done | bytes 262176 | tf_op jit(solution)/shard_map/all_to_all | solution.py:27
  29.2 8.2 %all-to-all-start.1 = ((f32[8,96,128]{2,1,0:T(8,128)}), f32[8,96,128]{2,1,0:T(8,128)S(1)}, u32[]{:S(2)}, u32[]{:S(2)}) async-start(f32[8,96,128]{2,1,0:T(8,128)} %pad_maximum_fusion), calls=%async_computation.1 | async-start | bytes 786432 | tf_op jit(solution)/shard_map/all_to_all | solution.py:214
  37.3 3.1 %collective-permute-start.1 = (f32[8,64,128]{2,1,0:T(8,128)S(1)}, f32[8,64,128]{2,1,0:T(8,128)S(1)}, u32[]{:S(2)}, u32[]{:S(2)}) collective-permute-start(f32[8,64,128]{2,1,0:T(8,128)S(1)} %all-to-all-done.near0_ref), channel_id=1, source_target_pairs={{0,1},{1,0},{2,3},{3,2},{4,5},{5,4},{6,7},{7,6},{8,9},{9,8},{10,11... | collective-permute-start | bytes 786440 | tf_op jit(solution)/shard_map/ppermute | solution.py:33
  40.4 5.9 %collective-permute-done.1.near1_ref = f32[8,64,128]{2,1,0:T(8,128)S(1)} collective-permute-done((f32[8,64,128]{2,1,0:T(8,128)S(1)}, f32[8,64,128]{2,1,0:T(8,128)S(1)}, u32[]{:S(2)}, u32[]{:S(2)}) %collective-permute-start.1) | collective-permute-done | bytes 262176 | tf_op jit(solution)/shard_map/ppermute | solution.py:33
  46.3 6.1 %all-to-all-done.1 = f32[8,96,128]{2,1,0:T(8,128)S(1)} async-done(((f32[8,96,128]{2,1,0:T(8,128)}), f32[8,96,128]{2,1,0:T(8,128)S(1)}, u32[]{:S(2)}, u32[]{:S(2)}) %all-to-all-start.1) | async-done | bytes 393248 | tf_op jit(solution)/shard_map/all_to_all | solution.py:214
  52.5 0.9 broadcast_in_dim.56
  53.3 4.4 %all-to-all-start.2 = ((f32[32,32,128]{2,1,0:T(8,128)}), f32[32,32,128]{2,1,0:T(8,128)S(1)}, u32[]{:S(2)}, u32[]{:S(2)}) async-start(f32[32,32,128]{2,1,0:T(8,128)} %broadcast_in_dim.56), calls=%async_computation.2 | async-start | bytes 1048576 | tf_op jit(solution)/shard_map/all_to_all | solution.py:220
  57.7 4.6 %collective-permute-start.3 = (f32[8,64,128]{2,1,0:T(8,128)S(1)}, f32[8,64,128]{2,1,0:T(8,128)S(1)}, u32[]{:S(2)}, u32[]{:S(2)}) collective-permute-start(f32[8,64,128]{2,1,0:T(8,128)S(1)} %all-to-all-done.near0_ref), channel_id=1, source_target_pairs={{0,2},{1,3},{2,0},{3,1},{4,6},{5,7},{6,4},{7,5},{8,10},{9,11},{10,... | collective-permute-start | bytes 786440 | tf_op jit(solution)/shard_map/ppermute | solution.py:33
  62.4 3.3 %collective-permute-start.2 = (f32[64,128]{1,0:T(8,128)S(1)}, f32[64,128]{1,0:T(8,128)S(1)}, u32[]{:S(2)}, u32[]{:S(2)}) collective-permute-start(f32[64,128]{1,0:T(8,128)S(1)} %slice.77), channel_id=1, source_target_pairs={{0,32},{32,0},{64,96},{96,64},{128,160},{160,128},{192,224},{224,1... | collective-permute-start | bytes 98312 | tf_op jit(solution)/shard_map/ppermute | solution.py:222
  65.7 0.8 collective-permute-done.2
  66.6 6.5 %collective-permute-done.3.near2_ref = f32[8,64,128]{2,1,0:T(8,128)S(1)} collective-permute-done((f32[8,64,128]{2,1,0:T(8,128)S(1)}, f32[8,64,128]{2,1,0:T(8,128)S(1)}, u32[]{:S(2)}, u32[]{:S(2)}) %collective-permute-start.3) | collective-permute-done | bytes 262176 | tf_op jit(solution)/shard_map/ppermute | solution.py:33
  73.0 1.2 %all-to-all-done.2.own_ref = f32[32,32,128]{2,1,0:T(8,128)S(1)} async-done(((f32[32,32,128]{2,1,0:T(8,128)}), f32[32,32,128]{2,1,0:T(8,128)S(1)}, u32[]{:S(2)}, u32[]{:S(2)}) %all-to-all-start.2) | async-done | bytes 524320 | tf_op jit(solution)/shard_map/all_to_all | solution.py:220
  74.2 0.8 broadcast_in_dim.57
  75.1 3.5 %all-to-all-start.3 = ((f32[8,128,128]{2,1,0:T(8,128)}), f32[8,128,128]{2,1,0:T(8,128)S(1)}, u32[]{:S(2)}, u32[]{:S(2)}) async-start(f32[8,128,128]{2,1,0:T(8,128)} %broadcast_in_dim.57), calls=%async_computation.3 | async-start | bytes 1048576 | tf_op jit(solution)/shard_map/all_to_all | solution.py:27
  78.6 4.1 %collective-permute-start.4 = (f32[32,32,128]{2,1,0:T(8,128)S(1)}, f32[32,32,128]{2,1,0:T(8,128)}, u32[]{:S(2)}, u32[]{:S(2)}) collective-permute-start(f32[32,32,128]{2,1,0:T(8,128)S(1)} %all-to-all-done.2.own_ref), channel_id=1, source_target_pairs={{0,32},{32,0},{64,96},{96,64},{128,160},{160,128},{192,224},{224,1... | collective-permute-start | bytes 1572872 | tf_op jit(solution)/shard_map/ppermute | solution.py:227
  82.7 3.7 %collective-permute-start.5 = (f32[8,64,128]{2,1,0:T(8,128)S(1)}, f32[8,64,128]{2,1,0:T(8,128)S(1)}, u32[]{:S(2)}, u32[]{:S(2)}) collective-permute-start(f32[8,64,128]{2,1,0:T(8,128)S(1)} %all-to-all-done.near0_ref), channel_id=1, source_target_pairs={{0,3},{1,2},{2,1},{3,0},{4,7},{5,6},{6,5},{7,4},{8,11},{9,10},{10,... | collective-permute-start | bytes 786440 | tf_op jit(solution)/shard_map/ppermute | solution.py:33
  86.4 7.3 %collective-permute-done.5.near3_ref = f32[8,64,128]{2,1,0:T(8,128)S(1)} collective-permute-done((f32[8,64,128]{2,1,0:T(8,128)S(1)}, f32[8,64,128]{2,1,0:T(8,128)S(1)}, u32[]{:S(2)}, u32[]{:S(2)}) %collective-permute-start.5) | collective-permute-done | bytes 262176 | tf_op jit(solution)/shard_map/ppermute | solution.py:33
  93.7 0.4 lower.1
  94.1 0.0 collective-permute-done.4.far_ref
  94.1 0.0 copy-start
  94.1 0.0 copy-start.1
  94.1 5.3 %squares.1 = (bf16[4,256,256]{2,1,0:T(8,128)(2,1)S(1)}, bf16[4,256,256]{2,1,0:T(8,128)(2,1)S(1)}) custom-call(s32[1]{0:T(128)} %bitcast.21.core_ref, f32[32,32,128]{2,1,0:T(8,128)S(1)} %all-to-all-done.2.own_ref, f32[32,32,128]{2,1,0:T(8,128)} %collective-permute-done.4.far_ref), custom_call_target="tpu_custom_call" | custom-call | flops 2818572288 | bytes 2097152 | tf_op jit(solution)/shard_map/squares/pallas_call | solution.py:77
  99.4 0.0 all-to-all-done.3.wide_ref
  99.4 0.0 copy-done
  99.4 0.0 copy-done.1
  99.5 2.6 %update.1 = f32[512,128]{1,0:T(8,128)} custom-call(s32[1]{0:T(128)} %bitcast.me_ref, s32[2,256]{1,0:T(2,128)S(1)} %copy-done.1, f32[8,128,128]{2,1,0:T(8,128)S(1)} %all-to-all-done.3.wide_ref, bf16[4,256,256]{2,1,0:T(8,128)(2,1)S(1)} %get-tuple-element.35.sq_high_ref, bf16[4,256,256]{2,1,0:T(8,128)(2,1)S(1)} %get-tuple-element.36.sq_low_ref, ...), custom_call_target="tpu_custom_call" | custom-call | flops 536870912 | bytes 3145728 | tf_op jit(solution)/shard_map/update/pallas_call | solution.py:161
  (17 shorter events, 0.2 us)
Async XLA Ops:
  2.8 0.8 copy-start.2
  4.0 12.9 %collective-permute-start = (f32[544,128]{1,0:T(8,128)S(1)}, f32[544,128]{1,0:T(8,128)S(1)}, u32[]{:S(2)}, u32[]{:S(2)}) collective-permute-start(f32[544,128]{1,0:T(8,128)S(1)} %pad_maximum_fusion.1), channel_id=1, source_target_pairs={{0,32},{32,0},{64,96},{96,64},{128,160},{160,128},{192,224},{224,1... | collective-permute-start | bytes 835592 | tf_op jit(solution)/shard_map/ppermute | solution.py:208
  13.5 15.7 %all-to-all-start = ((f32[8,64,128]{2,1,0:T(8,128)}), f32[8,64,128]{2,1,0:T(8,128)S(1)}, u32[]{:S(2)}, u32[]{:S(2)}) async-start(f32[8,64,128]{2,1,0:T(8,128)} %broadcast_in_dim.55), calls=%async_computation | async-start | bytes 524288 | tf_op jit(solution)/shard_map/all_to_all | solution.py:27
  29.2 23.3 %all-to-all-start.1 = ((f32[8,96,128]{2,1,0:T(8,128)}), f32[8,96,128]{2,1,0:T(8,128)S(1)}, u32[]{:S(2)}, u32[]{:S(2)}) async-start(f32[8,96,128]{2,1,0:T(8,128)} %pad_maximum_fusion), calls=%async_computation.1 | async-start | bytes 786432 | tf_op jit(solution)/shard_map/all_to_all | solution.py:214
  37.3 9.0 %collective-permute-start.1 = (f32[8,64,128]{2,1,0:T(8,128)S(1)}, f32[8,64,128]{2,1,0:T(8,128)S(1)}, u32[]{:S(2)}, u32[]{:S(2)}) collective-permute-start(f32[8,64,128]{2,1,0:T(8,128)S(1)} %all-to-all-done.near0_ref), channel_id=1, source_target_pairs={{0,1},{1,0},{2,3},{3,2},{4,5},{5,4},{6,7},{7,6},{8,9},{9,8},{10,11... | collective-permute-start | bytes 786440 | tf_op jit(solution)/shard_map/ppermute | solution.py:33
  53.3 20.9 %all-to-all-start.2 = ((f32[32,32,128]{2,1,0:T(8,128)}), f32[32,32,128]{2,1,0:T(8,128)S(1)}, u32[]{:S(2)}, u32[]{:S(2)}) async-start(f32[32,32,128]{2,1,0:T(8,128)} %broadcast_in_dim.56), calls=%async_computation.2 | async-start | bytes 1048576 | tf_op jit(solution)/shard_map/all_to_all | solution.py:220
  57.7 15.3 %collective-permute-start.3 = (f32[8,64,128]{2,1,0:T(8,128)S(1)}, f32[8,64,128]{2,1,0:T(8,128)S(1)}, u32[]{:S(2)}, u32[]{:S(2)}) collective-permute-start(f32[8,64,128]{2,1,0:T(8,128)S(1)} %all-to-all-done.near0_ref), channel_id=1, source_target_pairs={{0,2},{1,3},{2,0},{3,1},{4,6},{5,7},{6,4},{7,5},{8,10},{9,11},{10,... | collective-permute-start | bytes 786440 | tf_op jit(solution)/shard_map/ppermute | solution.py:33
  62.4 4.1 %collective-permute-start.2 = (f32[64,128]{1,0:T(8,128)S(1)}, f32[64,128]{1,0:T(8,128)S(1)}, u32[]{:S(2)}, u32[]{:S(2)}) collective-permute-start(f32[64,128]{1,0:T(8,128)S(1)} %slice.77), channel_id=1, source_target_pairs={{0,32},{32,0},{64,96},{96,64},{128,160},{160,128},{192,224},{224,1... | collective-permute-start | bytes 98312 | tf_op jit(solution)/shard_map/ppermute | solution.py:222
  75.1 24.4 %all-to-all-start.3 = ((f32[8,128,128]{2,1,0:T(8,128)}), f32[8,128,128]{2,1,0:T(8,128)S(1)}, u32[]{:S(2)}, u32[]{:S(2)}) async-start(f32[8,128,128]{2,1,0:T(8,128)} %broadcast_in_dim.57), calls=%async_computation.3 | async-start | bytes 1048576 | tf_op jit(solution)/shard_map/all_to_all | solution.py:27
  78.6 15.5 %collective-permute-start.4 = (f32[32,32,128]{2,1,0:T(8,128)S(1)}, f32[32,32,128]{2,1,0:T(8,128)}, u32[]{:S(2)}, u32[]{:S(2)}) collective-permute-start(f32[32,32,128]{2,1,0:T(8,128)S(1)} %all-to-all-done.2.own_ref), channel_id=1, source_target_pairs={{0,32},{32,0},{64,96},{96,64},{128,160},{160,128},{192,224},{224,1... | collective-permute-start | bytes 1572872 | tf_op jit(solution)/shard_map/ppermute | solution.py:227
  82.7 11.0 %collective-permute-start.5 = (f32[8,64,128]{2,1,0:T(8,128)S(1)}, f32[8,64,128]{2,1,0:T(8,128)S(1)}, u32[]{:S(2)}, u32[]{:S(2)}) collective-permute-start(f32[8,64,128]{2,1,0:T(8,128)S(1)} %all-to-all-done.near0_ref), channel_id=1, source_target_pairs={{0,3},{1,2},{2,1},{3,0},{4,7},{5,6},{6,5},{7,4},{8,11},{9,10},{10,... | collective-permute-start | bytes 786440 | tf_op jit(solution)/shard_map/ppermute | solution.py:33
  94.1 5.3 %copy-start = (f32[512,128]{1,0:T(8,128)S(1)}, f32[512,128]{1,0:T(8,128)}, u32[]{:S(2)}) copy-start(f32[512,128]{1,0:T(8,128)} %block_ref.1) | copy-start | bytes 786436
  94.1 5.3 %copy-start.1 = (s32[2,256]{1,0:T(2,128)S(1)}, s32[2,256]{1,0:T(2,128)}, u32[]{:S(2)}) copy-start(s32[2,256]{1,0:T(2,128)} %piv_ref.1) | copy-start | bytes 6148

commit v5 on v4

--- a/solution.py
+++ b/solution.py
@@ -10,8 +10,10 @@
 LIMIT = 16 << 20
 NZ, NC = 8, 2
 NY, NX = 8, 4
-Z_GROUPS = [[NC * z + core for z in range(NZ)] for core in range(NC)]
-Y_GROUPS = [[NX * y + x for y in range(NY)] for x in range(NX)]
+TURN = [0, 4, 1, 5, 2, 6, 3, 7]
+Z_GROUPS = [[NC * z + core for z in TURN] for core in range(NC)]
+Y_GROUPS = [[NX * y + x for y in TURN] for x in range(NX)]
+COL_GROUPS = [[NX * y + x for x in range(NX) for y in TURN]]
 PAIR = [(i, i ^ 1) for i in range(NZ * NC)]
 
 
@@ -46,6 +48,11 @@
     return dot(a[0], b[0]) + dot(a[0], b[1]) + dot(a[1], b[0])
 
 
+def dot3_narrow(a, b):
+    both = dot(a[0], jnp.concatenate(b, 1))
+    return both[:, :128] + both[:, 128:] + dot(a[1], b[0])
+
+
 def halves_of(core, own, far):
     return jnp.where(core == 0, own, far), jnp.where(core == 0, far, own)
 
@@ -54,8 +61,9 @@
     core = core_ref[0]
     squares = []
     for p in range(4):
-        own = own_ref[:, 8 * p : 8 * p + 8, :].reshape(PW, 128)
-        far = far_ref[:, 8 * p : 8 * p + 8, :].reshape(PW, 128)
+        order = [COL_GROUPS[0].index(c) for c in range(NX * NY)]
+        own = jnp.concatenate([own_ref[i, 8 * p : 8 * p + 8, :] for i in order], 0)
+        far = jnp.concatenate([far_ref[i, 8 * p : 8 * p + 8, :] for i in order], 0)
         squares.append(jnp.concatenate(halves_of(core, own, far), 1).T)
     row = lax.broadcasted_iota(jnp.int32, (PW, PW), 0)
     col = lax.broadcasted_iota(jnp.int32, (PW, PW), 1)
@@ -89,11 +97,11 @@
     x_at = col_ref[0] % NX
     for bits, ref in enumerate((near0_ref, near1_ref, near2_ref, near3_ref)):
         x = x_at ^ bits
-        for y in range(NY):
+        for i, y in enumerate(TURN):
             at = pl.multiple_of((NX * y + x) * 8, 8)
             for p in range(2):
                 for h in range(4):
-                    tile = ref[y, 32 * p + 8 * h : 32 * p + 8 * h + 8, :]
+                    tile = ref[i, 32 * p + 8 * h : 32 * p + 8 * h + 8, :]
                     turned_ref[p, pl.ds(at, 8), 128 * h : 128 * h + 128] = tile
 
     for p in range(2):
@@ -125,9 +133,9 @@
         return wide_ref[:, at : at + 32, :].reshape(PW, 128)
 
     square = [(sq_high_ref[p], sq_low_ref[p]) for p in range(4)]
-    upper0 = dot3(square[0], split(rows(0)))
+    upper0 = dot3_narrow(square[0], split(rows(0)))
     pair0 = split(upper0)
-    upper1 = dot3(square[1], split(rows(64) - dot3(square[3], pair0)))
+    upper1 = dot3_narrow(square[1], split(rows(64) - dot3_narrow(square[3], pair0)))
 
     @pl.when(me == 0)
     def _():
@@ -136,7 +144,7 @@
 
     @pl.when(me != 0)
     def _():
-        second = rows(96) - dot3(square[2], pair0)
+        second = rows(96) - dot3_narrow(square[2], pair0)
         at = lax.broadcasted_iota(jnp.int32, (512, PW), 0) + start
 
         def place(p, x, work):
@@ -151,9 +159,9 @@
             return jnp.where(one[:, 128:] > 0, moved, work)
 
         work = place(0, rows(32), block_ref[...])
-        work = work - dot3((lo_high_ref[0], lo_low_ref[0]), pair0)
+        work = work - dot3_narrow((lo_high_ref[0], lo_low_ref[0]), pair0)
         work = place(1, second, work)
-        out_ref[...] = work - dot3((lo_high_ref[1], lo_low_ref[1]), split(upper1))
+        out_ref[...] = work - dot3_narrow((lo_high_ref[1], lo_low_ref[1]), split(upper1))
 
 
 def update_of(me, pivots, wide, squares, lower, block):
@@ -217,7 +225,7 @@
 
     part = jnp.sum(part, 0)
     tile = jnp.broadcast_to(part[64:], (NX * NY, 32, 128))
-    tile = lax.all_to_all(tile, "col", 0, 0, tiled=True)
+    tile = lax.all_to_all(tile, "col", 0, 0, tiled=True, axis_index_groups=COL_GROUPS)
     near2 = flip(near, 2)
     far = lax.ppermute(part[:64], "row", PAIR)
     both = jnp.where(core == 0, jnp.concatenate([part[:64], far]), jnp.concatenate([far, part[:64]]))

time: 103 us -> 101 us (0.981)
  waiting for transfers between devices: 39.2 us -> 24 us
  starting transfers between devices: 47.1 us -> 60.7 us
    all_to_all x1, starting transfers between devices: 4.41 us -> 10.8 us  [step(): lax.all_to_all(tile, 'col', 0, 0, tiled=True, axis_index_groups=COL_GROUPS)]
    ppermute x3, waiting for transfers between devices: 19.6 us -> 13.5 us  [flip(): return lax.ppermute(x, 'col', [(i, i ^ bits) for i in range(NX * NY)])]
    all_to_all x1, waiting for transfers between devices: 6.1 us -> 0.88 us  [step(): lax.all_to_all(part, 'row', 0, 0, tiled=True, axis_index_groups=Z_GROUPS)]
    all_to_all x2, starting transfers between devices: 6.9 us -> 11.9 us  [spread(): lax.all_to_all(jnp.broadcast_to(x[None], (n,) + x.shape), axis, 0, 0, til...]
    all_to_all x2, waiting for transfers between devices: 11.4 us -> 7.17 us  [spread(): lax.all_to_all(jnp.broadcast_to(x[None], (n,) + x.shape), axis, 0, 0, til...]
    ppermute x1, starting transfers between devices: 3.29 us -> 5.63 us  [step(): far = lax.ppermute(part[:64], 'row', PAIR)]
    ppermute x1, starting transfers between devices: 4.15 us -> 5.51 us  [step(): far = lax.ppermute(tile, 'row', PAIR)]
where the time goes in v5:
time: 101 us; the launch traced here: 99.9 us
  starting transfers between devices  60.7 us (60%)
  waiting for transfers between devices  24 us (24%)
  Pallas kernels  7.84 us (8%)
  local copies, waits for them, and re-layouts  3.96 us (4%)
  matrix products  2 us (2%)
  other arithmetic  1.24 us (1%)
    ppermute x3, waiting for transfers between devices, flip(): return lax.ppermute(x, 'col', [(i, i ^ bits) for i in range(NX * NY)])  13.5 us
    all_to_all x2, starting transfers between devices, spread(): lax.all_to_all(jnp.broadcast_to(x[None], (n,) + x.shape), axis, 0, 0, til...  11.9 us
    ppermute x3, starting transfers between devices, flip(): return lax.ppermute(x, 'col', [(i, i ^ bits) for i in range(NX * NY)])  10.8 us
    all_to_all x1, starting transfers between devices, step(): lax.all_to_all(tile, 'col', 0, 0, tiled=True, axis_index_groups=COL_GROUPS)  10.8 us
    ppermute x1, starting transfers between devices, step(): part = halves(True) + lax.ppermute(halves(False), 'row', PAIR)  8.75 us
    all_to_all x1, starting transfers between devices, step(): lax.all_to_all(part, 'row', 0, 0, tiled=True, axis_index_groups=Z_GROUPS)  7.31 us
    all_to_all x2, waiting for transfers between devices, spread(): lax.all_to_all(jnp.broadcast_to(x[None], (n,) + x.shape), axis, 0, 0, til...  7.17 us
    ppermute x1, starting transfers between devices, step(): far = lax.ppermute(part[:64], 'row', PAIR)  5.63 us
  transfers between devices with their start and end apart: 10, of which 7 were waited for; matrix products, arithmetic and copies ran while one was open for 2% of the time, Pallas kernels for 6%

profile of v5, /device:TPU:1, one launch (start us, length us, event | category | flops | bytes accessed | tf_op | source)
XLA Modules:
  0.0 99.9 jit_solution(15046295593733149407)
XLA Ops:
  0.0 0.8 fusion.6
  0.8 0.2 select_reduce_fusion.1
  1.1 1.7 %fusion = f32[1024,128]{1,0:T(8,128)S(1)} fusion(f32[512,128]{1,0:T(8,128)} %block_ref.1, s32[1024]{0:T(1024)S(1)} %add_subtract_fusion), kind=kOutput, calls=%fused_computation.1 | convolution fusion | flops 403177472 | bytes 790528 | tf_op jit(solution)/shard_map/dot_general | solution.py:21
  2.8 0.0 copy-start.2
  2.8 0.7 copy-done.2
  3.5 0.3 convolution_bitcast_fusion
  3.8 0.1 slice_select_fusion.1
  4.0 8.7 %collective-permute-start = (f32[544,128]{1,0:T(8,128)S(1)}, f32[544,128]{1,0:T(8,128)S(1)}, u32[]{:S(2)}, u32[]{:S(2)}) collective-permute-start(f32[544,128]{1,0:T(8,128)S(1)} %pad_maximum_fusion.1), channel_id=1, source_target_pairs={{0,32},{32,0},{64,96},{96,64},{128,160},{160,128},{192,224},{224,1... | collective-permute-start | bytes 835592 | tf_op jit(solution)/shard_map/ppermute | solution.py:216
  12.7 0.7 broadcast_in_dim.55
  13.5 3.4 %all-to-all-start = ((f32[8,64,128]{2,1,0:T(8,128)}), f32[8,64,128]{2,1,0:T(8,128)S(1)}, u32[]{:S(2)}, u32[]{:S(2)}) async-start(f32[8,64,128]{2,1,0:T(8,128)} %broadcast_in_dim.55), calls=%async_computation | async-start | bytes 524288 | tf_op jit(solution)/shard_map/all_to_all | solution.py:29
  16.9 0.0 collective-permute-done
  17.0 0.8 pad_maximum_fusion
  17.8 7.2 %all-to-all-done.near0_ref = f32[8,64,128]{2,1,0:T(8,128)S(1)} async-done(((f32[8,64,128]{2,1,0:T(8,128)}), f32[8,64,128]{2,1,0:T(8,128)S(1)}, u32[]{:S(2)}, u32[]{:S(2)}) %all-to-all-start) | async-done | bytes 262176 | tf_op jit(solution)/shard_map/all_to_all | solution.py:29
  24.9 7.3 %all-to-all-start.1 = ((f32[8,96,128]{2,1,0:T(8,128)}), f32[8,96,128]{2,1,0:T(8,128)S(1)}, u32[]{:S(2)}, u32[]{:S(2)}) async-start(f32[8,96,128]{2,1,0:T(8,128)} %pad_maximum_fusion), calls=%async_computation.1 | async-start | bytes 786432 | tf_op jit(solution)/shard_map/all_to_all | solution.py:222
  32.2 3.1 %collective-permute-start.1 = (f32[8,64,128]{2,1,0:T(8,128)S(1)}, f32[8,64,128]{2,1,0:T(8,128)S(1)}, u32[]{:S(2)}, u32[]{:S(2)}) collective-permute-start(f32[8,64,128]{2,1,0:T(8,128)S(1)} %all-to-all-done.near0_ref), channel_id=1, source_target_pairs={{0,1},{1,0},{2,3},{3,2},{4,5},{5,4},{6,7},{7,6},{8,9},{9,8},{10,11... | collective-permute-start | bytes 786440 | tf_op jit(solution)/shard_map/ppermute | solution.py:35
  35.4 4.0 %collective-permute-done.1.near1_ref = f32[8,64,128]{2,1,0:T(8,128)S(1)} collective-permute-done((f32[8,64,128]{2,1,0:T(8,128)S(1)}, f32[8,64,128]{2,1,0:T(8,128)S(1)}, u32[]{:S(2)}, u32[]{:S(2)}) %collective-permute-start.1) | collective-permute-done | bytes 262176 | tf_op jit(solution)/shard_map/ppermute | solution.py:35
  39.3 0.9 all-to-all-done.1
  40.3 0.9 broadcast_in_dim.56
  41.1 10.8 %all-to-all-start.2 = ((f32[32,32,128]{2,1,0:T(8,128)}), f32[32,32,128]{2,1,0:T(8,128)S(1)}, u32[]{:S(2)}, u32[]{:S(2)}) async-start(f32[32,32,128]{2,1,0:T(8,128)} %broadcast_in_dim.56), calls=%async_computation.2 | async-start | bytes 1048576 | tf_op jit(solution)/shard_map/all_to_all | solution.py:228
  51.9 4.7 %collective-permute-start.3 = (f32[8,64,128]{2,1,0:T(8,128)S(1)}, f32[8,64,128]{2,1,0:T(8,128)S(1)}, u32[]{:S(2)}, u32[]{:S(2)}) collective-permute-start(f32[8,64,128]{2,1,0:T(8,128)S(1)} %all-to-all-done.near0_ref), channel_id=1, source_target_pairs={{0,2},{1,3},{2,0},{3,1},{4,6},{5,7},{6,4},{7,5},{8,10},{9,11},{10,... | collective-permute-start | bytes 786440 | tf_op jit(solution)/shard_map/ppermute | solution.py:35
  56.6 5.6 %collective-permute-start.2 = (f32[64,128]{1,0:T(8,128)S(1)}, f32[64,128]{1,0:T(8,128)S(1)}, u32[]{:S(2)}, u32[]{:S(2)}) collective-permute-start(f32[64,128]{1,0:T(8,128)S(1)} %slice.77), channel_id=1, source_target_pairs={{0,32},{32,0},{64,96},{96,64},{128,160},{160,128},{192,224},{224,1... | collective-permute-start | bytes 98312 | tf_op jit(solution)/shard_map/ppermute | solution.py:230
  62.2 0.8 collective-permute-done.2
  63.1 1.6 %collective-permute-done.3.near2_ref = f32[8,64,128]{2,1,0:T(8,128)S(1)} collective-permute-done((f32[8,64,128]{2,1,0:T(8,128)S(1)}, f32[8,64,128]{2,1,0:T(8,128)S(1)}, u32[]{:S(2)}, u32[]{:S(2)}) %collective-permute-start.3) | collective-permute-done | bytes 262176 | tf_op jit(solution)/shard_map/ppermute | solution.py:35
  64.6 1.6 %all-to-all-done.2.own_ref = f32[32,32,128]{2,1,0:T(8,128)S(1)} async-done(((f32[32,32,128]{2,1,0:T(8,128)}), f32[32,32,128]{2,1,0:T(8,128)S(1)}, u32[]{:S(2)}, u32[]{:S(2)}) %all-to-all-start.2) | async-done | bytes 524320 | tf_op jit(solution)/shard_map/all_to_all | solution.py:228
  66.2 0.8 broadcast_in_dim.57
  67.1 8.5 %all-to-all-start.3 = ((f32[8,128,128]{2,1,0:T(8,128)}), f32[8,128,128]{2,1,0:T(8,128)S(1)}, u32[]{:S(2)}, u32[]{:S(2)}) async-start(f32[8,128,128]{2,1,0:T(8,128)} %broadcast_in_dim.57), calls=%async_computation.3 | async-start | bytes 1048576 | tf_op jit(solution)/shard_map/all_to_all | solution.py:29
  75.6 5.5 %collective-permute-start.4 = (f32[32,32,128]{2,1,0:T(8,128)S(1)}, f32[32,32,128]{2,1,0:T(8,128)}, u32[]{:S(2)}, u32[]{:S(2)}) collective-permute-start(f32[32,32,128]{2,1,0:T(8,128)S(1)} %all-to-all-done.2.own_ref), channel_id=1, source_target_pairs={{0,32},{32,0},{64,96},{96,64},{128,160},{160,128},{192,224},{224,1... | collective-permute-start | bytes 1572872 | tf_op jit(solution)/shard_map/ppermute | solution.py:235
  81.1 3.0 %collective-permute-start.5 = (f32[8,64,128]{2,1,0:T(8,128)S(1)}, f32[8,64,128]{2,1,0:T(8,128)S(1)}, u32[]{:S(2)}, u32[]{:S(2)}) collective-permute-start(f32[8,64,128]{2,1,0:T(8,128)S(1)} %all-to-all-done.near0_ref), channel_id=1, source_target_pairs={{0,3},{1,2},{2,1},{3,0},{4,7},{5,6},{6,5},{7,4},{8,11},{9,10},{10,... | collective-permute-start | bytes 786440 | tf_op jit(solution)/shard_map/ppermute | solution.py:35
  84.1 7.9 %collective-permute-done.5.near3_ref = f32[8,64,128]{2,1,0:T(8,128)S(1)} collective-permute-done((f32[8,64,128]{2,1,0:T(8,128)S(1)}, f32[8,64,128]{2,1,0:T(8,128)S(1)}, u32[]{:S(2)}, u32[]{:S(2)}) %collective-permute-start.5) | collective-permute-done | bytes 262176 | tf_op jit(solution)/shard_map/ppermute | solution.py:35
  92.0 0.4 lower.1
  92.4 0.0 collective-permute-done.4.far_ref
  92.5 0.0 copy-start
  92.5 0.0 copy-start.1
  92.5 5.3 %squares.1 = (bf16[4,256,256]{2,1,0:T(8,128)(2,1)S(1)}, bf16[4,256,256]{2,1,0:T(8,128)(2,1)S(1)}) custom-call(s32[1]{0:T(128)} %bitcast.21.core_ref, f32[32,32,128]{2,1,0:T(8,128)S(1)} %all-to-all-done.2.own_ref, f32[32,32,128]{2,1,0:T(8,128)} %collective-permute-done.4.far_ref), custom_call_target="tpu_custom_call" | custom-call | flops 2818572288 | bytes 2097152 | tf_op jit(solution)/shard_map/squares/pallas_call | solution.py:85
  97.8 0.0 all-to-all-done.3.wide_ref
  97.8 0.0 copy-done
  97.8 0.0 copy-done.1
  97.8 2.1 %update.1 = f32[512,128]{1,0:T(8,128)} custom-call(s32[1]{0:T(128)} %bitcast.me_ref, s32[2,256]{1,0:T(2,128)S(1)} %copy-done.1, f32[8,128,128]{2,1,0:T(8,128)S(1)} %all-to-all-done.3.wide_ref, bf16[4,256,256]{2,1,0:T(8,128)(2,1)S(1)} %get-tuple-element.35.sq_high_ref, bf16[4,256,256]{2,1,0:T(8,128)(2,1)S(1)} %get-tuple-element.36.sq_low_ref, ...), custom_call_target="tpu_custom_call" | custom-call | flops 536870912 | bytes 3145728 | tf_op jit(solution)/shard_map/update/pallas_call | solution.py:169
  (17 shorter events, 0.2 us)
Async XLA Ops:
  2.8 0.8 copy-start.2
  4.0 12.9 %collective-permute-start = (f32[544,128]{1,0:T(8,128)S(1)}, f32[544,128]{1,0:T(8,128)S(1)}, u32[]{:S(2)}, u32[]{:S(2)}) collective-permute-start(f32[544,128]{1,0:T(8,128)S(1)} %pad_maximum_fusion.1), channel_id=1, source_target_pairs={{0,32},{32,0},{64,96},{96,64},{128,160},{160,128},{192,224},{224,1... | collective-permute-start | bytes 835592 | tf_op jit(solution)/shard_map/ppermute | solution.py:216
  13.5 11.5 %all-to-all-start = ((f32[8,64,128]{2,1,0:T(8,128)}), f32[8,64,128]{2,1,0:T(8,128)S(1)}, u32[]{:S(2)}, u32[]{:S(2)}) async-start(f32[8,64,128]{2,1,0:T(8,128)} %broadcast_in_dim.55), calls=%async_computation | async-start | bytes 524288 | tf_op jit(solution)/shard_map/all_to_all | solution.py:29
  24.9 15.3 %all-to-all-start.1 = ((f32[8,96,128]{2,1,0:T(8,128)}), f32[8,96,128]{2,1,0:T(8,128)S(1)}, u32[]{:S(2)}, u32[]{:S(2)}) async-start(f32[8,96,128]{2,1,0:T(8,128)} %pad_maximum_fusion), calls=%async_computation.1 | async-start | bytes 786432 | tf_op jit(solution)/shard_map/all_to_all | solution.py:222
  32.2 7.1 %collective-permute-start.1 = (f32[8,64,128]{2,1,0:T(8,128)S(1)}, f32[8,64,128]{2,1,0:T(8,128)S(1)}, u32[]{:S(2)}, u32[]{:S(2)}) collective-permute-start(f32[8,64,128]{2,1,0:T(8,128)S(1)} %all-to-all-done.near0_ref), channel_id=1, source_target_pairs={{0,1},{1,0},{2,3},{3,2},{4,5},{5,4},{6,7},{7,6},{8,9},{9,8},{10,11... | collective-permute-start | bytes 786440 | tf_op jit(solution)/shard_map/ppermute | solution.py:35
  41.1 25.1 %all-to-all-start.2 = ((f32[32,32,128]{2,1,0:T(8,128)}), f32[32,32,128]{2,1,0:T(8,128)S(1)}, u32[]{:S(2)}, u32[]{:S(2)}) async-start(f32[32,32,128]{2,1,0:T(8,128)} %broadcast_in_dim.56), calls=%async_computation.2 | async-start | bytes 1048576 | tf_op jit(solution)/shard_map/all_to_all | solution.py:228
  51.9 12.7 %collective-permute-start.3 = (f32[8,64,128]{2,1,0:T(8,128)S(1)}, f32[8,64,128]{2,1,0:T(8,128)S(1)}, u32[]{:S(2)}, u32[]{:S(2)}) collective-permute-start(f32[8,64,128]{2,1,0:T(8,128)S(1)} %all-to-all-done.near0_ref), channel_id=1, source_target_pairs={{0,2},{1,3},{2,0},{3,1},{4,6},{5,7},{6,4},{7,5},{8,10},{9,11},{10,... | collective-permute-start | bytes 786440 | tf_op jit(solution)/shard_map/ppermute | solution.py:35
  56.6 6.5 %collective-permute-start.2 = (f32[64,128]{1,0:T(8,128)S(1)}, f32[64,128]{1,0:T(8,128)S(1)}, u32[]{:S(2)}, u32[]{:S(2)}) collective-permute-start(f32[64,128]{1,0:T(8,128)S(1)} %slice.77), channel_id=1, source_target_pairs={{0,32},{32,0},{64,96},{96,64},{128,160},{160,128},{192,224},{224,1... | collective-permute-start | bytes 98312 | tf_op jit(solution)/shard_map/ppermute | solution.py:230
  67.1 30.7 %all-to-all-start.3 = ((f32[8,128,128]{2,1,0:T(8,128)}), f32[8,128,128]{2,1,0:T(8,128)S(1)}, u32[]{:S(2)}, u32[]{:S(2)}) async-start(f32[8,128,128]{2,1,0:T(8,128)} %broadcast_in_dim.57), calls=%async_computation.3 | async-start | bytes 1048576 | tf_op jit(solution)/shard_map/all_to_all | solution.py:29
  75.6 16.9 %collective-permute-start.4 = (f32[32,32,128]{2,1,0:T(8,128)S(1)}, f32[32,32,128]{2,1,0:T(8,128)}, u32[]{:S(2)}, u32[]{:S(2)}) collective-permute-start(f32[32,32,128]{2,1,0:T(8,128)S(1)} %all-to-all-done.2.own_ref), channel_id=1, source_target_pairs={{0,32},{32,0},{64,96},{96,64},{128,160},{160,128},{192,224},{224,1... | collective-permute-start | bytes 1572872 | tf_op jit(solution)/shard_map/ppermute | solution.py:235
  81.1 11.0 %collective-permute-start.5 = (f32[8,64,128]{2,1,0:T(8,128)S(1)}, f32[8,64,128]{2,1,0:T(8,128)S(1)}, u32[]{:S(2)}, u32[]{:S(2)}) collective-permute-start(f32[8,64,128]{2,1,0:T(8,128)S(1)} %all-to-all-done.near0_ref), channel_id=1, source_target_pairs={{0,3},{1,2},{2,1},{3,0},{4,7},{5,6},{6,5},{7,4},{8,11},{9,10},{10,... | collective-permute-start | bytes 786440 | tf_op jit(solution)/shard_map/ppermute | solution.py:35
  92.5 5.3 %copy-start = (f32[512,128]{1,0:T(8,128)S(1)}, f32[512,128]{1,0:T(8,128)}, u32[]{:S(2)}) copy-start(f32[512,128]{1,0:T(8,128)} %block_ref.1) | copy-start | bytes 786436
  92.5 5.3 %copy-start.1 = (s32[2,256]{1,0:T(2,128)S(1)}, s32[2,256]{1,0:T(2,128)}, u32[]{:S(2)}) copy-start(s32[2,256]{1,0:T(2,128)} %piv_ref.1) | copy-start | bytes 6148

commit v6 on v5

--- a/solution.py
+++ b/solution.py
@@ -10,10 +10,10 @@
 LIMIT = 16 << 20
 NZ, NC = 8, 2
 NY, NX = 8, 4
-TURN = [0, 4, 1, 5, 2, 6, 3, 7]
+TURN = [0, 4, 2, 6, 3, 7, 1, 5]
 Z_GROUPS = [[NC * z + core for z in TURN] for core in range(NC)]
 Y_GROUPS = [[NX * y + x for y in TURN] for x in range(NX)]
-COL_GROUPS = [[NX * y + x for x in range(NX) for y in TURN]]
+COL_GROUPS = [[NX * y + x for x in (0, 2, 1, 3) for y in range(NY)]]
 PAIR = [(i, i ^ 1) for i in range(NZ * NC)]
 
 
@@ -93,49 +93,36 @@
     )(core, own, far)
 
 
-def lower_kernel(col_ref, near0_ref, near1_ref, near2_ref, near3_ref, high_ref, low_ref, turned_ref):
-    x_at = col_ref[0] % NX
-    for bits, ref in enumerate((near0_ref, near1_ref, near2_ref, near3_ref)):
-        x = x_at ^ bits
+def update_kernel(
+    at_ref, piv_ref, wide_ref, sq_high_ref, sq_low_ref, block_ref, n0_ref, n1_ref, n2_ref, n3_ref,
+    out_ref, near_ref, turned_ref, sems,
+):
+    me = at_ref[0]
+    copies = [
+        pltpu.make_async_copy(ref, near_ref.at[bits], sems.at[bits])
+        for bits, ref in enumerate((n0_ref, n1_ref, n2_ref, n3_ref))
+    ]
+    for copy in copies:
+        copy.start()
+    start = me * 512
+
+    def rows(at):
+        return wide_ref[:, at : at + 32, :].reshape(PW, 128)
+
+    square = [(sq_high_ref[p], sq_low_ref[p]) for p in range(4)]
+    upper0 = dot3_narrow(square[0], split(rows(0)))
+    pair0 = split(upper0)
+    upper1 = dot3_narrow(square[1], split(rows(64) - dot3_narrow(square[3], pair0)))
+
+    for bits, copy in enumerate(copies):
+        copy.wait()
+        x = (at_ref[1] % NX) ^ bits
         for i, y in enumerate(TURN):
             at = pl.multiple_of((NX * y + x) * 8, 8)
             for p in range(2):
                 for h in range(4):
-                    tile = ref[i, 32 * p + 8 * h : 32 * p + 8 * h + 8, :]
+                    tile = near_ref[bits, i, 32 * p + 8 * h : 32 * p + 8 * h + 8, :]
                     turned_ref[p, pl.ds(at, 8), 128 * h : 128 * h + 128] = tile
-
-    for p in range(2):
-        high, low = split(turned_ref[p].T)
-        high_ref[p] = high
-        low_ref[p] = low
-
-
-def lower_of(col, *near):
-    vmem = pl.BlockSpec(memory_space=pltpu.VMEM)
-    pair = jax.ShapeDtypeStruct((2, 512, PW), jnp.bfloat16)
-    return pl.pallas_call(
-        lower_kernel,
-        out_shape=(pair, pair),
-        in_specs=[pl.BlockSpec(memory_space=pltpu.SMEM)] + [vmem] * 4,
-        out_specs=(vmem, vmem),
-        scratch_shapes=[pltpu.VMEM((2, PW, 512), jnp.float32)],
-        cost_estimate=pl.CostEstimate(flops=1 << 20, bytes_accessed=2 << 20, transcendentals=0),
-        compiler_params=pltpu.CompilerParams(vmem_limit_bytes=LIMIT),
-        name="lower",
-    )(col, *near)
-
-
-def update_kernel(me_ref, piv_ref, wide_ref, sq_high_ref, sq_low_ref, lo_high_ref, lo_low_ref, block_ref, out_ref):
-    me = me_ref[0]
-    start = me * 512
-
-    def rows(at):
-        return wide_ref[:, at : at + 32, :].reshape(PW, 128)
-
-    square = [(sq_high_ref[p], sq_low_ref[p]) for p in range(4)]
-    upper0 = dot3_narrow(square[0], split(rows(0)))
-    pair0 = split(upper0)
-    upper1 = dot3_narrow(square[1], split(rows(64) - dot3_narrow(square[3], pair0)))
 
     @pl.when(me == 0)
     def _():
@@ -159,22 +146,27 @@
             return jnp.where(one[:, 128:] > 0, moved, work)
 
         work = place(0, rows(32), block_ref[...])
-        work = work - dot3_narrow((lo_high_ref[0], lo_low_ref[0]), pair0)
+        work = work - dot3_narrow(split(turned_ref[0].T), pair0)
         work = place(1, second, work)
-        out_ref[...] = work - dot3_narrow((lo_high_ref[1], lo_low_ref[1]), split(upper1))
-
-
-def update_of(me, pivots, wide, squares, lower, block):
+        out_ref[...] = work - dot3_narrow(split(turned_ref[1].T), split(upper1))
+
+
+def update_of(at, pivots, wide, squares, block, near):
     vmem = pl.BlockSpec(memory_space=pltpu.VMEM)
     return pl.pallas_call(
         update_kernel,
         out_shape=jax.ShapeDtypeStruct((512, 128), jnp.float32),
-        in_specs=[pl.BlockSpec(memory_space=pltpu.SMEM)] + [vmem] * 7,
+        in_specs=[pl.BlockSpec(memory_space=pltpu.SMEM)] + [vmem] * 5 + [pl.BlockSpec(memory_space=pl.ANY)] * 4,
         out_specs=vmem,
+        scratch_shapes=[
+            pltpu.VMEM((NX, NY, 64, 128), jnp.float32),
+            pltpu.VMEM((2, PW, 512), jnp.float32),
+            pltpu.SemaphoreType.DMA((NX,)),
+        ],
         cost_estimate=pl.CostEstimate(flops=1 << 29, bytes_accessed=3 << 20, transcendentals=0),
         compiler_params=pltpu.CompilerParams(vmem_limit_bytes=LIMIT),
         name="update",
-    )(me, pivots, wide, *squares, *lower, block)
+    )(at, pivots, wide, *squares, block, *near)
 
 
 def step(block, panels, pivots):
@@ -235,9 +227,9 @@
     far = lax.ppermute(tile, "row", PAIR)
     near3 = flip(near, 3)
     squares = squares_of(core.reshape(1), tile, far)
-    lower = lower_of(lax.axis_index("col").reshape(1), near, near1, near2, near3)
-    wide, squares, lower = lax.optimization_barrier((wide, squares, lower))
-    return update_of(me.reshape(1), pivots, wide, squares, lower, block)
+    wide, squares = lax.optimization_barrier((wide, squares))
+    at = jnp.stack([me, lax.axis_index("col")])
+    return update_of(at, pivots, wide, squares, block, (near, near1, near2, near3))
 
 
 def solution(mesh):

time: 101 us -> 94.9 us (0.940)
  starting transfers between devices: 60.7 us -> 52.2 us
  local copies, waits for them, and re-layouts: 3.96 us -> 5.79 us
  waiting for transfers between devices: 24 us -> 25.4 us
    all_to_all x2, starting transfers between devices: 11.9 us -> 7.72 us  [spread(): lax.all_to_all(jnp.broadcast_to(x[None], (n,) + x.shape), axis, 0, 0, til...]
    all_to_all x1, waiting for transfers between devices: 0.88 us -> 4.09 us  [step(): lax.all_to_all(part, 'row', 0, 0, tiled=True, axis_index_groups=Z_GROUPS)]
    all_to_all x1, starting transfers between devices: 10.8 us -> 8 us  [step(): lax.all_to_all(tile, 'col', 0, 0, tiled=True, axis_index_groups=COL_GROUPS)]
    unnamed x6 -> x10, local copies, waits for them, and re-layouts: 0.72 us -> 2.56 us
    all_to_all x1, waiting for transfers between devices: 1.62 us -> 0.01 us  [step(): lax.all_to_all(tile, 'col', 0, 0, tiled=True, axis_index_groups=COL_GROUPS)]
    ppermute x3, waiting for transfers between devices: 13.5 us -> 12 us  [flip(): return lax.ppermute(x, 'col', [(i, i ^ bits) for i in range(NX * NY)])]
    ppermute x1, starting transfers between devices: 5.63 us -> 4.31 us  [step(): far = lax.ppermute(part[:64], 'row', PAIR)]
    all_to_all x2, waiting for transfers between devices: 7.17 us -> 8.44 us  [spread(): lax.all_to_all(jnp.broadcast_to(x[None], (n,) + x.shape), axis, 0, 0, til...]
  transfers between devices with their start and end apart: 10 -> 10, of which waited for: 7 -> 6; matrix products, arithmetic and copies ran while one was open for 2% -> 2% of each run, Pallas kernels for 6% -> 4%
where the time goes in v6:
time: 94.9 us; the launch traced here: 94.1 us
  starting transfers between devices  52.2 us (55%)
  waiting for transfers between devices  25.4 us (27%)
  Pallas kernels  7.11 us (7%)
  local copies, waits for them, and re-layouts  5.79 us (6%)
  matrix products  2 us (2%)
  other arithmetic  1.32 us (1%)
    ppermute x3, waiting for transfers between devices, flip(): return lax.ppermute(x, 'col', [(i, i ^ bits) for i in range(NX * NY)])  12 us
    ppermute x3, starting transfers between devices, flip(): return lax.ppermute(x, 'col', [(i, i ^ bits) for i in range(NX * NY)])  10.3 us
    ppermute x1, starting transfers between devices, step(): part = halves(True) + lax.ppermute(halves(False), 'row', PAIR)  8.75 us
    all_to_all x2, waiting for transfers between devices, spread(): lax.all_to_all(jnp.broadcast_to(x[None], (n,) + x.shape), axis, 0, 0, til...  8.44 us
    all_to_all x1, starting transfers between devices, step(): lax.all_to_all(tile, 'col', 0, 0, tiled=True, axis_index_groups=COL_GROUPS)  8 us
    all_to_all x2, starting transfers between devices, spread(): lax.all_to_all(jnp.broadcast_to(x[None], (n,) + x.shape), axis, 0, 0, til...  7.72 us
    all_to_all x1, starting transfers between devices, step(): lax.all_to_all(part, 'row', 0, 0, tiled=True, axis_index_groups=Z_GROUPS)  7.41 us
    ppermute x1, starting transfers between devices, step(): far = lax.ppermute(tile, 'row', PAIR)  5.72 us
  transfers between devices with their start and end apart: 10, of which 6 were waited for; matrix products, arithmetic and copies ran while one was open for 2% of the time, Pallas kernels for 4%

profile of v6, /device:TPU:1, one launch (start us, length us, event | category | flops | bytes accessed | tf_op | source)
XLA Modules:
  0.0 94.1 jit_solution(10017893224537127092)
XLA Ops:
  0.0 0.8 fusion.6
  0.8 0.2 select_reduce_fusion.1
  1.1 1.7 %fusion = f32[1024,128]{1,0:T(8,128)S(1)} fusion(f32[512,128]{1,0:T(8,128)} %block_ref.1, s32[1024]{0:T(1024)S(1)} %add_subtract_fusion), kind=kOutput, calls=%fused_computation.1 | convolution fusion | flops 403177472 | bytes 790528 | tf_op jit(solution)/shard_map/dot_general | solution.py:21
  2.8 0.0 copy-start.4
  2.8 0.7 copy-done.4
  3.5 0.3 convolution_bitcast_fusion
  3.8 0.1 slice_select_fusion.1
  4.0 8.7 %collective-permute-start = (f32[544,128]{1,0:T(8,128)S(1)}, f32[544,128]{1,0:T(8,128)S(1)}, u32[]{:S(2)}, u32[]{:S(2)}) collective-permute-start(f32[544,128]{1,0:T(8,128)S(1)} %pad_maximum_fusion.1), channel_id=1, source_target_pairs={{0,32},{32,0},{64,96},{96,64},{128,160},{160,128},{192,224},{224,1... | collective-permute-start | bytes 835592 | tf_op jit(solution)/shard_map/ppermute | solution.py:208
  12.7 0.7 broadcast_in_dim.55
  13.5 3.4 %all-to-all-start = ((f32[8,64,128]{2,1,0:T(8,128)}), f32[8,64,128]{2,1,0:T(8,128)S(1)}, u32[]{:S(2)}, u32[]{:S(2)}) async-start(f32[8,64,128]{2,1,0:T(8,128)} %broadcast_in_dim.55), calls=%async_computation | async-start | bytes 524288 | tf_op jit(solution)/shard_map/all_to_all | solution.py:29
  16.9 0.0 collective-permute-done
  17.0 0.8 pad_maximum_fusion
  17.8 8.4 %all-to-all-done.n0_ref = f32[8,64,128]{2,1,0:T(8,128)S(1)} async-done(((f32[8,64,128]{2,1,0:T(8,128)}), f32[8,64,128]{2,1,0:T(8,128)S(1)}, u32[]{:S(2)}, u32[]{:S(2)}) %all-to-all-start) | async-done | bytes 262176 | tf_op jit(solution)/shard_map/all_to_all | solution.py:29
  26.2 7.4 %all-to-all-start.1 = ((f32[8,96,128]{2,1,0:T(8,128)}), f32[8,96,128]{2,1,0:T(8,128)S(1)}, u32[]{:S(2)}, u32[]{:S(2)}) async-start(f32[8,96,128]{2,1,0:T(8,128)} %pad_maximum_fusion), calls=%async_computation.1 | async-start | bytes 786432 | tf_op jit(solution)/shard_map/all_to_all | solution.py:214
  33.6 3.1 %collective-permute-start.1 = (f32[8,64,128]{2,1,0:T(8,128)S(1)}, f32[8,64,128]{2,1,0:T(8,128)S(1)}, u32[]{:S(2)}, u32[]{:S(2)}) collective-permute-start(f32[8,64,128]{2,1,0:T(8,128)S(1)} %all-to-all-done.n0_ref), channel_id=1, source_target_pairs={{0,1},{1,0},{2,3},{3,2},{4,5},{5,4},{6,7},{7,6},{8,9},{9,8},{10,11... | collective-permute-start | bytes 786440 | tf_op jit(solution)/shard_map/ppermute | solution.py:35
  36.7 4.4 %collective-permute-done.1.n1_ref = f32[8,64,128]{2,1,0:T(8,128)S(1)} collective-permute-done((f32[8,64,128]{2,1,0:T(8,128)S(1)}, f32[8,64,128]{2,1,0:T(8,128)S(1)}, u32[]{:S(2)}, u32[]{:S(2)}) %collective-permute-start.1) | collective-permute-done | bytes 262176 | tf_op jit(solution)/shard_map/ppermute | solution.py:35
  41.1 4.1 %all-to-all-done.1 = f32[8,96,128]{2,1,0:T(8,128)S(1)} async-done(((f32[8,96,128]{2,1,0:T(8,128)}), f32[8,96,128]{2,1,0:T(8,128)S(1)}, u32[]{:S(2)}, u32[]{:S(2)}) %all-to-all-start.1) | async-done | bytes 393248 | tf_op jit(solution)/shard_map/all_to_all | solution.py:214
  45.3 0.8 broadcast_in_dim.56
  46.1 8.0 %all-to-all-start.2 = ((f32[32,32,128]{2,1,0:T(8,128)}), f32[32,32,128]{2,1,0:T(8,128)S(1)}, u32[]{:S(2)}, u32[]{:S(2)}) async-start(f32[32,32,128]{2,1,0:T(8,128)} %broadcast_in_dim.56), calls=%async_computation.2 | async-start | bytes 1048576 | tf_op jit(solution)/shard_map/all_to_all | solution.py:220
  54.1 4.6 %collective-permute-start.3 = (f32[8,64,128]{2,1,0:T(8,128)S(1)}, f32[8,64,128]{2,1,0:T(8,128)S(1)}, u32[]{:S(2)}, u32[]{:S(2)}) collective-permute-start(f32[8,64,128]{2,1,0:T(8,128)S(1)} %all-to-all-done.n0_ref), channel_id=1, source_target_pairs={{0,2},{1,3},{2,0},{3,1},{4,6},{5,7},{6,4},{7,5},{8,10},{9,11},{10,... | collective-permute-start | bytes 786440 | tf_op jit(solution)/shard_map/ppermute | solution.py:35
  58.8 4.3 %collective-permute-start.2 = (f32[64,128]{1,0:T(8,128)S(1)}, f32[64,128]{1,0:T(8,128)S(1)}, u32[]{:S(2)}, u32[]{:S(2)}) collective-permute-start(f32[64,128]{1,0:T(8,128)S(1)} %slice.77), channel_id=1, source_target_pairs={{0,32},{32,0},{64,96},{96,64},{128,160},{160,128},{192,224},{224,1... | collective-permute-start | bytes 98312 | tf_op jit(solution)/shard_map/ppermute | solution.py:222
  63.1 0.8 collective-permute-done.2
  64.0 5.3 %collective-permute-done.3.n2_ref = f32[8,64,128]{2,1,0:T(8,128)S(1)} collective-permute-done((f32[8,64,128]{2,1,0:T(8,128)S(1)}, f32[8,64,128]{2,1,0:T(8,128)S(1)}, u32[]{:S(2)}, u32[]{:S(2)}) %collective-permute-start.3) | collective-permute-done | bytes 262176 | tf_op jit(solution)/shard_map/ppermute | solution.py:35
  69.3 0.0 all-to-all-done.2.own_ref
  69.3 0.8 broadcast_in_dim.57
  70.1 4.3 %all-to-all-start.3 = ((f32[8,128,128]{2,1,0:T(8,128)}), f32[8,128,128]{2,1,0:T(8,128)S(1)}, u32[]{:S(2)}, u32[]{:S(2)}) async-start(f32[8,128,128]{2,1,0:T(8,128)} %broadcast_in_dim.57), calls=%async_computation.3 | async-start | bytes 1048576 | tf_op jit(solution)/shard_map/all_to_all | solution.py:29
  74.4 5.7 %collective-permute-start.4 = (f32[32,32,128]{2,1,0:T(8,128)S(1)}, f32[32,32,128]{2,1,0:T(8,128)S(1)}, u32[]{:S(2)}, u32[]{:S(2)}) collective-permute-start(f32[32,32,128]{2,1,0:T(8,128)S(1)} %all-to-all-done.2.own_ref), channel_id=1, source_target_pairs={{0,32},{32,0},{64,96},{96,64},{128,160},{160,128},{192,224},{224,1... | collective-permute-start | bytes 1572872 | tf_op jit(solution)/shard_map/ppermute | solution.py:227
  80.2 0.1 pad_add_fusion.at_ref
  80.2 2.5 %collective-permute-start.5 = (f32[8,64,128]{2,1,0:T(8,128)S(1)}, f32[8,64,128]{2,1,0:T(8,128)S(1)}, u32[]{:S(2)}, u32[]{:S(2)}) collective-permute-start(f32[8,64,128]{2,1,0:T(8,128)S(1)} %all-to-all-done.n0_ref), channel_id=1, source_target_pairs={{0,3},{1,2},{2,1},{3,0},{4,7},{5,6},{6,5},{7,4},{8,11},{9,10},{10,... | collective-permute-start | bytes 786440 | tf_op jit(solution)/shard_map/ppermute | solution.py:35
  82.8 0.0 collective-permute-done.4.far_ref
  82.8 0.0 copy-start.2
  82.8 0.8 copy-done.2
  83.6 0.0 copy-start.3
  83.6 1.0 %copy-done.3 = f32[32,32,128]{2,1,0:T(8,128)S(1)} copy-done((f32[32,32,128]{2,1,0:T(8,128)S(1)}, f32[32,32,128]{2,1,0:T(8,128)}, u32[]{:S(2)}) %copy-start.3) | copy-done | bytes 524312
  84.6 0.0 copy-start
  84.7 0.0 copy-start.1
  84.7 4.2 %squares.1 = (bf16[4,256,256]{2,1,0:T(8,128)(2,1)S(1)}, bf16[4,256,256]{2,1,0:T(8,128)(2,1)S(1)}) custom-call(s32[1]{0:T(128)} %bitcast.22.core_ref, f32[32,32,128]{2,1,0:T(8,128)S(1)} %all-to-all-done.2.own_ref, f32[32,32,128]{2,1,0:T(8,128)S(1)} %copy-done.3), custom_call_target="tpu_custom_call" | custom-call | flops 2818572288 | bytes 2097152 | tf_op jit(solution)/shard_map/squares/pallas_call | solution.py:85
  88.9 0.0 all-to-all-done.3.wide_ref
  88.9 2.3 %collective-permute-done.5.n3_ref = f32[8,64,128]{2,1,0:T(8,128)S(1)} collective-permute-done((f32[8,64,128]{2,1,0:T(8,128)S(1)}, f32[8,64,128]{2,1,0:T(8,128)S(1)}, u32[]{:S(2)}, u32[]{:S(2)}) %collective-permute-start.5) | collective-permute-done | bytes 262176 | tf_op jit(solution)/shard_map/ppermute | solution.py:35
  91.2 0.0 copy-done
  91.2 0.0 copy-done.1
  91.2 2.9 %update.1 = f32[512,128]{1,0:T(8,128)} custom-call(s32[2]{0:T(128)S(1)} %pad_add_fusion.at_ref, s32[2,256]{1,0:T(2,128)S(1)} %copy-done.1, f32[8,128,128]{2,1,0:T(8,128)S(1)} %all-to-all-done.3.wide_ref, bf16[4,256,256]{2,1,0:T(8,128)(2,1)S(1)} %get-tuple-element.27.sq_high_ref, bf16[4,256,256]{2,1,0:T(8,128)(2,1)S(1)} %get-tuple-element.28.sq_low_ref, ...), custom_call_target="tpu_custom_call" | custom-call | flops 536870912 | bytes 3145728 | tf_op jit(solution)/shard_map/update/pallas_call | solution.py:156
  (17 shorter events, 0.2 us)
Async XLA Ops:
  2.8 0.8 copy-start.4
  4.0 12.9 %collective-permute-start = (f32[544,128]{1,0:T(8,128)S(1)}, f32[544,128]{1,0:T(8,128)S(1)}, u32[]{:S(2)}, u32[]{:S(2)}) collective-permute-start(f32[544,128]{1,0:T(8,128)S(1)} %pad_maximum_fusion.1), channel_id=1, source_target_pairs={{0,32},{32,0},{64,96},{96,64},{128,160},{160,128},{192,224},{224,1... | collective-permute-start | bytes 835592 | tf_op jit(solution)/shard_map/ppermute | solution.py:208
  13.5 12.7 %all-to-all-start = ((f32[8,64,128]{2,1,0:T(8,128)}), f32[8,64,128]{2,1,0:T(8,128)S(1)}, u32[]{:S(2)}, u32[]{:S(2)}) async-start(f32[8,64,128]{2,1,0:T(8,128)} %broadcast_in_dim.55), calls=%async_computation | async-start | bytes 524288 | tf_op jit(solution)/shard_map/all_to_all | solution.py:29
  26.2 19.0 %all-to-all-start.1 = ((f32[8,96,128]{2,1,0:T(8,128)}), f32[8,96,128]{2,1,0:T(8,128)S(1)}, u32[]{:S(2)}, u32[]{:S(2)}) async-start(f32[8,96,128]{2,1,0:T(8,128)} %pad_maximum_fusion), calls=%async_computation.1 | async-start | bytes 786432 | tf_op jit(solution)/shard_map/all_to_all | solution.py:214
  33.6 7.5 %collective-permute-start.1 = (f32[8,64,128]{2,1,0:T(8,128)S(1)}, f32[8,64,128]{2,1,0:T(8,128)S(1)}, u32[]{:S(2)}, u32[]{:S(2)}) collective-permute-start(f32[8,64,128]{2,1,0:T(8,128)S(1)} %all-to-all-done.n0_ref), channel_id=1, source_target_pairs={{0,1},{1,0},{2,3},{3,2},{4,5},{5,4},{6,7},{7,6},{8,9},{9,8},{10,11... | collective-permute-start | bytes 786440 | tf_op jit(solution)/shard_map/ppermute | solution.py:35
  46.1 23.2 %all-to-all-start.2 = ((f32[32,32,128]{2,1,0:T(8,128)}), f32[32,32,128]{2,1,0:T(8,128)S(1)}, u32[]{:S(2)}, u32[]{:S(2)}) async-start(f32[32,32,128]{2,1,0:T(8,128)} %broadcast_in_dim.56), calls=%async_computation.2 | async-start | bytes 1048576 | tf_op jit(solution)/shard_map/all_to_all | solution.py:220
  54.1 15.2 %collective-permute-start.3 = (f32[8,64,128]{2,1,0:T(8,128)S(1)}, f32[8,64,128]{2,1,0:T(8,128)S(1)}, u32[]{:S(2)}, u32[]{:S(2)}) collective-permute-start(f32[8,64,128]{2,1,0:T(8,128)S(1)} %all-to-all-done.n0_ref), channel_id=1, source_target_pairs={{0,2},{1,3},{2,0},{3,1},{4,6},{5,7},{6,4},{7,5},{8,10},{9,11},{10,... | collective-permute-start | bytes 786440 | tf_op jit(solution)/shard_map/ppermute | solution.py:35
  58.8 5.2 %collective-permute-start.2 = (f32[64,128]{1,0:T(8,128)S(1)}, f32[64,128]{1,0:T(8,128)S(1)}, u32[]{:S(2)}, u32[]{:S(2)}) collective-permute-start(f32[64,128]{1,0:T(8,128)S(1)} %slice.77), channel_id=1, source_target_pairs={{0,32},{32,0},{64,96},{96,64},{128,160},{160,128},{192,224},{224,1... | collective-permute-start | bytes 98312 | tf_op jit(solution)/shard_map/ppermute | solution.py:222
  70.1 18.7 %all-to-all-start.3 = ((f32[8,128,128]{2,1,0:T(8,128)}), f32[8,128,128]{2,1,0:T(8,128)S(1)}, u32[]{:S(2)}, u32[]{:S(2)}) async-start(f32[8,128,128]{2,1,0:T(8,128)} %broadcast_in_dim.57), calls=%async_computation.3 | async-start | bytes 1048576 | tf_op jit(solution)/shard_map/all_to_all | solution.py:29
  74.4 8.4 %collective-permute-start.4 = (f32[32,32,128]{2,1,0:T(8,128)S(1)}, f32[32,32,128]{2,1,0:T(8,128)S(1)}, u32[]{:S(2)}, u32[]{:S(2)}) collective-permute-start(f32[32,32,128]{2,1,0:T(8,128)S(1)} %all-to-all-done.2.own_ref), channel_id=1, source_target_pairs={{0,32},{32,0},{64,96},{96,64},{128,160},{160,128},{192,224},{224,1... | collective-permute-start | bytes 1572872 | tf_op jit(solution)/shard_map/ppermute | solution.py:227
  80.2 10.9 %collective-permute-start.5 = (f32[8,64,128]{2,1,0:T(8,128)S(1)}, f32[8,64,128]{2,1,0:T(8,128)S(1)}, u32[]{:S(2)}, u32[]{:S(2)}) collective-permute-start(f32[8,64,128]{2,1,0:T(8,128)S(1)} %all-to-all-done.n0_ref), channel_id=1, source_target_pairs={{0,3},{1,2},{2,1},{3,0},{4,7},{5,6},{6,5},{7,4},{8,11},{9,10},{10,... | collective-permute-start | bytes 786440 | tf_op jit(solution)/shard_map/ppermute | solution.py:35
  82.8 0.8 copy-start.2
  83.6 1.0 %copy-start.3 = (f32[32,32,128]{2,1,0:T(8,128)S(1)}, f32[32,32,128]{2,1,0:T(8,128)}, u32[]{:S(2)}) copy-start(f32[32,32,128]{2,1,0:T(8,128)} %copy-done.2) | copy-start | bytes 1572868
  84.6 6.5 %copy-start = (f32[512,128]{1,0:T(8,128)S(1)}, f32[512,128]{1,0:T(8,128)}, u32[]{:S(2)}) copy-start(f32[512,128]{1,0:T(8,128)} %block_ref.1) | copy-start | bytes 786436
  84.7 6.5 %copy-start.1 = (s32[2,256]{1,0:T(2,128)S(1)}, s32[2,256]{1,0:T(2,128)}, u32[]{:S(2)}) copy-start(s32[2,256]{1,0:T(2,128)} %piv_ref.1) | copy-start | bytes 6148

commit v7 on v6

--- a/solution.py
+++ b/solution.py
@@ -94,7 +94,7 @@
 
 
 def update_kernel(
-    at_ref, piv_ref, wide_ref, sq_high_ref, sq_low_ref, block_ref, n0_ref, n1_ref, n2_ref, n3_ref,
+    at_ref, piv_ref, col_ref, local_ref, wide_ref, sq_high_ref, sq_low_ref, block_ref, n0_ref, n1_ref, n2_ref, n3_ref,
     out_ref, near_ref, turned_ref, sems,
 ):
     me = at_ref[0]
@@ -106,13 +106,18 @@
         copy.start()
     start = me * 512
 
-    def rows(at):
-        return wide_ref[:, at : at + 32, :].reshape(PW, 128)
+    got = [wide_ref[:, 32 * p : 32 * p + 32, :].reshape(PW, 128) for p in range(2)]
+    held = [local_ref[:PW], local_ref[PW:]]
+    named = [jnp.broadcast_to(col_ref[:, p : p + 1], (PW, PW)) for p in range(2)]
+    again = jnp.logical_and(named[1] == piv_ref[0:1, :], me != 0).astype(jnp.bfloat16)
+    twice = dot(again, jnp.concatenate(split(got[0]), 1))
+    held[1] = held[1] + twice[:, :128] + twice[:, 128:]
+    top = [jnp.where(lax.shift_right_logical(named[p][:, :128], 9) == me, held[p], got[p]) for p in range(2)]
 
     square = [(sq_high_ref[p], sq_low_ref[p]) for p in range(4)]
-    upper0 = dot3_narrow(square[0], split(rows(0)))
+    upper0 = dot3_narrow(square[0], split(top[0]))
     pair0 = split(upper0)
-    upper1 = dot3_narrow(square[1], split(rows(64) - dot3_narrow(square[3], pair0)))
+    upper1 = dot3_narrow(square[1], split(top[1] - dot3_narrow(square[3], pair0)))
 
     for bits, copy in enumerate(copies):
         copy.wait()
@@ -131,7 +136,7 @@
 
     @pl.when(me != 0)
     def _():
-        second = rows(96) - dot3_narrow(square[2], pair0)
+        second = got[1] - dot3_narrow(square[2], pair0)
         at = lax.broadcasted_iota(jnp.int32, (512, PW), 0) + start
 
         def place(p, x, work):
@@ -145,18 +150,18 @@
             moved = one[:, :128] + two[:, :128] + two[:, 128:]
             return jnp.where(one[:, 128:] > 0, moved, work)
 
-        work = place(0, rows(32), block_ref[...])
+        work = place(0, got[0], block_ref[...])
         work = work - dot3_narrow(split(turned_ref[0].T), pair0)
         work = place(1, second, work)
         out_ref[...] = work - dot3_narrow(split(turned_ref[1].T), split(upper1))
 
 
-def update_of(at, pivots, wide, squares, block, near):
+def update_of(at, pivots, local, wide, squares, block, near):
     vmem = pl.BlockSpec(memory_space=pltpu.VMEM)
     return pl.pallas_call(
         update_kernel,
         out_shape=jax.ShapeDtypeStruct((512, 128), jnp.float32),
-        in_specs=[pl.BlockSpec(memory_space=pltpu.SMEM)] + [vmem] * 5 + [pl.BlockSpec(memory_space=pl.ANY)] * 4,
+        in_specs=[pl.BlockSpec(memory_space=pltpu.SMEM)] + [vmem] * 7 + [pl.BlockSpec(memory_space=pl.ANY)] * 4,
         out_specs=vmem,
         scratch_shapes=[
             pltpu.VMEM((NX, NY, 64, 128), jnp.float32),
@@ -166,7 +171,7 @@
         cost_estimate=pl.CostEstimate(flops=1 << 29, bytes_accessed=3 << 20, transcendentals=0),
         compiler_params=pltpu.CompilerParams(vmem_limit_bytes=LIMIT),
         name="update",
-    )(at, pivots, wide, *squares, block, *near)
+    )(at, pivots, pivots.T, local, wide, *squares, block, *near)
 
 
 def step(block, panels, pivots):
@@ -185,7 +190,8 @@
 
     source = jnp.concatenate([p0, through0(p1), j, through0(PW + j)])
     pick = (source[:, None] - start == lane[None, :]).astype(jnp.float32)
-    rows = mm(pick, block).reshape(2, NC, NZ, 32, 128)
+    picked = mm(pick, block)
+    rows = picked.reshape(2, NC, NZ, 32, 128)
     rows = rows.transpose(1, 2, 0, 3, 4).reshape(NC, NZ, 64, 128)
 
     pan_t = panels.transpose(0, 2, 1)
@@ -220,16 +226,24 @@
     tile = lax.all_to_all(tile, "col", 0, 0, tiled=True, axis_index_groups=COL_GROUPS)
     near2 = flip(near, 2)
     far = lax.ppermute(part[:64], "row", PAIR)
-    both = jnp.where(core == 0, jnp.concatenate([part[:64], far]), jnp.concatenate([far, part[:64]]))
-    tile, both, near2 = lax.optimization_barrier((tile, both, near2))
-
-    wide = spread(both, "row", Z_GROUPS)
+    mine = part[:64].reshape(2, 32, 128)
+    far = far.reshape(2, 32, 128)
+    both = jnp.where(core == 0, jnp.stack([mine, far]), jnp.stack([far, mine]))
+    turn = jnp.array(TURN, jnp.int32)
+    here = (turn == me // NC)[None, :, None]
+    place = jnp.sum(jnp.where(here, pivots.reshape(2, NZ, 32), 0), 1) // 512
+    owner = (NC * turn + core)[:, None, None] == place[None]
+    wide = jnp.where(owner[..., None], both[None, :, 1], both[None, :, 0]).reshape(NZ, 64, 128)
+    tile, wide, near2 = lax.optimization_barrier((tile, wide, near2))
+
+    wide = lax.all_to_all(wide, "row", 0, 0, tiled=True, axis_index_groups=Z_GROUPS)
     far = lax.ppermute(tile, "row", PAIR)
     near3 = flip(near, 3)
     squares = squares_of(core.reshape(1), tile, far)
     wide, squares = lax.optimization_barrier((wide, squares))
     at = jnp.stack([me, lax.axis_index("col")])
-    return update_of(at, pivots, wide, squares, block, (near, near1, near2, near3))
+    near, near1, near2, near3 = (pltpu.with_memory_space_constraint(x, pltpu.HBM) for x in (near, near1, near2, near3))
+    return update_of(at, pivots, picked[:512], wide, squares, block, (near, near1, near2, near3))
 
 
 def solution(mesh):

time: 94.9 us -> 97.2 us (1.024)
  waiting for transfers between devices: 25.4 us -> 28.9 us
  local copies, waits for them, and re-layouts: 5.79 us -> 3.46 us
  starting transfers between devices: 52.2 us -> 49.9 us
  other arithmetic: 1.32 us -> 3.05 us
    all_to_all x2 -> x1, starting transfers between devices: 7.72 us -> 3.41 us  [spread(): lax.all_to_all(jnp.broadcast_to(x[None], (n,) + x.shape), axis, 0, 0, til...]
    all_to_all x0 -> x1, starting transfers between devices: none -> 4.3 us  [step(): lax.all_to_all(wide, 'row', 0, 0, tiled=True, axis_index_groups=Z_GROUPS)]
    ppermute x3, waiting for transfers between devices: 12 us -> 15.7 us  [flip(): return lax.ppermute(x, 'col', [(i, i ^ bits) for i in range(NX * NY)])]
    ppermute x1, starting transfers between devices: 5.72 us -> 2.67 us  [step(): far = lax.ppermute(tile, 'row', PAIR)]
    unnamed x10 -> x19, local copies, waits for them, and re-layouts: 2.56 us -> 0.86 us
    ppermute x3, starting transfers between devices: 10.3 us -> 11.5 us  [flip(): return lax.ppermute(x, 'col', [(i, i ^ bits) for i in range(NX * NY)])]
    all_to_all x2 -> x1, waiting for transfers between devices: 8.44 us -> 8.45 us  [spread(): lax.all_to_all(jnp.broadcast_to(x[None], (n,) + x.shape), axis, 0, 0, til...]
  transfers between devices with their start and end apart: 10 -> 10, of which waited for: 6 -> 6; matrix products, arithmetic and copies ran while one was open for 2% -> 3% of each run, Pallas kernels for 4% -> 4%
where the time goes in v7:
time: 97.2 us; the launch traced here: 96.3 us
  starting transfers between devices  49.9 us (51%)
  waiting for transfers between devices  28.9 us (30%)
  Pallas kernels  7.95 us (8%)
  local copies, waits for them, and re-layouts  3.46 us (4%)
  other arithmetic  3.05 us (3%)
  matrix products  2.71 us (3%)
    ppermute x3, waiting for transfers between devices, flip(): return lax.ppermute(x, 'col', [(i, i ^ bits) for i in range(NX * NY)])  15.7 us
    ppermute x3, starting transfers between devices, flip(): return lax.ppermute(x, 'col', [(i, i ^ bits) for i in range(NX * NY)])  11.5 us
    ppermute x1, starting transfers between devices, step(): part = halves(True) + lax.ppermute(halves(False), 'row', PAIR)  8.75 us
    all_to_all x1, waiting for transfers between devices, spread(): lax.all_to_all(jnp.broadcast_to(x[None], (n,) + x.shape), axis, 0, 0, til...  8.45 us
    all_to_all x1, starting transfers between devices, step(): lax.all_to_all(tile, 'col', 0, 0, tiled=True, axis_index_groups=COL_GROUPS)  8.13 us
    all_to_all x1, starting transfers between devices, step(): lax.all_to_all(part, 'row', 0, 0, tiled=True, axis_index_groups=Z_GROUPS)  7.41 us
    all_to_all x1, starting transfers between devices, step(): lax.all_to_all(wide, 'row', 0, 0, tiled=True, axis_index_groups=Z_GROUPS)  4.3 us
    pallas_call x1, Pallas kernels, squares_of(): pl.pallas_call(squares_kernel, out_shape=(pair, pair), in_specs=[pl.Block...  4.21 us
  transfers between devices with their start and end apart: 10, of which 6 were waited for; matrix products, arithmetic and copies ran while one was open for 3% of the time, Pallas kernels for 4%

profile of v7, /device:TPU:1, one launch (start us, length us, event | category | flops | bytes accessed | tf_op | source)
XLA Modules:
  0.0 96.3 jit_solution(15348653541370691513)
XLA Ops:
  0.0 0.8 fusion.7
  0.8 0.2 select_reduce_fusion.1
  1.0 1.0 %convolution_bitcast_fusion = f32[1,8,2,128]{3,1,2,0:T(8,128)S(1)} fusion(s32[256]{0:T(256)S(1)} %get-tuple-element.44, f32[2,8,512]{2,1,0:T(8,128)} %bitcast.59), kind=kOutput, calls=%fused_computation.2 | convolution fusion | flops 6422528 | bytes 25600 | tf_op jit(solution)/shard_map/dot_general | solution.py:21
  2.0 0.8 fusion.5
  2.8 1.7 %fusion = f32[1024,128]{1,0:T(8,128)S(1)} fusion(f32[512,128]{1,0:T(8,128)} %block_ref.1, s32[1024]{0:T(1024)S(1)} %add_subtract_fusion), kind=kOutput, calls=%fused_computation.1 | convolution fusion | flops 403177472 | bytes 790528 | tf_op jit(solution)/shard_map/dot_general | solution.py:21
  4.7 0.0 copy-start.6
  4.7 8.7 %collective-permute-start = (f32[544,128]{1,0:T(8,128)S(1)}, f32[544,128]{1,0:T(8,128)S(1)}, u32[]{:S(2)}, u32[]{:S(2)}) collective-permute-start(f32[544,128]{1,0:T(8,128)S(1)} %pad_maximum_fusion.1), channel_id=1, source_target_pairs={{0,32},{32,0},{64,96},{96,64},{128,160},{160,128},{192,224},{224,1... | collective-permute-start | bytes 835592 | tf_op jit(solution)/shard_map/ppermute | solution.py:214
  13.5 0.0 copy-done.6
  13.5 0.7 broadcast_in_dim.93
  14.2 3.4 %all-to-all-start = ((f32[8,64,128]{2,1,0:T(8,128)}), f32[8,64,128]{2,1,0:T(8,128)S(1)}, u32[]{:S(2)}, u32[]{:S(2)}) async-start(f32[8,64,128]{2,1,0:T(8,128)} %broadcast_in_dim.93), calls=%async_computation | async-start | bytes 524288 | tf_op jit(solution)/shard_map/all_to_all | solution.py:29
  17.6 0.0 collective-permute-done
  17.7 0.8 pad_maximum_fusion
  18.5 8.4 %all-to-all-done.n0_ref = f32[8,64,128]{2,1,0:T(8,128)S(1)} async-done(((f32[8,64,128]{2,1,0:T(8,128)}), f32[8,64,128]{2,1,0:T(8,128)S(1)}, u32[]{:S(2)}, u32[]{:S(2)}) %all-to-all-start) | async-done | bytes 262176 | tf_op jit(solution)/shard_map/all_to_all | solution.py:29
  26.9 7.4 %all-to-all-start.1 = ((f32[8,96,128]{2,1,0:T(8,128)}), f32[8,96,128]{2,1,0:T(8,128)S(1)}, u32[]{:S(2)}, u32[]{:S(2)}) async-start(f32[8,96,128]{2,1,0:T(8,128)} %pad_maximum_fusion), calls=%async_computation.1 | async-start | bytes 786432 | tf_op jit(solution)/shard_map/all_to_all | solution.py:220
  34.4 0.0 copy-done.1
  34.4 0.1 reshape.122
  34.4 0.0 copy-done.8
  34.4 3.1 %collective-permute-start.1 = (f32[8,64,128]{2,1,0:T(8,128)S(1)}, f32[8,64,128]{2,1,0:T(8,128)S(1)}, u32[]{:S(2)}, u32[]{:S(2)}) collective-permute-start(f32[8,64,128]{2,1,0:T(8,128)S(1)} %all-to-all-done.n0_ref), channel_id=1, source_target_pairs={{0,1},{1,0},{2,3},{3,2},{4,5},{5,4},{6,7},{7,6},{8,9},{9,8},{10,11... | collective-permute-start | bytes 786440 | tf_op jit(solution)/shard_map/ppermute | solution.py:35
  37.6 0.1 select_reduce_fusion.2
  37.7 0.1 reduce_sum.22
  37.8 4.2 %collective-permute-done.1.n1_ref = f32[8,64,128]{2,1,0:T(8,128)S(1)} collective-permute-done((f32[8,64,128]{2,1,0:T(8,128)S(1)}, f32[8,64,128]{2,1,0:T(8,128)S(1)}, u32[]{:S(2)}, u32[]{:S(2)}) %collective-permute-start.1) | collective-permute-done | bytes 262176 | tf_op jit(solution)/shard_map/ppermute | solution.py:35
  42.0 4.0 %all-to-all-done.1 = f32[8,96,128]{2,1,0:T(8,128)S(1)} async-done(((f32[8,96,128]{2,1,0:T(8,128)}), f32[8,96,128]{2,1,0:T(8,128)S(1)}, u32[]{:S(2)}, u32[]{:S(2)}) %all-to-all-start.1) | async-done | bytes 393248 | tf_op jit(solution)/shard_map/all_to_all | solution.py:220
  46.0 0.9 broadcast_in_dim.94
  46.9 0.0 copy-done.3
  46.9 8.1 %all-to-all-start.2 = ((f32[32,32,128]{2,1,0:T(8,128)}), f32[32,32,128]{2,1,0:T(8,128)S(1)}, u32[]{:S(2)}, u32[]{:S(2)}) async-start(f32[32,32,128]{2,1,0:T(8,128)} %broadcast_in_dim.94), calls=%async_computation.2 | async-start | bytes 1048576 | tf_op jit(solution)/shard_map/all_to_all | solution.py:226
  55.0 0.0 copy-done.7
  55.1 3.8 %collective-permute-start.2 = (f32[64,128]{1,0:T(8,128)S(1)}, f32[64,128]{1,0:T(8,128)S(1)}, u32[]{:S(2)}, u32[]{:S(2)}) collective-permute-start(f32[64,128]{1,0:T(8,128)S(1)} %slice.89), channel_id=1, source_target_pairs={{0,32},{32,0},{64,96},{96,64},{128,160},{160,128},{192,224},{224,1... | collective-permute-start | bytes 98312 | tf_op jit(solution)/shard_map/ppermute | solution.py:228
  58.8 0.1 broadcast_compare_fusion
  58.9 4.9 %collective-permute-start.3 = (f32[8,64,128]{2,1,0:T(8,128)S(1)}, f32[8,64,128]{2,1,0:T(8,128)S(1)}, u32[]{:S(2)}, u32[]{:S(2)}) collective-permute-start(f32[8,64,128]{2,1,0:T(8,128)S(1)} %all-to-all-done.n0_ref), channel_id=1, source_target_pairs={{0,2},{1,3},{2,0},{3,1},{4,6},{5,7},{6,4},{7,5},{8,10},{9,11},{10,... | collective-permute-start | bytes 786440 | tf_op jit(solution)/shard_map/ppermute | solution.py:35
  63.8 0.0 collective-permute-done.2
  63.9 0.8 broadcast_select_fusion
  64.7 9.2 %collective-permute-done.3.n2_ref = f32[8,64,128]{2,1,0:T(8,128)S(1)} collective-permute-done((f32[8,64,128]{2,1,0:T(8,128)S(1)}, f32[8,64,128]{2,1,0:T(8,128)S(1)}, u32[]{:S(2)}, u32[]{:S(2)}) %collective-permute-start.3) | collective-permute-done | bytes 262176 | tf_op jit(solution)/shard_map/ppermute | solution.py:35
  73.9 0.0 all-to-all-done.2.own_ref
  73.9 2.7 %collective-permute-start.4 = (f32[32,32,128]{2,1,0:T(8,128)S(1)}, f32[32,32,128]{2,1,0:T(8,128)S(1)}, u32[]{:S(2)}, u32[]{:S(2)}) collective-permute-start(f32[32,32,128]{2,1,0:T(8,128)S(1)} %all-to-all-done.2.own_ref), channel_id=1, source_target_pairs={{0,32},{32,0},{64,96},{96,64},{128,160},{160,128},{192,224},{224,1... | collective-permute-start | bytes 1572872 | tf_op jit(solution)/shard_map/ppermute | solution.py:240
  76.6 4.3 %all-to-all-start.3 = ((f32[8,64,128]{2,1,0:T(8,128)}), f32[8,64,128]{2,1,0:T(8,128)S(1)}, u32[]{:S(2)}, u32[]{:S(2)}) async-start(f32[8,64,128]{2,1,0:T(8,128)} %broadcast_select_fusion), calls=%async_computation.3 | async-start | bytes 524288 | tf_op jit(solution)/shard_map/all_to_all | solution.py:239
  80.9 0.1 copy.16
  81.1 0.0 copy-done.4
  81.1 0.1 pad_add_fusion.at_ref
  81.2 0.0 copy-done.2
  81.2 3.5 %collective-permute-start.5 = (f32[8,64,128]{2,1,0:T(8,128)S(1)}, f32[8,64,128]{2,1,0:T(8,128)S(1)}, u32[]{:S(2)}, u32[]{:S(2)}) collective-permute-start(f32[8,64,128]{2,1,0:T(8,128)S(1)} %all-to-all-done.n0_ref), channel_id=1, source_target_pairs={{0,3},{1,2},{2,1},{3,0},{4,7},{5,6},{6,5},{7,4},{8,11},{9,10},{10,... | collective-permute-start | bytes 786440 | tf_op jit(solution)/shard_map/ppermute | solution.py:35
  84.7 0.0 collective-permute-done.4.far_ref
  84.7 0.0 copy-start
  84.7 4.2 %squares.1 = (bf16[4,256,256]{2,1,0:T(8,128)(2,1)S(1)}, bf16[4,256,256]{2,1,0:T(8,128)(2,1)S(1)}) custom-call(s32[1]{0:T(128)} %bitcast.31.core_ref, f32[32,32,128]{2,1,0:T(8,128)S(1)} %all-to-all-done.2.own_ref, f32[32,32,128]{2,1,0:T(8,128)S(1)} %collective-permute-done.4.far_ref), custom_call_target="tpu_custom_call" | custom-call | flops 2818572288 | bytes 2097152 | tf_op jit(solution)/shard_map/squares/pallas_call | solution.py:85
  88.9 0.7 all-to-all-done.3.wide_ref
  89.6 2.3 %collective-permute-done.5.n3_ref = f32[8,64,128]{2,1,0:T(8,128)S(1)} collective-permute-done((f32[8,64,128]{2,1,0:T(8,128)S(1)}, f32[8,64,128]{2,1,0:T(8,128)S(1)}, u32[]{:S(2)}, u32[]{:S(2)}) %collective-permute-start.5) | collective-permute-done | bytes 262176 | tf_op jit(solution)/shard_map/ppermute | solution.py:35
  91.8 0.7 copy-done.5
  92.5 0.0 copy-done
  92.5 3.7 %update.1 = f32[512,128]{1,0:T(8,128)} custom-call(s32[2]{0:T(128)S(1)} %pad_add_fusion.at_ref, s32[2,256]{1,0:T(2,128)S(1)} %copy-done.1, s32[256,2]{1,0:T(8,128)S(1)} %bitcast.50, f32[512,128]{1,0:T(8,128)S(1)} %slice.77.local_ref, f32[8,64,128]{2,1,0:T(8,128)S(1)} %all-to-all-done.3.wide_ref, bf16[4,256,256]{2,1,0:T(8,128)(2,1)S(1)} %get-tuple-element.27.sq_high_ref, ...), custom_call_target="tpu_custom_call" | custom-call | flops 536870912 | bytes 3145728 | tf_op jit(solution)/shard_map/update/pallas_call | solution.py:161
  (29 shorter events, 0.3 us)
Async XLA Ops:
  4.7 8.8 %copy-start.6 = (f32[2,512,8]{1,2,0:T(8,128)S(1)}, f32[2,512,8]{1,2,0:T(8,128)}, u32[]{:S(2)}) copy-start(f32[2,512,8]{1,2,0:T(8,128)} %param.5) | copy-start | bytes 98308
  4.7 12.9 %collective-permute-start = (f32[544,128]{1,0:T(8,128)S(1)}, f32[544,128]{1,0:T(8,128)S(1)}, u32[]{:S(2)}, u32[]{:S(2)}) collective-permute-start(f32[544,128]{1,0:T(8,128)S(1)} %pad_maximum_fusion.1), channel_id=1, source_target_pairs={{0,32},{32,0},{64,96},{96,64},{128,160},{160,128},{192,224},{224,1... | collective-permute-start | bytes 835592 | tf_op jit(solution)/shard_map/ppermute | solution.py:214
  14.2 12.7 %all-to-all-start = ((f32[8,64,128]{2,1,0:T(8,128)}), f32[8,64,128]{2,1,0:T(8,128)S(1)}, u32[]{:S(2)}, u32[]{:S(2)}) async-start(f32[8,64,128]{2,1,0:T(8,128)} %broadcast_in_dim.93), calls=%async_computation | async-start | bytes 524288 | tf_op jit(solution)/shard_map/all_to_all | solution.py:29
  18.5 15.9 %copy-start.1 = (s32[2,256]{1,0:T(2,128)S(1)}, s32[2,256]{1,0:T(2,128)}, u32[]{:S(2)}) copy-start(s32[2,256]{1,0:T(2,128)} %piv_ref.1) | copy-start | bytes 6148
  18.5 15.9 %copy-start.8 = (s32[8]{0:T(128)S(1)}, s32[8]{0:T(128)}, u32[]{:S(2)}) copy-start(s32[8]{0:T(128)} %constant.62.clone) | copy-start | bytes 100
  26.9 54.2 %copy-start.2 = (f32[8,64,128]{2,1,0:T(8,128)}, f32[8,64,128]{2,1,0:T(8,128)S(1)}, u32[]{:S(2)}) copy-start(f32[8,64,128]{2,1,0:T(8,128)S(1)} %all-to-all-done.n0_ref) | copy-start | bytes 786436
  26.9 19.0 %all-to-all-start.1 = ((f32[8,96,128]{2,1,0:T(8,128)}), f32[8,96,128]{2,1,0:T(8,128)S(1)}, u32[]{:S(2)}, u32[]{:S(2)}) async-start(f32[8,96,128]{2,1,0:T(8,128)} %pad_maximum_fusion), calls=%async_computation.1 | async-start | bytes 786432 | tf_op jit(solution)/shard_map/all_to_all | solution.py:220
  34.4 7.5 %collective-permute-start.1 = (f32[8,64,128]{2,1,0:T(8,128)S(1)}, f32[8,64,128]{2,1,0:T(8,128)S(1)}, u32[]{:S(2)}, u32[]{:S(2)}) collective-permute-start(f32[8,64,128]{2,1,0:T(8,128)S(1)} %all-to-all-done.n0_ref), channel_id=1, source_target_pairs={{0,1},{1,0},{2,3},{3,2},{4,5},{5,4},{6,7},{7,6},{8,9},{9,8},{10,11... | collective-permute-start | bytes 786440 | tf_op jit(solution)/shard_map/ppermute | solution.py:35
  42.0 4.9 %copy-start.3 = (f32[8,64,128]{2,1,0:T(8,128)}, f32[8,64,128]{2,1,0:T(8,128)S(1)}, u32[]{:S(2)}) copy-start(f32[8,64,128]{2,1,0:T(8,128)S(1)} %collective-permute-done.1.n1_ref) | copy-start | bytes 786436
  46.9 8.1 %copy-start.7 = (s32[8]{0:T(128)S(1)}, s32[8]{0:T(128)}, u32[]{:S(2)}) copy-start(s32[8]{0:T(128)} %constant.64) | copy-start | bytes 100
  46.9 27.1 %all-to-all-start.2 = ((f32[32,32,128]{2,1,0:T(8,128)}), f32[32,32,128]{2,1,0:T(8,128)S(1)}, u32[]{:S(2)}, u32[]{:S(2)}) async-start(f32[32,32,128]{2,1,0:T(8,128)} %broadcast_in_dim.94), calls=%async_computation.2 | async-start | bytes 1048576 | tf_op jit(solution)/shard_map/all_to_all | solution.py:226
  55.1 8.8 %collective-permute-start.2 = (f32[64,128]{1,0:T(8,128)S(1)}, f32[64,128]{1,0:T(8,128)S(1)}, u32[]{:S(2)}, u32[]{:S(2)}) collective-permute-start(f32[64,128]{1,0:T(8,128)S(1)} %slice.89), channel_id=1, source_target_pairs={{0,32},{32,0},{64,96},{96,64},{128,160},{160,128},{192,224},{224,1... | collective-permute-start | bytes 98312 | tf_op jit(solution)/shard_map/ppermute | solution.py:228
  58.9 15.0 %collective-permute-start.3 = (f32[8,64,128]{2,1,0:T(8,128)S(1)}, f32[8,64,128]{2,1,0:T(8,128)S(1)}, u32[]{:S(2)}, u32[]{:S(2)}) collective-permute-start(f32[8,64,128]{2,1,0:T(8,128)S(1)} %all-to-all-done.n0_ref), channel_id=1, source_target_pairs={{0,2},{1,3},{2,0},{3,1},{4,6},{5,7},{6,4},{7,5},{8,10},{9,11},{10,... | collective-permute-start | bytes 786440 | tf_op jit(solution)/shard_map/ppermute | solution.py:35
  73.9 7.2 %copy-start.4 = (f32[8,64,128]{2,1,0:T(8,128)}, f32[8,64,128]{2,1,0:T(8,128)S(1)}, u32[]{:S(2)}) copy-start(f32[8,64,128]{2,1,0:T(8,128)S(1)} %collective-permute-done.3.n2_ref) | copy-start | bytes 786436
  73.9 10.7 %collective-permute-start.4 = (f32[32,32,128]{2,1,0:T(8,128)S(1)}, f32[32,32,128]{2,1,0:T(8,128)S(1)}, u32[]{:S(2)}, u32[]{:S(2)}) collective-permute-start(f32[32,32,128]{2,1,0:T(8,128)S(1)} %all-to-all-done.2.own_ref), channel_id=1, source_target_pairs={{0,32},{32,0},{64,96},{96,64},{128,160},{160,128},{192,224},{224,1... | collective-permute-start | bytes 1572872 | tf_op jit(solution)/shard_map/ppermute | solution.py:240
  76.6 12.9 %all-to-all-start.3 = ((f32[8,64,128]{2,1,0:T(8,128)}), f32[8,64,128]{2,1,0:T(8,128)S(1)}, u32[]{:S(2)}, u32[]{:S(2)}) async-start(f32[8,64,128]{2,1,0:T(8,128)} %broadcast_select_fusion), calls=%async_computation.3 | async-start | bytes 524288 | tf_op jit(solution)/shard_map/all_to_all | solution.py:239
  81.2 10.7 %collective-permute-start.5 = (f32[8,64,128]{2,1,0:T(8,128)S(1)}, f32[8,64,128]{2,1,0:T(8,128)S(1)}, u32[]{:S(2)}, u32[]{:S(2)}) collective-permute-start(f32[8,64,128]{2,1,0:T(8,128)S(1)} %all-to-all-done.n0_ref), channel_id=1, source_target_pairs={{0,3},{1,2},{2,1},{3,0},{4,7},{5,6},{6,5},{7,4},{8,11},{9,10},{10,... | collective-permute-start | bytes 786440 | tf_op jit(solution)/shard_map/ppermute | solution.py:35
  84.7 7.9 %copy-start = (f32[512,128]{1,0:T(8,128)S(1)}, f32[512,128]{1,0:T(8,128)}, u32[]{:S(2)}) copy-start(f32[512,128]{1,0:T(8,128)} %block_ref.1) | copy-start | bytes 786436
  91.8 0.7 copy-start.5

commit v8 on v7

--- a/solution.py
+++ b/solution.py
@@ -70,9 +70,19 @@
     eye = (row == col).astype(jnp.float32)
     power = [split(jnp.where(row > col, x, 0.0)) for x in squares[:2]]
     inverse = [eye - jnp.where(row > col, x, 0.0) for x in squares[:2]]
-    for _ in range(1, PW.bit_length() - 1):
-        power = [split(dot3(x, x)) for x in power]
-        inverse = [x + dot3(split(x), y) for x, y in zip(inverse, power)]
+    for level in range(1, PW.bit_length() - 1):
+        cut = 1 << level if level >= 4 else 0
+
+        def square(x):
+            full = dot3((x[0][cut:], x[1][cut:]), x)
+            return split(jnp.concatenate([jnp.zeros((cut, PW), jnp.float32), full], 0) if cut else full)
+
+        def extend(x, y):
+            full = x[cut:] + dot3(split(x[cut:]), y)
+            return jnp.concatenate([x[:cut], full], 0) if cut else full
+
+        power = [square(x) for x in power]
+        inverse = [extend(x, y) for x, y in zip(inverse, power)]
     for p, x in enumerate(inverse + squares[2:]):
         high, low = split(x)
         high_ref[p] = high
@@ -104,7 +114,6 @@
     ]
     for copy in copies:
         copy.start()
-    start = me * 512
 
     got = [wide_ref[:, 32 * p : 32 * p + 32, :].reshape(PW, 128) for p in range(2)]
     held = [local_ref[:PW], local_ref[PW:]]
@@ -114,13 +123,9 @@
     held[1] = held[1] + twice[:, :128] + twice[:, 128:]
     top = [jnp.where(lax.shift_right_logical(named[p][:, :128], 9) == me, held[p], got[p]) for p in range(2)]
 
-    square = [(sq_high_ref[p], sq_low_ref[p]) for p in range(4)]
-    upper0 = dot3_narrow(square[0], split(top[0]))
-    pair0 = split(upper0)
-    upper1 = dot3_narrow(square[1], split(top[1] - dot3_narrow(square[3], pair0)))
-
-    for bits, copy in enumerate(copies):
+    for copy in copies:
         copy.wait()
+    for bits in range(NX):
         x = (at_ref[1] % NX) ^ bits
         for i, y in enumerate(TURN):
             at = pl.multiple_of((NX * y + x) * 8, 8)
@@ -128,32 +133,32 @@
                 for h in range(4):
                     tile = near_ref[bits, i, 32 * p + 8 * h : 32 * p + 8 * h + 8, :]
                     turned_ref[p, pl.ds(at, 8), 128 * h : 128 * h + 128] = tile
-
-    @pl.when(me == 0)
-    def _():
-        out_ref[:PW] = upper0
-        out_ref[PW:] = upper1
-
-    @pl.when(me != 0)
-    def _():
-        second = got[1] - dot3_narrow(square[2], pair0)
-        at = lax.broadcasted_iota(jnp.int32, (512, PW), 0) + start
-
-        def place(p, x, work):
-            select = (at == piv_ref[p : p + 1, :]).astype(jnp.bfloat16)
-            high = x.astype(jnp.bfloat16)
-            rest = x - high.astype(jnp.float32)
-            mid = rest.astype(jnp.bfloat16)
-            low = (rest - mid.astype(jnp.float32)).astype(jnp.bfloat16)
-            one = dot(select, jnp.concatenate([high, jnp.ones((PW, 128), jnp.bfloat16)], 1))
-            two = dot(select, jnp.concatenate([mid, low], 1))
-            moved = one[:, :128] + two[:, :128] + two[:, 128:]
-            return jnp.where(one[:, 128:] > 0, moved, work)
-
-        work = place(0, got[0], block_ref[...])
-        work = work - dot3_narrow(split(turned_ref[0].T), pair0)
-        work = place(1, second, work)
-        out_ref[...] = work - dot3_narrow(split(turned_ref[1].T), split(upper1))
+    lower = [split(turned_ref[p].T) for p in range(2)]
+
+    square = [(sq_high_ref[p], sq_low_ref[p]) for p in range(4)]
+    upper0 = dot3_narrow(square[0], split(top[0]))
+    pair0 = split(upper0)
+    upper1 = dot3_narrow(square[1], split(top[1] - dot3_narrow(square[3], pair0)))
+    second = got[1] - dot3_narrow(square[2], pair0)
+    rank = lax.broadcasted_iota(jnp.int32, (512, PW), 0) + me * 512
+
+    def place(p, x, work):
+        select = (rank == piv_ref[p : p + 1, :]).astype(jnp.bfloat16)
+        high = x.astype(jnp.bfloat16)
+        rest = x - high.astype(jnp.float32)
+        mid = rest.astype(jnp.bfloat16)
+        low = (rest - mid.astype(jnp.float32)).astype(jnp.bfloat16)
+        one = dot(select, jnp.concatenate([high, jnp.ones((PW, 128), jnp.bfloat16)], 1))
+        two = dot(select, jnp.concatenate([mid, low], 1))
+        moved = one[:, :128] + two[:, :128] + two[:, 128:]
+        return jnp.where(one[:, 128:] > 0, moved, work)
+
+    work = place(0, got[0], block_ref[...])
+    work = work - dot3_narrow(lower[0], pair0)
+    work = place(1, second, work)
+    work = work - dot3_narrow(lower[1], split(upper1))
+    out_ref[:PW] = jnp.where(me == 0, upper0, work[:PW])
+    out_ref[PW:] = jnp.where(me == 0, upper1, work[PW:])
 
 
 def update_of(at, pivots, local, wide, squares, block, near):

time: 97.2 us -> 97.2 us (level)
  no operation moved by 1% of the time
where the time goes in v8:
time: 97.2 us; the launch traced here: 96.3 us
  starting transfers between devices  49.9 us (51%)
  waiting for transfers between devices  29.3 us (30%)
  Pallas kernels  7.57 us (8%)
  local copies, waits for them, and re-layouts  3.46 us (4%)
  other arithmetic  3.05 us (3%)
  matrix products  2.71 us (3%)
    ppermute x3, waiting for transfers between devices, flip(): return lax.ppermute(x, 'col', [(i, i ^ bits) for i in range(NX * NY)])  15.7 us
    ppermute x3, starting transfers between devices, flip(): return lax.ppermute(x, 'col', [(i, i ^ bits) for i in range(NX * NY)])  11.5 us
    ppermute x1, starting transfers between devices, step(): part = halves(True) + lax.ppermute(halves(False), 'row', PAIR)  8.75 us
    all_to_all x1, waiting for transfers between devices, spread(): lax.all_to_all(jnp.broadcast_to(x[None], (n,) + x.shape), axis, 0, 0, til...  8.45 us
    all_to_all x1, starting transfers between devices, step(): lax.all_to_all(tile, 'col', 0, 0, tiled=True, axis_index_groups=COL_GROUPS)  8.13 us
    all_to_all x1, starting transfers between devices, step(): lax.all_to_all(part, 'row', 0, 0, tiled=True, axis_index_groups=Z_GROUPS)  7.41 us
    all_to_all x1, starting transfers between devices, step(): lax.all_to_all(wide, 'row', 0, 0, tiled=True, axis_index_groups=Z_GROUPS)  4.3 us
    all_to_all x1, waiting for transfers between devices, step(): lax.all_to_all(part, 'row', 0, 0, tiled=True, axis_index_groups=Z_GROUPS)  3.99 us
  transfers between devices with their start and end apart: 10, of which 6 were waited for; matrix products, arithmetic and copies ran while one was open for 3% of the time, Pallas kernels for 4%

profile of v8, /device:TPU:1, one launch (start us, length us, event | category | flops | bytes accessed | tf_op | source)
XLA Modules:
  0.0 96.3 jit_solution(8504025816812113326)
XLA Ops:
  0.0 0.8 fusion.7
  0.8 0.2 select_reduce_fusion.1
  1.0 1.0 %convolution_bitcast_fusion = f32[1,8,2,128]{3,1,2,0:T(8,128)S(1)} fusion(s32[256]{0:T(256)S(1)} %get-tuple-element.44, f32[2,8,512]{2,1,0:T(8,128)} %bitcast.59), kind=kOutput, calls=%fused_computation.2 | convolution fusion | flops 6422528 | bytes 25600 | tf_op jit(solution)/shard_map/dot_general | solution.py:21
  2.0 0.8 fusion.5
  2.8 1.7 %fusion = f32[1024,128]{1,0:T(8,128)S(1)} fusion(f32[512,128]{1,0:T(8,128)} %block_ref.1, s32[1024]{0:T(1024)S(1)} %add_subtract_fusion), kind=kOutput, calls=%fused_computation.1 | convolution fusion | flops 403177472 | bytes 790528 | tf_op jit(solution)/shard_map/dot_general | solution.py:21
  4.7 0.0 copy-start.6
  4.7 8.7 %collective-permute-start = (f32[544,128]{1,0:T(8,128)S(1)}, f32[544,128]{1,0:T(8,128)S(1)}, u32[]{:S(2)}, u32[]{:S(2)}) collective-permute-start(f32[544,128]{1,0:T(8,128)S(1)} %pad_maximum_fusion.1), channel_id=1, source_target_pairs={{0,32},{32,0},{64,96},{96,64},{128,160},{160,128},{192,224},{224,1... | collective-permute-start | bytes 835592 | tf_op jit(solution)/shard_map/ppermute | solution.py:219
  13.5 0.0 copy-done.6
  13.5 0.7 broadcast_in_dim.93
  14.2 3.4 %all-to-all-start = ((f32[8,64,128]{2,1,0:T(8,128)}), f32[8,64,128]{2,1,0:T(8,128)S(1)}, u32[]{:S(2)}, u32[]{:S(2)}) async-start(f32[8,64,128]{2,1,0:T(8,128)} %broadcast_in_dim.93), calls=%async_computation | async-start | bytes 524288 | tf_op jit(solution)/shard_map/all_to_all | solution.py:29
  17.6 0.0 collective-permute-done
  17.7 0.8 pad_maximum_fusion
  18.5 8.4 %all-to-all-done.n0_ref = f32[8,64,128]{2,1,0:T(8,128)S(1)} async-done(((f32[8,64,128]{2,1,0:T(8,128)}), f32[8,64,128]{2,1,0:T(8,128)S(1)}, u32[]{:S(2)}, u32[]{:S(2)}) %all-to-all-start) | async-done | bytes 262176 | tf_op jit(solution)/shard_map/all_to_all | solution.py:29
  26.9 7.4 %all-to-all-start.1 = ((f32[8,96,128]{2,1,0:T(8,128)}), f32[8,96,128]{2,1,0:T(8,128)S(1)}, u32[]{:S(2)}, u32[]{:S(2)}) async-start(f32[8,96,128]{2,1,0:T(8,128)} %pad_maximum_fusion), calls=%async_computation.1 | async-start | bytes 786432 | tf_op jit(solution)/shard_map/all_to_all | solution.py:225
  34.4 0.0 copy-done.1
  34.4 0.1 reshape.122
  34.4 0.0 copy-done.8
  34.4 3.1 %collective-permute-start.1 = (f32[8,64,128]{2,1,0:T(8,128)S(1)}, f32[8,64,128]{2,1,0:T(8,128)S(1)}, u32[]{:S(2)}, u32[]{:S(2)}) collective-permute-start(f32[8,64,128]{2,1,0:T(8,128)S(1)} %all-to-all-done.n0_ref), channel_id=1, source_target_pairs={{0,1},{1,0},{2,3},{3,2},{4,5},{5,4},{6,7},{7,6},{8,9},{9,8},{10,11... | collective-permute-start | bytes 786440 | tf_op jit(solution)/shard_map/ppermute | solution.py:35
  37.6 0.1 select_reduce_fusion.2
  37.7 0.1 reduce_sum.22
  37.8 4.2 %collective-permute-done.1.n1_ref = f32[8,64,128]{2,1,0:T(8,128)S(1)} collective-permute-done((f32[8,64,128]{2,1,0:T(8,128)S(1)}, f32[8,64,128]{2,1,0:T(8,128)S(1)}, u32[]{:S(2)}, u32[]{:S(2)}) %collective-permute-start.1) | collective-permute-done | bytes 262176 | tf_op jit(solution)/shard_map/ppermute | solution.py:35
  42.0 4.0 %all-to-all-done.1 = f32[8,96,128]{2,1,0:T(8,128)S(1)} async-done(((f32[8,96,128]{2,1,0:T(8,128)}), f32[8,96,128]{2,1,0:T(8,128)S(1)}, u32[]{:S(2)}, u32[]{:S(2)}) %all-to-all-start.1) | async-done | bytes 393248 | tf_op jit(solution)/shard_map/all_to_all | solution.py:225
  46.0 0.9 broadcast_in_dim.94
  46.9 0.0 copy-done.3
  46.9 8.1 %all-to-all-start.2 = ((f32[32,32,128]{2,1,0:T(8,128)}), f32[32,32,128]{2,1,0:T(8,128)S(1)}, u32[]{:S(2)}, u32[]{:S(2)}) async-start(f32[32,32,128]{2,1,0:T(8,128)} %broadcast_in_dim.94), calls=%async_computation.2 | async-start | bytes 1048576 | tf_op jit(solution)/shard_map/all_to_all | solution.py:231
  55.0 0.0 copy-done.7
  55.1 3.8 %collective-permute-start.2 = (f32[64,128]{1,0:T(8,128)S(1)}, f32[64,128]{1,0:T(8,128)S(1)}, u32[]{:S(2)}, u32[]{:S(2)}) collective-permute-start(f32[64,128]{1,0:T(8,128)S(1)} %slice.89), channel_id=1, source_target_pairs={{0,32},{32,0},{64,96},{96,64},{128,160},{160,128},{192,224},{224,1... | collective-permute-start | bytes 98312 | tf_op jit(solution)/shard_map/ppermute | solution.py:233
  58.8 0.1 broadcast_compare_fusion
  58.9 4.9 %collective-permute-start.3 = (f32[8,64,128]{2,1,0:T(8,128)S(1)}, f32[8,64,128]{2,1,0:T(8,128)S(1)}, u32[]{:S(2)}, u32[]{:S(2)}) collective-permute-start(f32[8,64,128]{2,1,0:T(8,128)S(1)} %all-to-all-done.n0_ref), channel_id=1, source_target_pairs={{0,2},{1,3},{2,0},{3,1},{4,6},{5,7},{6,4},{7,5},{8,10},{9,11},{10,... | collective-permute-start | bytes 786440 | tf_op jit(solution)/shard_map/ppermute | solution.py:35
  63.8 0.0 collective-permute-done.2
  63.9 0.8 broadcast_select_fusion
  64.7 9.2 %collective-permute-done.3.n2_ref = f32[8,64,128]{2,1,0:T(8,128)S(1)} collective-permute-done((f32[8,64,128]{2,1,0:T(8,128)S(1)}, f32[8,64,128]{2,1,0:T(8,128)S(1)}, u32[]{:S(2)}, u32[]{:S(2)}) %collective-permute-start.3) | collective-permute-done | bytes 262176 | tf_op jit(solution)/shard_map/ppermute | solution.py:35
  73.9 0.0 all-to-all-done.2.own_ref
  73.9 2.7 %collective-permute-start.4 = (f32[32,32,128]{2,1,0:T(8,128)S(1)}, f32[32,32,128]{2,1,0:T(8,128)S(1)}, u32[]{:S(2)}, u32[]{:S(2)}) collective-permute-start(f32[32,32,128]{2,1,0:T(8,128)S(1)} %all-to-all-done.2.own_ref), channel_id=1, source_target_pairs={{0,32},{32,0},{64,96},{96,64},{128,160},{160,128},{192,224},{224,1... | collective-permute-start | bytes 1572872 | tf_op jit(solution)/shard_map/ppermute | solution.py:245
  76.6 4.3 %all-to-all-start.3 = ((f32[8,64,128]{2,1,0:T(8,128)}), f32[8,64,128]{2,1,0:T(8,128)S(1)}, u32[]{:S(2)}, u32[]{:S(2)}) async-start(f32[8,64,128]{2,1,0:T(8,128)} %broadcast_select_fusion), calls=%async_computation.3 | async-start | bytes 524288 | tf_op jit(solution)/shard_map/all_to_all | solution.py:244
  80.9 0.1 copy.16
  81.1 0.0 copy-done.4
  81.1 0.1 pad_add_fusion.at_ref
  81.2 0.0 copy-done.2
  81.2 3.5 %collective-permute-start.5 = (f32[8,64,128]{2,1,0:T(8,128)S(1)}, f32[8,64,128]{2,1,0:T(8,128)S(1)}, u32[]{:S(2)}, u32[]{:S(2)}) collective-permute-start(f32[8,64,128]{2,1,0:T(8,128)S(1)} %all-to-all-done.n0_ref), channel_id=1, source_target_pairs={{0,3},{1,2},{2,1},{3,0},{4,7},{5,6},{6,5},{7,4},{8,11},{9,10},{10,... | collective-permute-start | bytes 786440 | tf_op jit(solution)/shard_map/ppermute | solution.py:35
  84.7 0.0 collective-permute-done.4.far_ref
  84.7 0.0 copy-start
  84.7 3.8 %squares.1 = (bf16[4,256,256]{2,1,0:T(8,128)(2,1)S(1)}, bf16[4,256,256]{2,1,0:T(8,128)(2,1)S(1)}) custom-call(s32[1]{0:T(128)} %bitcast.31.core_ref, f32[32,32,128]{2,1,0:T(8,128)S(1)} %all-to-all-done.2.own_ref, f32[32,32,128]{2,1,0:T(8,128)S(1)} %collective-permute-done.4.far_ref), custom_call_target="tpu_custom_call" | custom-call | flops 2818572288 | bytes 2097152 | tf_op jit(solution)/shard_map/squares/pallas_call | solution.py:95
  88.5 1.1 %all-to-all-done.3.wide_ref = f32[8,64,128]{2,1,0:T(8,128)S(1)} async-done(((f32[8,64,128]{2,1,0:T(8,128)}), f32[8,64,128]{2,1,0:T(8,128)S(1)}, u32[]{:S(2)}, u32[]{:S(2)}) %all-to-all-start.3) | async-done | bytes 262176 | tf_op jit(solution)/shard_map/all_to_all | solution.py:244
  89.6 2.3 %collective-permute-done.5.n3_ref = f32[8,64,128]{2,1,0:T(8,128)S(1)} collective-permute-done((f32[8,64,128]{2,1,0:T(8,128)S(1)}, f32[8,64,128]{2,1,0:T(8,128)S(1)}, u32[]{:S(2)}, u32[]{:S(2)}) %collective-permute-start.5) | collective-permute-done | bytes 262176 | tf_op jit(solution)/shard_map/ppermute | solution.py:35
  91.8 0.7 copy-done.5
  92.5 0.0 copy-done
  92.5 3.8 %update.1 = f32[512,128]{1,0:T(8,128)} custom-call(s32[2]{0:T(128)S(1)} %pad_add_fusion.at_ref, s32[2,256]{1,0:T(2,128)S(1)} %copy-done.1, s32[256,2]{1,0:T(8,128)S(1)} %bitcast.50, f32[512,128]{1,0:T(8,128)S(1)} %slice.77.local_ref, f32[8,64,128]{2,1,0:T(8,128)S(1)} %all-to-all-done.3.wide_ref, bf16[4,256,256]{2,1,0:T(8,128)(2,1)S(1)} %get-tuple-element.27.sq_high_ref, ...), custom_call_target="tpu_custom_call" | custom-call | flops 536870912 | bytes 3145728 | tf_op jit(solution)/shard_map/update/pallas_call | solution.py:166
  (29 shorter events, 0.3 us)
Async XLA Ops:
  4.7 8.8 %copy-start.6 = (f32[2,512,8]{1,2,0:T(8,128)S(1)}, f32[2,512,8]{1,2,0:T(8,128)}, u32[]{:S(2)}) copy-start(f32[2,512,8]{1,2,0:T(8,128)} %param.5) | copy-start | bytes 98308
  4.7 12.9 %collective-permute-start = (f32[544,128]{1,0:T(8,128)S(1)}, f32[544,128]{1,0:T(8,128)S(1)}, u32[]{:S(2)}, u32[]{:S(2)}) collective-permute-start(f32[544,128]{1,0:T(8,128)S(1)} %pad_maximum_fusion.1), channel_id=1, source_target_pairs={{0,32},{32,0},{64,96},{96,64},{128,160},{160,128},{192,224},{224,1... | collective-permute-start | bytes 835592 | tf_op jit(solution)/shard_map/ppermute | solution.py:219
  14.2 12.7 %all-to-all-start = ((f32[8,64,128]{2,1,0:T(8,128)}), f32[8,64,128]{2,1,0:T(8,128)S(1)}, u32[]{:S(2)}, u32[]{:S(2)}) async-start(f32[8,64,128]{2,1,0:T(8,128)} %broadcast_in_dim.93), calls=%async_computation | async-start | bytes 524288 | tf_op jit(solution)/shard_map/all_to_all | solution.py:29
  18.5 15.9 %copy-start.1 = (s32[2,256]{1,0:T(2,128)S(1)}, s32[2,256]{1,0:T(2,128)}, u32[]{:S(2)}) copy-start(s32[2,256]{1,0:T(2,128)} %piv_ref.1) | copy-start | bytes 6148
  18.5 15.9 %copy-start.8 = (s32[8]{0:T(128)S(1)}, s32[8]{0:T(128)}, u32[]{:S(2)}) copy-start(s32[8]{0:T(128)} %constant.62.clone) | copy-start | bytes 100
  26.9 54.2 %copy-start.2 = (f32[8,64,128]{2,1,0:T(8,128)}, f32[8,64,128]{2,1,0:T(8,128)S(1)}, u32[]{:S(2)}) copy-start(f32[8,64,128]{2,1,0:T(8,128)S(1)} %all-to-all-done.n0_ref) | copy-start | bytes 786436
  26.9 19.0 %all-to-all-start.1 = ((f32[8,96,128]{2,1,0:T(8,128)}), f32[8,96,128]{2,1,0:T(8,128)S(1)}, u32[]{:S(2)}, u32[]{:S(2)}) async-start(f32[8,96,128]{2,1,0:T(8,128)} %pad_maximum_fusion), calls=%async_computation.1 | async-start | bytes 786432 | tf_op jit(solution)/shard_map/all_to_all | solution.py:225
  34.4 7.5 %collective-permute-start.1 = (f32[8,64,128]{2,1,0:T(8,128)S(1)}, f32[8,64,128]{2,1,0:T(8,128)S(1)}, u32[]{:S(2)}, u32[]{:S(2)}) collective-permute-start(f32[8,64,128]{2,1,0:T(8,128)S(1)} %all-to-all-done.n0_ref), channel_id=1, source_target_pairs={{0,1},{1,0},{2,3},{3,2},{4,5},{5,4},{6,7},{7,6},{8,9},{9,8},{10,11... | collective-permute-start | bytes 786440 | tf_op jit(solution)/shard_map/ppermute | solution.py:35
  42.0 4.9 %copy-start.3 = (f32[8,64,128]{2,1,0:T(8,128)}, f32[8,64,128]{2,1,0:T(8,128)S(1)}, u32[]{:S(2)}) copy-start(f32[8,64,128]{2,1,0:T(8,128)S(1)} %collective-permute-done.1.n1_ref) | copy-start | bytes 786436
  46.9 8.1 %copy-start.7 = (s32[8]{0:T(128)S(1)}, s32[8]{0:T(128)}, u32[]{:S(2)}) copy-start(s32[8]{0:T(128)} %constant.64) | copy-start | bytes 100
  46.9 27.1 %all-to-all-start.2 = ((f32[32,32,128]{2,1,0:T(8,128)}), f32[32,32,128]{2,1,0:T(8,128)S(1)}, u32[]{:S(2)}, u32[]{:S(2)}) async-start(f32[32,32,128]{2,1,0:T(8,128)} %broadcast_in_dim.94), calls=%async_computation.2 | async-start | bytes 1048576 | tf_op jit(solution)/shard_map/all_to_all | solution.py:231
  55.1 8.8 %collective-permute-start.2 = (f32[64,128]{1,0:T(8,128)S(1)}, f32[64,128]{1,0:T(8,128)S(1)}, u32[]{:S(2)}, u32[]{:S(2)}) collective-permute-start(f32[64,128]{1,0:T(8,128)S(1)} %slice.89), channel_id=1, source_target_pairs={{0,32},{32,0},{64,96},{96,64},{128,160},{160,128},{192,224},{224,1... | collective-permute-start | bytes 98312 | tf_op jit(solution)/shard_map/ppermute | solution.py:233
  58.9 15.0 %collective-permute-start.3 = (f32[8,64,128]{2,1,0:T(8,128)S(1)}, f32[8,64,128]{2,1,0:T(8,128)S(1)}, u32[]{:S(2)}, u32[]{:S(2)}) collective-permute-start(f32[8,64,128]{2,1,0:T(8,128)S(1)} %all-to-all-done.n0_ref), channel_id=1, source_target_pairs={{0,2},{1,3},{2,0},{3,1},{4,6},{5,7},{6,4},{7,5},{8,10},{9,11},{10,... | collective-permute-start | bytes 786440 | tf_op jit(solution)/shard_map/ppermute | solution.py:35
  73.9 7.2 %copy-start.4 = (f32[8,64,128]{2,1,0:T(8,128)}, f32[8,64,128]{2,1,0:T(8,128)S(1)}, u32[]{:S(2)}) copy-start(f32[8,64,128]{2,1,0:T(8,128)S(1)} %collective-permute-done.3.n2_ref) | copy-start | bytes 786436
  73.9 10.7 %collective-permute-start.4 = (f32[32,32,128]{2,1,0:T(8,128)S(1)}, f32[32,32,128]{2,1,0:T(8,128)S(1)}, u32[]{:S(2)}, u32[]{:S(2)}) collective-permute-start(f32[32,32,128]{2,1,0:T(8,128)S(1)} %all-to-all-done.2.own_ref), channel_id=1, source_target_pairs={{0,32},{32,0},{64,96},{96,64},{128,160},{160,128},{192,224},{224,1... | collective-permute-start | bytes 1572872 | tf_op jit(solution)/shard_map/ppermute | solution.py:245
  76.6 12.9 %all-to-all-start.3 = ((f32[8,64,128]{2,1,0:T(8,128)}), f32[8,64,128]{2,1,0:T(8,128)S(1)}, u32[]{:S(2)}, u32[]{:S(2)}) async-start(f32[8,64,128]{2,1,0:T(8,128)} %broadcast_select_fusion), calls=%async_computation.3 | async-start | bytes 524288 | tf_op jit(solution)/shard_map/all_to_all | solution.py:244
  81.2 10.7 %collective-permute-start.5 = (f32[8,64,128]{2,1,0:T(8,128)S(1)}, f32[8,64,128]{2,1,0:T(8,128)S(1)}, u32[]{:S(2)}, u32[]{:S(2)}) collective-permute-start(f32[8,64,128]{2,1,0:T(8,128)S(1)} %all-to-all-done.n0_ref), channel_id=1, source_target_pairs={{0,3},{1,2},{2,1},{3,0},{4,7},{5,6},{6,5},{7,4},{8,11},{9,10},{10,... | collective-permute-start | bytes 786440 | tf_op jit(solution)/shard_map/ppermute | solution.py:35
  84.7 7.9 %copy-start = (f32[512,128]{1,0:T(8,128)S(1)}, f32[512,128]{1,0:T(8,128)}, u32[]{:S(2)}) copy-start(f32[512,128]{1,0:T(8,128)} %block_ref.1) | copy-start | bytes 786436
  91.8 0.7 copy-start.5

commit v9 on v8

--- a/solution.py
+++ b/solution.py
@@ -123,9 +123,8 @@
     held[1] = held[1] + twice[:, :128] + twice[:, 128:]
     top = [jnp.where(lax.shift_right_logical(named[p][:, :128], 9) == me, held[p], got[p]) for p in range(2)]
 
-    for copy in copies:
+    for bits, copy in enumerate(copies):
         copy.wait()
-    for bits in range(NX):
         x = (at_ref[1] % NX) ^ bits
         for i, y in enumerate(TURN):
             at = pl.multiple_of((NX * y + x) * 8, 8)
@@ -247,7 +246,7 @@
     squares = squares_of(core.reshape(1), tile, far)
     wide, squares = lax.optimization_barrier((wide, squares))
     at = jnp.stack([me, lax.axis_index("col")])
-    near, near1, near2, near3 = (pltpu.with_memory_space_constraint(x, pltpu.HBM) for x in (near, near1, near2, near3))
+    near, near1 = (pltpu.with_memory_space_constraint(x, pltpu.HBM) for x in (near, near1))
     return update_of(at, pivots, picked[:512], wide, squares, block, (near, near1, near2, near3))
 
 

time: 97.2 us -> 96.8 us (level)
  no operation moved by 1% of the time
where the time goes in v9:
time: 96.8 us; the launch traced here: 95.9 us
  starting transfers between devices  49.9 us (52%)
  waiting for transfers between devices  29.7 us (31%)
  Pallas kernels  7.43 us (8%)
  other arithmetic  3.07 us (3%)
  local copies, waits for them, and re-layouts  2.76 us (3%)
  matrix products  2.71 us (3%)
    ppermute x3, waiting for transfers between devices, flip(): return lax.ppermute(x, 'col', [(i, i ^ bits) for i in range(NX * NY)])  16.3 us
    ppermute x3, starting transfers between devices, flip(): return lax.ppermute(x, 'col', [(i, i ^ bits) for i in range(NX * NY)])  11.4 us
    ppermute x1, starting transfers between devices, step(): part = halves(True) + lax.ppermute(halves(False), 'row', PAIR)  8.75 us
    all_to_all x1, waiting for transfers between devices, spread(): lax.all_to_all(jnp.broadcast_to(x[None], (n,) + x.shape), axis, 0, 0, til...  8.51 us
    all_to_all x1, starting transfers between devices, step(): lax.all_to_all(tile, 'col', 0, 0, tiled=True, axis_index_groups=COL_GROUPS)  8.13 us
    all_to_all x1, starting transfers between devices, step(): lax.all_to_all(part, 'row', 0, 0, tiled=True, axis_index_groups=Z_GROUPS)  6.79 us
    all_to_all x1, starting transfers between devices, step(): lax.all_to_all(wide, 'row', 0, 0, tiled=True, axis_index_groups=Z_GROUPS)  4.34 us
    all_to_all x1, starting transfers between devices, spread(): lax.all_to_all(jnp.broadcast_to(x[None], (n,) + x.shape), axis, 0, 0, til...  4.05 us
  transfers between devices with their start and end apart: 10, of which 6 were waited for; matrix products, arithmetic and copies ran while one was open for 3% of the time, Pallas kernels for 4%

profile of v9, /device:TPU:1, one launch (start us, length us, event | category | flops | bytes accessed | tf_op | source)
XLA Modules:
  0.0 95.9 jit_solution(12371854650770109169)
XLA Ops:
  0.0 0.8 fusion.7
  0.8 0.2 select_reduce_fusion.1
  1.0 1.0 %convolution_bitcast_fusion = f32[1,8,2,128]{3,1,2,0:T(8,128)S(1)} fusion(s32[256]{0:T(256)S(1)} %get-tuple-element.44, f32[2,8,512]{2,1,0:T(8,128)} %bitcast.59), kind=kOutput, calls=%fused_computation.2 | convolution fusion | flops 6422528 | bytes 25600 | tf_op jit(solution)/shard_map/dot_general | solution.py:21
  2.0 0.8 fusion.5
  2.8 1.7 %fusion = f32[1024,128]{1,0:T(8,128)S(1)} fusion(f32[512,128]{1,0:T(8,128)} %block_ref.1, s32[1024]{0:T(1024)S(1)} %add_subtract_fusion), kind=kOutput, calls=%fused_computation.1 | convolution fusion | flops 403177472 | bytes 790528 | tf_op jit(solution)/shard_map/dot_general | solution.py:21
  4.7 0.0 copy-start.3
  4.7 8.7 %collective-permute-start = (f32[544,128]{1,0:T(8,128)S(1)}, f32[544,128]{1,0:T(8,128)S(1)}, u32[]{:S(2)}, u32[]{:S(2)}) collective-permute-start(f32[544,128]{1,0:T(8,128)S(1)} %pad_maximum_fusion.1), channel_id=1, source_target_pairs={{0,32},{32,0},{64,96},{96,64},{128,160},{160,128},{192,224},{224,1... | collective-permute-start | bytes 835592 | tf_op jit(solution)/shard_map/ppermute | solution.py:218
  13.5 0.0 copy-done.3
  13.5 0.7 broadcast_in_dim.93
  14.2 4.1 %all-to-all-start = ((f32[8,64,128]{2,1,0:T(8,128)}), f32[8,64,128]{2,1,0:T(8,128)}, u32[]{:S(2)}, u32[]{:S(2)}) async-start(f32[8,64,128]{2,1,0:T(8,128)} %broadcast_in_dim.93), calls=%async_computation | async-start | bytes 524288 | tf_op jit(solution)/shard_map/all_to_all | solution.py:29
  18.3 0.0 collective-permute-done
  18.4 0.8 pad_maximum_fusion
  19.1 0.0 copy-start.1
  19.2 0.0 copy-start.5
  19.2 8.5 %all-to-all-done.n0_ref = f32[8,64,128]{2,1,0:T(8,128)} async-done(((f32[8,64,128]{2,1,0:T(8,128)}), f32[8,64,128]{2,1,0:T(8,128)}, u32[]{:S(2)}, u32[]{:S(2)}) %all-to-all-start) | async-done | bytes 262176 | tf_op jit(solution)/shard_map/all_to_all | solution.py:29
  27.7 6.8 %all-to-all-start.1 = ((f32[8,96,128]{2,1,0:T(8,128)}), f32[8,96,128]{2,1,0:T(8,128)S(1)}, u32[]{:S(2)}, u32[]{:S(2)}) async-start(f32[8,96,128]{2,1,0:T(8,128)} %pad_maximum_fusion), calls=%async_computation.1 | async-start | bytes 786432 | tf_op jit(solution)/shard_map/all_to_all | solution.py:224
  34.5 0.0 copy-done.1
  34.5 0.1 reshape.122
  34.5 0.0 copy-done.5
  34.6 3.1 %collective-permute-start.1 = (f32[8,64,128]{2,1,0:T(8,128)}, f32[8,64,128]{2,1,0:T(8,128)S(1)}, u32[]{:S(2)}, u32[]{:S(2)}) collective-permute-start(f32[8,64,128]{2,1,0:T(8,128)} %all-to-all-done.n0_ref), channel_id=1, source_target_pairs={{0,1},{1,0},{2,3},{3,2},{4,5},{5,4},{6,7},{7,6},{8,9},{9,8},{10,11... | collective-permute-start | bytes 786440 | tf_op jit(solution)/shard_map/ppermute | solution.py:35
  37.7 0.1 select_reduce_fusion.2
  37.8 0.1 reduce_sum.22
  37.9 4.4 %collective-permute-done.1.n1_ref = f32[8,64,128]{2,1,0:T(8,128)S(1)} collective-permute-done((f32[8,64,128]{2,1,0:T(8,128)}, f32[8,64,128]{2,1,0:T(8,128)S(1)}, u32[]{:S(2)}, u32[]{:S(2)}) %collective-permute-start.1) | collective-permute-done | bytes 262176 | tf_op jit(solution)/shard_map/ppermute | solution.py:35
  42.3 0.0 copy-start.2
  42.3 3.8 %all-to-all-done.1 = f32[8,96,128]{2,1,0:T(8,128)S(1)} async-done(((f32[8,96,128]{2,1,0:T(8,128)}), f32[8,96,128]{2,1,0:T(8,128)S(1)}, u32[]{:S(2)}, u32[]{:S(2)}) %all-to-all-start.1) | async-done | bytes 393248 | tf_op jit(solution)/shard_map/all_to_all | solution.py:224
  46.1 0.9 broadcast_in_dim.94
  47.0 0.0 copy-done.2
  47.0 8.1 %all-to-all-start.2 = ((f32[32,32,128]{2,1,0:T(8,128)}), f32[32,32,128]{2,1,0:T(8,128)S(1)}, u32[]{:S(2)}, u32[]{:S(2)}) async-start(f32[32,32,128]{2,1,0:T(8,128)} %broadcast_in_dim.94), calls=%async_computation.2 | async-start | bytes 1048576 | tf_op jit(solution)/shard_map/all_to_all | solution.py:230
  55.1 0.0 copy-done.4
  55.2 3.8 %collective-permute-start.2 = (f32[64,128]{1,0:T(8,128)S(1)}, f32[64,128]{1,0:T(8,128)S(1)}, u32[]{:S(2)}, u32[]{:S(2)}) collective-permute-start(f32[64,128]{1,0:T(8,128)S(1)} %slice.89), channel_id=1, source_target_pairs={{0,32},{32,0},{64,96},{96,64},{128,160},{160,128},{192,224},{224,1... | collective-permute-start | bytes 98312 | tf_op jit(solution)/shard_map/ppermute | solution.py:232
  58.9 0.1 broadcast_compare_fusion
  59.0 4.9 %collective-permute-start.3 = (f32[8,64,128]{2,1,0:T(8,128)}, f32[8,64,128]{2,1,0:T(8,128)S(1)}, u32[]{:S(2)}, u32[]{:S(2)}) collective-permute-start(f32[8,64,128]{2,1,0:T(8,128)} %all-to-all-done.n0_ref), channel_id=1, source_target_pairs={{0,2},{1,3},{2,0},{3,1},{4,6},{5,7},{6,4},{7,5},{8,10},{9,11},{10,... | collective-permute-start | bytes 786440 | tf_op jit(solution)/shard_map/ppermute | solution.py:35
  63.9 0.0 collective-permute-done.2
  63.9 0.8 broadcast_select_fusion
  64.8 9.3 %collective-permute-done.3.n2_ref = f32[8,64,128]{2,1,0:T(8,128)S(1)} collective-permute-done((f32[8,64,128]{2,1,0:T(8,128)}, f32[8,64,128]{2,1,0:T(8,128)S(1)}, u32[]{:S(2)}, u32[]{:S(2)}) %collective-permute-start.3) | collective-permute-done | bytes 262176 | tf_op jit(solution)/shard_map/ppermute | solution.py:35
  74.1 0.0 all-to-all-done.2.own_ref
  74.1 2.7 %collective-permute-start.4 = (f32[32,32,128]{2,1,0:T(8,128)S(1)}, f32[32,32,128]{2,1,0:T(8,128)S(1)}, u32[]{:S(2)}, u32[]{:S(2)}) collective-permute-start(f32[32,32,128]{2,1,0:T(8,128)S(1)} %all-to-all-done.2.own_ref), channel_id=1, source_target_pairs={{0,32},{32,0},{64,96},{96,64},{128,160},{160,128},{192,224},{224,1... | collective-permute-start | bytes 1572872 | tf_op jit(solution)/shard_map/ppermute | solution.py:244
  76.8 4.3 %all-to-all-start.3 = ((f32[8,64,128]{2,1,0:T(8,128)}), f32[8,64,128]{2,1,0:T(8,128)S(1)}, u32[]{:S(2)}, u32[]{:S(2)}) async-start(f32[8,64,128]{2,1,0:T(8,128)} %broadcast_select_fusion), calls=%async_computation.3 | async-start | bytes 524288 | tf_op jit(solution)/shard_map/all_to_all | solution.py:243
  81.2 0.1 copy.16
  81.3 0.1 pad_add_fusion.at_ref
  81.4 3.4 %collective-permute-start.5 = (f32[8,64,128]{2,1,0:T(8,128)}, f32[8,64,128]{2,1,0:T(8,128)S(1)}, u32[]{:S(2)}, u32[]{:S(2)}) collective-permute-start(f32[8,64,128]{2,1,0:T(8,128)} %all-to-all-done.n0_ref), channel_id=1, source_target_pairs={{0,3},{1,2},{2,1},{3,0},{4,7},{5,6},{6,5},{7,4},{8,11},{9,10},{10,... | collective-permute-start | bytes 786440 | tf_op jit(solution)/shard_map/ppermute | solution.py:35
  84.8 0.0 collective-permute-done.4.far_ref
  84.8 0.0 copy-start
  84.8 3.8 %squares.1 = (bf16[4,256,256]{2,1,0:T(8,128)(2,1)S(1)}, bf16[4,256,256]{2,1,0:T(8,128)(2,1)S(1)}) custom-call(s32[1]{0:T(128)} %bitcast.31.core_ref, f32[32,32,128]{2,1,0:T(8,128)S(1)} %all-to-all-done.2.own_ref, f32[32,32,128]{2,1,0:T(8,128)S(1)} %collective-permute-done.4.far_ref), custom_call_target="tpu_custom_call" | custom-call | flops 2818572288 | bytes 2097152 | tf_op jit(solution)/shard_map/squares/pallas_call | solution.py:95
  88.7 1.1 %all-to-all-done.3.wide_ref = f32[8,64,128]{2,1,0:T(8,128)S(1)} async-done(((f32[8,64,128]{2,1,0:T(8,128)}), f32[8,64,128]{2,1,0:T(8,128)S(1)}, u32[]{:S(2)}, u32[]{:S(2)}) %all-to-all-start.3) | async-done | bytes 262176 | tf_op jit(solution)/shard_map/all_to_all | solution.py:243
  89.8 2.5 %collective-permute-done.5.n3_ref = f32[8,64,128]{2,1,0:T(8,128)S(1)} collective-permute-done((f32[8,64,128]{2,1,0:T(8,128)}, f32[8,64,128]{2,1,0:T(8,128)S(1)}, u32[]{:S(2)}, u32[]{:S(2)}) %collective-permute-start.5) | collective-permute-done | bytes 262176 | tf_op jit(solution)/shard_map/ppermute | solution.py:35
  92.3 0.0 copy-done
  92.3 3.6 %update.1 = f32[512,128]{1,0:T(8,128)} custom-call(s32[2]{0:T(128)S(1)} %pad_add_fusion.at_ref, s32[2,256]{1,0:T(2,128)S(1)} %copy-done.1, s32[256,2]{1,0:T(8,128)S(1)} %bitcast.50, f32[512,128]{1,0:T(8,128)S(1)} %slice.77.local_ref, f32[8,64,128]{2,1,0:T(8,128)S(1)} %all-to-all-done.3.wide_ref, bf16[4,256,256]{2,1,0:T(8,128)(2,1)S(1)} %get-tuple-element.27.sq_high_ref, ...), custom_call_target="tpu_custom_call" | custom-call | flops 536870912 | bytes 3145728 | tf_op jit(solution)/shard_map/update/pallas_call | solution.py:165
  (23 shorter events, 0.3 us)
Async XLA Ops:
  4.7 8.8 %copy-start.3 = (f32[2,512,8]{1,2,0:T(8,128)S(1)}, f32[2,512,8]{1,2,0:T(8,128)}, u32[]{:S(2)}) copy-start(f32[2,512,8]{1,2,0:T(8,128)} %param.5) | copy-start | bytes 98308
  4.7 13.5 %collective-permute-start = (f32[544,128]{1,0:T(8,128)S(1)}, f32[544,128]{1,0:T(8,128)S(1)}, u32[]{:S(2)}, u32[]{:S(2)}) collective-permute-start(f32[544,128]{1,0:T(8,128)S(1)} %pad_maximum_fusion.1), channel_id=1, source_target_pairs={{0,32},{32,0},{64,96},{96,64},{128,160},{160,128},{192,224},{224,1... | collective-permute-start | bytes 835592 | tf_op jit(solution)/shard_map/ppermute | solution.py:218
  14.2 13.5 %all-to-all-start = ((f32[8,64,128]{2,1,0:T(8,128)}), f32[8,64,128]{2,1,0:T(8,128)}, u32[]{:S(2)}, u32[]{:S(2)}) async-start(f32[8,64,128]{2,1,0:T(8,128)} %broadcast_in_dim.93), calls=%async_computation | async-start | bytes 524288 | tf_op jit(solution)/shard_map/all_to_all | solution.py:29
  19.1 15.3 %copy-start.1 = (s32[2,256]{1,0:T(2,128)S(1)}, s32[2,256]{1,0:T(2,128)}, u32[]{:S(2)}) copy-start(s32[2,256]{1,0:T(2,128)} %piv_ref.1) | copy-start | bytes 6148
  19.2 15.4 %copy-start.5 = (s32[8]{0:T(128)S(1)}, s32[8]{0:T(128)}, u32[]{:S(2)}) copy-start(s32[8]{0:T(128)} %constant.62.clone) | copy-start | bytes 100
  27.7 18.4 %all-to-all-start.1 = ((f32[8,96,128]{2,1,0:T(8,128)}), f32[8,96,128]{2,1,0:T(8,128)S(1)}, u32[]{:S(2)}, u32[]{:S(2)}) async-start(f32[8,96,128]{2,1,0:T(8,128)} %pad_maximum_fusion), calls=%async_computation.1 | async-start | bytes 786432 | tf_op jit(solution)/shard_map/all_to_all | solution.py:224
  34.6 7.7 %collective-permute-start.1 = (f32[8,64,128]{2,1,0:T(8,128)}, f32[8,64,128]{2,1,0:T(8,128)S(1)}, u32[]{:S(2)}, u32[]{:S(2)}) collective-permute-start(f32[8,64,128]{2,1,0:T(8,128)} %all-to-all-done.n0_ref), channel_id=1, source_target_pairs={{0,1},{1,0},{2,3},{3,2},{4,5},{5,4},{6,7},{7,6},{8,9},{9,8},{10,11... | collective-permute-start | bytes 786440 | tf_op jit(solution)/shard_map/ppermute | solution.py:35
  42.3 4.7 %copy-start.2 = (f32[8,64,128]{2,1,0:T(8,128)}, f32[8,64,128]{2,1,0:T(8,128)S(1)}, u32[]{:S(2)}) copy-start(f32[8,64,128]{2,1,0:T(8,128)S(1)} %collective-permute-done.1.n1_ref) | copy-start | bytes 786436
  47.0 8.1 %copy-start.4 = (s32[8]{0:T(128)S(1)}, s32[8]{0:T(128)}, u32[]{:S(2)}) copy-start(s32[8]{0:T(128)} %constant.64) | copy-start | bytes 100
  47.0 27.1 %all-to-all-start.2 = ((f32[32,32,128]{2,1,0:T(8,128)}), f32[32,32,128]{2,1,0:T(8,128)S(1)}, u32[]{:S(2)}, u32[]{:S(2)}) async-start(f32[32,32,128]{2,1,0:T(8,128)} %broadcast_in_dim.94), calls=%async_computation.2 | async-start | bytes 1048576 | tf_op jit(solution)/shard_map/all_to_all | solution.py:230
  55.2 8.8 %collective-permute-start.2 = (f32[64,128]{1,0:T(8,128)S(1)}, f32[64,128]{1,0:T(8,128)S(1)}, u32[]{:S(2)}, u32[]{:S(2)}) collective-permute-start(f32[64,128]{1,0:T(8,128)S(1)} %slice.89), channel_id=1, source_target_pairs={{0,32},{32,0},{64,96},{96,64},{128,160},{160,128},{192,224},{224,1... | collective-permute-start | bytes 98312 | tf_op jit(solution)/shard_map/ppermute | solution.py:232
  59.0 15.1 %collective-permute-start.3 = (f32[8,64,128]{2,1,0:T(8,128)}, f32[8,64,128]{2,1,0:T(8,128)S(1)}, u32[]{:S(2)}, u32[]{:S(2)}) collective-permute-start(f32[8,64,128]{2,1,0:T(8,128)} %all-to-all-done.n0_ref), channel_id=1, source_target_pairs={{0,2},{1,3},{2,0},{3,1},{4,6},{5,7},{6,4},{7,5},{8,10},{9,11},{10,... | collective-permute-start | bytes 786440 | tf_op jit(solution)/shard_map/ppermute | solution.py:35
  74.1 10.7 %collective-permute-start.4 = (f32[32,32,128]{2,1,0:T(8,128)S(1)}, f32[32,32,128]{2,1,0:T(8,128)S(1)}, u32[]{:S(2)}, u32[]{:S(2)}) collective-permute-start(f32[32,32,128]{2,1,0:T(8,128)S(1)} %all-to-all-done.2.own_ref), channel_id=1, source_target_pairs={{0,32},{32,0},{64,96},{96,64},{128,160},{160,128},{192,224},{224,1... | collective-permute-start | bytes 1572872 | tf_op jit(solution)/shard_map/ppermute | solution.py:244
  76.8 13.0 %all-to-all-start.3 = ((f32[8,64,128]{2,1,0:T(8,128)}), f32[8,64,128]{2,1,0:T(8,128)S(1)}, u32[]{:S(2)}, u32[]{:S(2)}) async-start(f32[8,64,128]{2,1,0:T(8,128)} %broadcast_select_fusion), calls=%async_computation.3 | async-start | bytes 524288 | tf_op jit(solution)/shard_map/all_to_all | solution.py:243
  81.4 10.9 %collective-permute-start.5 = (f32[8,64,128]{2,1,0:T(8,128)}, f32[8,64,128]{2,1,0:T(8,128)S(1)}, u32[]{:S(2)}, u32[]{:S(2)}) collective-permute-start(f32[8,64,128]{2,1,0:T(8,128)} %all-to-all-done.n0_ref), channel_id=1, source_target_pairs={{0,3},{1,2},{2,1},{3,0},{4,7},{5,6},{6,5},{7,4},{8,11},{9,10},{10,... | collective-permute-start | bytes 786440 | tf_op jit(solution)/shard_map/ppermute | solution.py:35
  84.8 7.5 %copy-start = (f32[512,128]{1,0:T(8,128)S(1)}, f32[512,128]{1,0:T(8,128)}, u32[]{:S(2)}) copy-start(f32[512,128]{1,0:T(8,128)} %block_ref.1) | copy-start | bytes 786436
